TPU v7x, 256 devices: a whole 4x4x8 slice. The times are simulated.
256 devices in a mesh: dp: 64 (over x, z, core), mp: 4 (over y).
Axes of the slice: x: 4, y: 4, z: 8, core: 2. Of those that a mesh axis runs over, the one named last changes fastest.
Arguments:
- query_rows: bfloat16 [16384, 2048], P('dp', 'mp'), may hold values from -6 to 6
- key_rows: bfloat16 [16384, 512], P('dp', 'mp'), may hold values from -6 to 6
- value_matrix: bfloat16 [16384, 512], P('dp', 'mp'), may hold values from -6 to 6
- out_weight: bfloat16 [2048, 5120], P('mp', 'dp'), may hold values from -0.125 to 0.125
- out_grad: bfloat16 [16384, 5120], P('dp', 'mp'), may hold values from -16 to 16
- doc_lengths: int32 [64, 8], P('dp'), may hold values from 1 to 249, as said below
Outputs:
- layer_out: bfloat16 [16384, 5120], P('dp', 'mp')
- query_grad: bfloat16 [16384, 2048], P('dp', 'mp')
- key_grad: bfloat16 [16384, 512], P('dp', 'mp')
- value_grad: bfloat16 [16384, 512], P('dp', 'mp')
- weight_grad: float32 [2048, 5120], P('mp', 'dp')
Inputs may be any that keep to these rules, and one draw needn't show every extreme that they name: `doc_lengths`: each row holds 8 lengths of 1 or more that sum to 256.
All inputs are finite; a program needn't handle non-finite values.
Results may differ from a plain program's by a relative error of at most 0.014.
Values may be sent and summed in bfloat16 or wider, within the bound.
No kernel may reach another device: no remote copies, remote signals or barrier semaphores. Data moves between devices by JAX's collectives and lax.ppermute only.
A program may use at most 64 MiB of HBM per device.

v0:
```python
import jax
import jax.numpy as jnp
from jax import lax
from jax.experimental import pallas as pl
from jax.experimental.pallas import tpu as pltpu
from jax.sharding import PartitionSpec as P


NX, NZ, NC, NY = 4, 8, 2, 4
HEAD = 128
TOK = 256
HEADS = 4
GROUP = HEADS * HEAD
COLS = 1280
SHARD = 80
AXES = ("dp", "mp")
BF, F32 = jnp.bfloat16, jnp.float32
SCALE = HEAD ** -0.5


def route(target):
    pairs = []
    for x in range(NX):
        for z in range(NZ):
            for c in range(NC):
                for y in range(NY):
                    tx, tz, tc, ty = target(x, z, c, y)
                    src = ((x * NZ + z) * NC + c) * NY + y
                    pairs.append((src, ((tx * NZ + tz) * NC + tc) * NY + ty))
    return pairs


SWAP = route(lambda x, z, c, y: (x, z, 1 - c, y))
ACROSS = route(lambda x, z, c, y: (x ^ 1, z, c, y))
TO_PLANE = [
    route(lambda x, z, c, y, k=k: (2 * ((c + k) % 2) + y // 2, z, y % 2, x)) for k in range(2)
]
TO_OWNER = [
    route(lambda x, z, c, y, k=k: (y, z, (x // 2 + k) % 2, 2 * (x % 2) + c)) for k in range(2)
]
HEADS_OUT = [
    route(lambda x, z, c, y, k=k: (x // 2 * 2 + y // 2, z, y % 2, (2 * (x % 2) + c + k) % 4))
    for k in range(4)
]
HEADS_BACK = [
    route(lambda x, z, c, y, k=k: (x // 2 * 2 + (y + k) % 4 // 2, z, (y + k) % 2, 2 * (x % 2) + c))
    for k in range(4)
]
Z_GROUPS = [[(x * NZ + z) * NC + c for z in range(NZ)] for x in range(NX) for c in range(NC)]


def send(value, pairs):
    return lax.ppermute(value, AXES, pairs)


def exchange(blocks, groups):
    return lax.all_to_all(blocks, "dp", 0, 0, axis_index_groups=groups, tiled=True)


def dot(a, b, dims):
    return lax.dot_general(a, b, (dims, ((), ())), preferred_element_type=F32)


def whole(array):
    dims = array.shape
    return pl.BlockSpec(dims, lambda i: (0,) * len(dims), pipeline_mode=pl.Buffered(1))


def call(body, outs, scratch=(), flops=0, moved=0, limit=63):
    def run(scalars, *operands):
        return pl.pallas_call(
            body,
            out_shape=outs,
            grid=(1,),
            in_specs=[pl.BlockSpec(memory_space=pltpu.SMEM)] + [whole(a) for a in operands],
            out_specs=jax.tree.map(whole, outs),
            scratch_shapes=list(scratch),
            compiler_params=pltpu.CompilerParams(vmem_limit_bytes=limit << 20),
            cost_estimate=pl.CostEstimate(flops=flops, bytes_accessed=moved, transcendentals=0),
        )(scalars, *operands)

    return run


def shape(*dims, dtype=BF):
    return jax.ShapeDtypeStruct(dims, dtype)


def forward_body(lengths, q_ref, k_ref, v_ref, att_ref, prob_ref):
    rows = lax.broadcasted_iota(jnp.int32, (TOK, TOK), 0)
    cols = lax.broadcasted_iota(jnp.int32, (TOK, TOK), 1)
    row_at = lax.broadcasted_iota(jnp.int32, (TOK, 1), 0)
    col_at = lax.broadcasted_iota(jnp.int32, (1, TOK), 1)
    row_seg = jnp.zeros((TOK, 1), jnp.int32)
    col_seg = jnp.zeros((1, TOK), jnp.int32)
    end = jnp.int32(0)
    for i in range(8):
        end = end + lengths[i]
        row_seg = row_seg + (row_at >= end).astype(jnp.int32)
        col_seg = col_seg + (col_at >= end).astype(jnp.int32)
    allowed = (row_seg == col_seg) & (rows >= cols)
    for h in range(HEADS):
        at = slice(h * HEAD, (h + 1) * HEAD)
        logits = dot(q_ref[:, at], k_ref[...], ((1,), (1,))) * SCALE
        logits = jnp.where(allowed, logits, -jnp.inf)
        terms = jnp.exp(logits - jnp.max(logits, axis=-1, keepdims=True))
        prob = terms / jnp.sum(terms, axis=-1, keepdims=True)
        prob_ref[h] = prob
        att_ref[:, at] = dot(prob.astype(BF), v_ref[...], ((1,), (0,))).astype(BF)


def backward_body(_, a0, a1, a2, a3, q_ref, k_ref, v_ref, prob_ref, dq_ref, dk_ref, dv_ref):
    key_sum = jnp.zeros((TOK, HEAD), F32)
    value_sum = jnp.zeros((TOK, HEAD), F32)
    for h in range(HEADS):
        at = slice(h * HEAD, (h + 1) * HEAD)
        up = (
            (a0[:, at].astype(F32) + a1[:, at].astype(F32))
            + (a2[:, at].astype(F32) + a3[:, at].astype(F32))
        ).astype(BF)
        prob = prob_ref[h]
        prob_grad = dot(up, v_ref[...], ((1,), (1,)))
        delta = jnp.sum(prob * prob_grad, axis=-1, keepdims=True)
        score = (prob * (prob_grad - delta) * SCALE).astype(BF)
        dq_ref[:, at] = dot(score, k_ref[...], ((1,), (0,))).astype(BF)
        key_sum = key_sum + dot(score, q_ref[:, at], ((0,), (0,)))
        value_sum = value_sum + dot(prob.astype(BF), up, ((0,), (0,)))
    dk_ref[...] = key_sum.astype(BF)
    dv_ref[...] = value_sum.astype(BF)


def weight_grad_body(place, o0, o1, o2, o3, r0, r1, r2, r3, grad_ref, att_ref):
    g, y = place[0], place[1]
    for k, ref in enumerate((r0, r1, r2, r3)):
        att_ref[jnp.bitwise_xor((y + 4 - k) % 4, g)] = ref[...]
    for i in range(COLS // 256):
        at = slice(i * 256, (i + 1) * 256)
        total = dot(o0[:, at], att_ref[0], ((0,), (0,)))
        for r, ref in ((1, o1), (2, o2), (3, o3)):
            total = total + dot(ref[:, at], att_ref[r], ((0,), (0,)))
        grad_ref[at, :] = total.astype(BF)


def layer_out_body(place, att, w0, w1, mine_ref, across_ref, pair_ref, wt_ref):
    high = place[2]
    for k, ref in enumerate((w0, w1)):
        c = (high + k) % 2
        for z in range(NZ):
            wt_ref[pl.ds(pl.multiple_of(z * 160 + c * SHARD, 16), SHARD), :] = ref[z]
    pair_ref[0] = dot(att[1], wt_ref[...], ((1,), (1,))).astype(BF)
    pair_ref[1] = dot(att[3], wt_ref[...], ((1,), (1,))).astype(BF)
    across_ref[...] = dot(att[2], wt_ref[...], ((1,), (1,)))
    mine_ref[...] = dot(att[0], wt_ref[...], ((1,), (1,)))


def attn_grad_body(place, o0, o1, o2, o3, wt, g0, g1, g2, g3, og):
    g, y = place[0], place[1]
    for r, ref in enumerate((o0, o1, o2, o3)):
        og[r] = ref[...]
    for k, ref in enumerate((g0, g1, g2, g3)):
        at = jnp.bitwise_xor((y + k) % 4, g)
        ref[...] = dot(og[at], wt[...], ((1,), (0,))).astype(BF)


def sum_z_body(place, blocks, o0, o1):
    high = place[2]
    for k, ref in enumerate((o0, o1)):
        at = pl.ds(pl.multiple_of((high + k) % 2 * SHARD, 16), SHARD)
        total = blocks[0, at, :].astype(F32)
        for z in range(1, NZ):
            total = total + blocks[z, at, :].astype(F32)
        ref[...] = total.astype(BF)


def per_device(query_rows, key_rows, value_matrix, out_weight, out_grad, doc_lengths):
    dp, y = lax.axis_index("dp"), lax.axis_index("mp")
    x = dp // (NZ * NC)
    place = jnp.stack([2 * (x % 2) + dp % NC, y, x // 2]).astype(jnp.int32)
    across_grad = send(out_grad, ACROSS)
    cols = [out_grad, send(out_grad, SWAP), across_grad, send(across_grad, SWAP)]

    wt = jnp.broadcast_to(out_weight.T[None], (NZ, SHARD, GROUP))
    wt = exchange(wt, Z_GROUPS)
    blocks = [send(wt, pairs) for pairs in TO_PLANE]

    attended, prob = call(
        forward_body,
        (shape(TOK, GROUP), shape(HEADS, TOK, TOK, dtype=F32)),
        flops=4 * 4 * TOK * TOK * HEAD,
        moved=2 << 20,
    )(doc_lengths[0], query_rows, key_rows, value_matrix)
    heads = [send(attended, pairs) for pairs in HEADS_OUT]

    big = 2 * 4 * TOK * COLS * GROUP
    grad_part, attended_all = call(
        weight_grad_body, (shape(COLS, GROUP), shape(4, TOK, GROUP)), flops=big, moved=6 << 20
    )(place, *cols, *heads)
    grad_rows = exchange(grad_part.reshape(NZ, 2 * SHARD, GROUP), Z_GROUPS)

    mine, across, pair, wt_all = call(
        layer_out_body,
        (shape(TOK, COLS, dtype=F32), shape(TOK, COLS, dtype=F32), shape(2, TOK, COLS), shape(COLS, GROUP)),
        flops=big,
        moved=8 << 20,
    )(place, attended_all, *blocks)
    pair = send(pair, SWAP)
    across = (across + pair[1].astype(F32)).astype(BF)
    across = send(across, ACROSS)
    layer_out = (mine + pair[0].astype(F32) + across.astype(F32)).astype(BF)

    partials = call(
        attn_grad_body,
        (shape(TOK, GROUP),) * 4,
        scratch=(pltpu.VMEM((4, TOK, COLS), BF),),
        flops=big,
        moved=6 << 20,
    )(place, *cols, wt_all)
    upstream = [send(partial, pairs) for partial, pairs in zip(partials, HEADS_BACK)]

    query_grad, key_grad, value_grad = call(
        backward_body,
        (shape(TOK, GROUP), shape(TOK, HEAD), shape(TOK, HEAD)),
        flops=5 * 4 * 2 * TOK * TOK * HEAD,
        moved=3 << 20,
    )(place, *upstream, query_rows, key_rows, value_matrix, prob)

    pieces = call(sum_z_body, (shape(SHARD, GROUP),) * 2, moved=2 << 20)(place, grad_rows)
    pieces = [send(piece, pairs).astype(F32) for piece, pairs in zip(pieces, TO_OWNER)]
    weight_grad = pieces[0] + pieces[1]
    return (layer_out, query_grad, key_grad, value_grad, weight_grad.T)


def solution(mesh):
    placed = (
        P("dp", "mp"),
        P("dp", "mp"),
        P("dp", "mp"),
        P("mp", "dp"),
        P("dp", "mp"),
        P("dp", None),
    )
    return jax.shard_map(
        per_device,
        mesh=mesh,
        in_specs=placed,
        out_specs=(P("dp", "mp"), P("dp", "mp"), P("dp", "mp"), P("dp", "mp"), P("mp", "dp")),
        check_vma=False,
    )
```

profile of v0, /device:TPU:8, one launch (start us, length us, event | category | flops | bytes accessed | tf_op | source)
XLA Modules:
  0.0 148.8 jit_solution(4654317906858647736)
XLA Ops:
  0.6 1.8 %broadcast_in_dim.2 = bf16[8,80,512]{2,1,0:T(8,128)(2,1)} broadcast(bf16[80,512]{1,0:T(8,128)(2,1)} %bitcast.19), dimensions={1,2} | broadcast | bytes 737280 | tf_op jit(solution)/shard_map/broadcast_in_dim | solution.py:182
  2.4 8.5 %all-to-all-start = ((bf16[8,80,512]{2,1,0:T(8,128)(2,1)}), bf16[8,80,512]{2,1,0:T(8,128)(2,1)S(1)}, u32[]{:S(2)}, u32[]{:S(2)}) async-start(bf16[8,80,512]{2,1,0:T(8,128)(2,1)} %broadcast_in_dim.2), calls=%async_computation | async-start | bytes 1310720 | tf_op jit(solution)/shard_map/all_to_all | solution.py:57
  10.9 1.5 %collective-permute-start.1 = (bf16[256,1280]{1,0:T(8,128)(2,1)}, bf16[256,1280]{1,0:T(8,128)(2,1)}, u32[]{:S(2)}, u32[]{:S(2)}) collective-permute-start(bf16[256,1280]{1,0:T(8,128)(2,1)} %o0.3), channel_id=1, source_target_pairs={{0,64},{1,65},{2,66},{3,67},{4,68},{5,69},{6,70},{7,71},{8,72},{9,... | collective-permute-start | bytes 1966088 | tf_op jit(solution)/shard_map/ppermute | solution.py:53
  12.4 3.1 %shard_map.101 = (bf16[256,512]{1,0:T(8,128)(2,1)}, f32[4,256,256]{2,1,0:T(8,128)}) custom-call(s32[8]{0:T(128)} %bitcast.20, bf16[256,512]{1,0:T(8,128)(2,1)} %q_ref.3, bf16[256,128]{1,0:T(8,128)(2,1)} %k_ref.3, bf16[256,128]{1,0:T(8,128)(2,1)} %v_ref.3), custom_call_target="tpu_custom_call" | custom-call | flops 134217728 | bytes 2097152 | tf_op jit(solution)/shard_map/pallas_call | solution.py:71
  15.4 1.2 collective-permute-start.6
  16.6 0.4 collective-permute-start.5
  17.0 0.0 collective-permute-start
  17.1 11.7 %collective-permute-done.1.o2 = bf16[256,1280]{1,0:T(8,128)(2,1)} collective-permute-done((bf16[256,1280]{1,0:T(8,128)(2,1)}, bf16[256,1280]{1,0:T(8,128)(2,1)}, u32[]{:S(2)}, u32[]{:S(2)}) %collective-permute-start.1) | collective-permute-done | bytes 655392 | tf_op jit(solution)/shard_map/ppermute | solution.py:53
  28.8 0.0 collective-permute-start.2
  28.8 2.4 %all-to-all-done = bf16[8,80,512]{2,1,0:T(8,128)(2,1)S(1)} async-done(((bf16[8,80,512]{2,1,0:T(8,128)(2,1)}), bf16[8,80,512]{2,1,0:T(8,128)(2,1)S(1)}, u32[]{:S(2)}, u32[]{:S(2)}) %all-to-all-start) | async-done | bytes 655392 | tf_op jit(solution)/shard_map/all_to_all | solution.py:57
  31.2 2.5 %collective-permute-start.8 = (bf16[8,80,512]{2,1,0:T(8,128)(2,1)S(1)}, bf16[8,80,512]{2,1,0:T(8,128)(2,1)}, u32[]{:S(2)}, u32[]{:S(2)}) collective-permute-start(bf16[8,80,512]{2,1,0:T(8,128)(2,1)S(1)} %all-to-all-done), channel_id=1, source_target_pairs={{0,128},{1,132},{2,192},{3,196},{4,0},{5,4},{6,64},{7,68},{8,136},... | collective-permute-start | bytes 1966088 | tf_op jit(solution)/shard_map/ppermute | solution.py:53
  33.7 0.5 collective-permute-done.6.r3
  34.2 0.0 copy-start.2
  34.2 1.9 %collective-permute-start.7 = (bf16[8,80,512]{2,1,0:T(8,128)(2,1)S(1)}, bf16[8,80,512]{2,1,0:T(8,128)(2,1)}, u32[]{:S(2)}, u32[]{:S(2)}) collective-permute-start(bf16[8,80,512]{2,1,0:T(8,128)(2,1)S(1)} %all-to-all-done), channel_id=1, source_target_pairs={{0,0},{1,4},{2,64},{3,68},{4,128},{5,132},{6,192},{7,196},{8,8},{9... | collective-permute-start | bytes 1966088 | tf_op jit(solution)/shard_map/ppermute | solution.py:53
  36.1 1.0 collective-permute-done.5.r2
  37.1 2.0 %collective-permute-start.4 = (bf16[256,512]{1,0:T(8,128)(2,1)}, bf16[256,512]{1,0:T(8,128)(2,1)}, u32[]{:S(2)}, u32[]{:S(2)}) collective-permute-start(bf16[256,512]{1,0:T(8,128)(2,1)} %get-tuple-element.22), channel_id=1, source_target_pairs={{0,1},{1,5},{2,65},{3,69},{4,2},{5,6},{6,66},{7,70},{8,9},{9,13},{... | collective-permute-start | bytes 786440 | tf_op jit(solution)/shard_map/ppermute | solution.py:53
  39.1 32.3 %collective-permute-done.4.r1 = bf16[256,512]{1,0:T(8,128)(2,1)} collective-permute-done((bf16[256,512]{1,0:T(8,128)(2,1)}, bf16[256,512]{1,0:T(8,128)(2,1)}, u32[]{:S(2)}, u32[]{:S(2)}) %collective-permute-start.4) | collective-permute-done | bytes 262176 | tf_op jit(solution)/shard_map/ppermute | solution.py:53
  71.3 1.9 %collective-permute-start.3 = (bf16[256,512]{1,0:T(8,128)(2,1)}, bf16[256,512]{1,0:T(8,128)(2,1)}, u32[]{:S(2)}, u32[]{:S(2)}) collective-permute-start(bf16[256,512]{1,0:T(8,128)(2,1)} %get-tuple-element.22), channel_id=1, source_target_pairs={{0,0},{1,4},{2,64},{3,68},{4,1},{5,5},{6,65},{7,69},{8,8},{9,12},{... | collective-permute-start | bytes 786440 | tf_op jit(solution)/shard_map/ppermute | solution.py:53
  73.3 0.7 pad_add_fusion.place._
  74.0 5.4 %collective-permute-done.3.r0 = bf16[256,512]{1,0:T(8,128)(2,1)} collective-permute-done((bf16[256,512]{1,0:T(8,128)(2,1)}, bf16[256,512]{1,0:T(8,128)(2,1)}, u32[]{:S(2)}, u32[]{:S(2)}) %collective-permute-start.3) | collective-permute-done | bytes 262176 | tf_op jit(solution)/shard_map/ppermute | solution.py:53
  79.4 0.0 collective-permute-done.o1
  79.4 0.0 collective-permute-done.2.o3
  79.4 0.0 copy-done.2
  79.4 4.7 %shard_map.102 = (bf16[1280,512]{1,0:T(8,128)(2,1)}, bf16[4,256,512]{2,1,0:T(8,128)(2,1)}) custom-call(s32[3]{0:T(128)} %pad_add_fusion.place._, bf16[256,1280]{1,0:T(8,128)(2,1)} %o0.3, bf16[256,1280]{1,0:T(8,128)(2,1)} %collective-permute-done.o1, bf16[256,1280]{1,0:T(8,128)(2,1)} %collective-permute-done.1.o2, ...), custom_call_target="tpu_custom_call" | custom-call | flops 1342177280 | bytes 6291456 | tf_op jit(solution)/shard_map/pallas_call | solution.py:71
  84.0 5.3 %all-to-all-start.1 = ((bf16[8,160,512]{2,1,0:T(8,128)(2,1)}), bf16[8,160,512]{2,1,0:T(8,128)(2,1)}, u32[]{:S(2)}, u32[]{:S(2)}) async-start(bf16[8,160,512]{2,1,0:T(8,128)(2,1)} %bitcast.18), calls=%async_computation.1 | async-start | bytes 2621440 | tf_op jit(solution)/shard_map/all_to_all | solution.py:57
  89.3 0.0 collective-permute-done.8.w1
  89.3 0.0 collective-permute-done.7.w0
  89.3 5.3 %shard_map.103 = (f32[256,1280]{1,0:T(8,128)}, f32[256,1280]{1,0:T(8,128)}, bf16[2,256,1280]{2,1,0:T(8,128)(2,1)}, bf16[1280,512]{1,0:T(8,128)(2,1)}) custom-call(s32[3]{0:T(128)} %pad_add_fusion.place._, bf16[4,256,512]{2,1,0:T(8,128)(2,1)} %get-tuple-element.23.att, bf16[8,80,512]{2,1,0:T(8,128)(2,1)} %collective-permute-done.7.w0, ...), custom_call_target="tpu_custom_call" | custom-call | flops 1342177280 | bytes 8388608 | tf_op jit(solution)/shard_map/pallas_call | solution.py:71
  94.7 0.0 collective-permute-start.9
  94.7 3.2 %collective-permute-done.9 = bf16[2,256,1280]{2,1,0:T(8,128)(2,1)S(1)} collective-permute-done((bf16[2,256,1280]{2,1,0:T(8,128)(2,1)}, bf16[2,256,1280]{2,1,0:T(8,128)(2,1)S(1)}, u32[]{:S(2)}, u32[]{:S(2)}) %collective-permute-start.9) | collective-permute-done | bytes 1310752 | tf_op jit(solution)/shard_map/ppermute | solution.py:53
  97.9 0.0 copy-start
  97.9 1.9 %fusion = bf16[256,1280]{1,0:T(8,128)(2,1)S(1)} fusion(f32[256,1280]{1,0:T(8,128)} %get-tuple-element.26, bf16[2,256,1280]{2,1,0:T(8,128)(2,1)S(1)} %collective-permute-done.9), kind=kLoop, calls=%fused_computation.1 | loop fusion | flops 983040 | bytes 2621440 | tf_op jit(solution)/shard_map/convert_element_type | solution.py:207
  99.9 0.0 copy-done
  99.9 6.3 %collective-permute-start.10 = (bf16[256,1280]{1,0:T(8,128)(2,1)S(1)}, bf16[256,1280]{1,0:T(8,128)(2,1)}, u32[]{:S(2)}, u32[]{:S(2)}) collective-permute-start(bf16[256,1280]{1,0:T(8,128)(2,1)S(1)} %fusion), channel_id=1, source_target_pairs={{0,64},{1,65},{2,66},{3,67},{4,68},{5,69},{6,70},{7,71},{8,72},{9,... | collective-permute-start | bytes 1966088 | tf_op jit(solution)/shard_map/ppermute | solution.py:53
  106.2 4.5 %shard_map.104 = (bf16[256,512]{1,0:T(8,128)(2,1)}, bf16[256,512]{1,0:T(8,128)(2,1)}, bf16[256,512]{1,0:T(8,128)(2,1)}, bf16[256,512]{1,0:T(8,128)(2,1)}) custom-call(s32[3]{0:T(128)} %pad_add_fusion.place._, bf16[256,1280]{1,0:T(8,128)(2,1)} %o0.3, bf16[256,1280]{1,0:T(8,128)(2,1)} %collective-permute-done.o1, bf16[256,1280]{1,0:T(8,128)(2,1)} %collective-permute-done.1.o2, ...), custom_call_target="tpu_custom_call" | custom-call | flops 1342177280 | bytes 6291456 | tf_op jit(solution)/shard_map/pallas_call | solution.py:71
  110.7 6.3 %collective-permute-start.11 = (bf16[256,512]{1,0:T(8,128)(2,1)}, bf16[256,512]{1,0:T(8,128)(2,1)S(1)}, u32[]{:S(2)}, u32[]{:S(2)}) collective-permute-start(bf16[256,512]{1,0:T(8,128)(2,1)} %get-tuple-element.28), channel_id=1, source_target_pairs={{0,0},{1,4},{2,64},{3,68},{4,1},{5,5},{6,65},{7,69},{8,8},{9,12},{... | collective-permute-start | bytes 786440 | tf_op jit(solution)/shard_map/ppermute | solution.py:53
  117.0 0.8 collective-permute-start.12
  117.8 0.0 collective-permute-start.13
  117.8 0.7 collective-permute-start.14
  118.5 0.0 all-to-all-done.1.blocks
  118.5 2.1 %shard_map.106 = (bf16[80,512]{1,0:T(8,128)(2,1)}, bf16[80,512]{1,0:T(8,128)(2,1)}) custom-call(s32[3]{0:T(128)} %pad_add_fusion.place._, bf16[8,160,512]{2,1,0:T(8,128)(2,1)} %all-to-all-done.1.blocks), custom_call_target="tpu_custom_call" | custom-call | bytes 2097152 | tf_op jit(solution)/shard_map/pallas_call | solution.py:71
  120.6 1.9 %collective-permute-done.11.a0 = bf16[256,512]{1,0:T(8,128)(2,1)S(1)} collective-permute-done((bf16[256,512]{1,0:T(8,128)(2,1)}, bf16[256,512]{1,0:T(8,128)(2,1)S(1)}, u32[]{:S(2)}, u32[]{:S(2)}) %collective-permute-start.11) | collective-permute-done | bytes 262176 | tf_op jit(solution)/shard_map/ppermute | solution.py:53
  122.5 0.0 copy-start.1
  122.5 14.9 %collective-permute-start.15 = (bf16[80,512]{1,0:T(8,128)(2,1)}, bf16[80,512]{1,0:T(8,128)(2,1)}, u32[]{:S(2)}, u32[]{:S(2)}) collective-permute-start(bf16[80,512]{1,0:T(8,128)(2,1)} %get-tuple-element.37), channel_id=1, source_target_pairs={{0,0},{1,64},{2,128},{3,192},{4,1},{5,65},{6,129},{7,193},{8,8},{9... | collective-permute-start | bytes 245768 | tf_op jit(solution)/shard_map/ppermute | solution.py:53
  137.4 0.0 collective-permute-done.12.a1
  137.4 0.1 collective-permute-start.16
  137.5 0.0 collective-permute-done.13.a2
  137.5 0.0 collective-permute-done.14.a3
  137.5 0.0 copy-done.1
  137.5 4.0 %shard_map.105 = (bf16[256,512]{1,0:T(8,128)(2,1)}, bf16[256,128]{1,0:T(8,128)(2,1)}, bf16[256,128]{1,0:T(8,128)(2,1)}) custom-call(s32[3]{0:T(128)} %pad_add_fusion.place._, bf16[256,512]{1,0:T(8,128)(2,1)} %copy-done.1, bf16[256,512]{1,0:T(8,128)(2,1)} %collective-permute-done.12.a1, bf16[256,512]{1,0:T(8,128)(2,1)} %collective-permute-done.13.a2, ...), custom_call_target="tpu_custom_call" | custom-call | flops 335544320 | bytes 3145728 | tf_op jit(solution)/shard_map/pallas_call | solution.py:71
  141.5 0.0 collective-permute-done.15
  141.5 3.0 %collective-permute-done.16 = bf16[80,512]{1,0:T(8,128)(2,1)} collective-permute-done((bf16[80,512]{1,0:T(8,128)(2,1)}, bf16[80,512]{1,0:T(8,128)(2,1)}, u32[]{:S(2)}, u32[]{:S(2)}) %collective-permute-start.16) | collective-permute-done | bytes 81952 | tf_op jit(solution)/shard_map/ppermute | solution.py:53
  144.5 1.6 %add_bitcast_fusion = f32[512,80]{0,1:T(8,128)} fusion(bf16[80,512]{1,0:T(8,128)(2,1)} %collective-permute-done.16, bf16[80,512]{1,0:T(8,128)(2,1)} %collective-permute-done.15), kind=kLoop, calls=%fused_computation.7 | loop fusion | flops 122880 | bytes 327680 | tf_op jit(solution)/shard_map/transpose | solution.py:230
  146.1 0.0 collective-permute-done.10
  146.1 2.7 %fusion.2 = bf16[256,1280]{1,0:T(8,128)(2,1)} fusion(f32[256,1280]{1,0:T(8,128)} %get-tuple-element.24, bf16[256,1280]{1,0:T(8,128)(2,1)} %collective-permute-done.10, bf16[2,256,1280]{2,1,0:T(8,128)(2,1)} %copy-done), kind=kLoop, calls=%fused_computation.4 | loop fusion | flops 1638400 | bytes 3276800 | tf_op jit(solution)/shard_map/convert_element_type | solution.py:209
Async XLA Ops:
  2.4 28.8 %all-to-all-start = ((bf16[8,80,512]{2,1,0:T(8,128)(2,1)}), bf16[8,80,512]{2,1,0:T(8,128)(2,1)S(1)}, u32[]{:S(2)}, u32[]{:S(2)}) async-start(bf16[8,80,512]{2,1,0:T(8,128)(2,1)} %broadcast_in_dim.2), calls=%async_computation | async-start | bytes 1310720 | tf_op jit(solution)/shard_map/all_to_all | solution.py:57
  10.9 17.9 %collective-permute-start.1 = (bf16[256,1280]{1,0:T(8,128)(2,1)}, bf16[256,1280]{1,0:T(8,128)(2,1)}, u32[]{:S(2)}, u32[]{:S(2)}) collective-permute-start(bf16[256,1280]{1,0:T(8,128)(2,1)} %o0.3), channel_id=1, source_target_pairs={{0,64},{1,65},{2,66},{3,67},{4,68},{5,69},{6,70},{7,71},{8,72},{9,... | collective-permute-start | bytes 1966088 | tf_op jit(solution)/shard_map/ppermute | solution.py:53
  15.4 18.7 %collective-permute-start.6 = (bf16[256,512]{1,0:T(8,128)(2,1)}, bf16[256,512]{1,0:T(8,128)(2,1)S(1)}, u32[]{:S(2)}, u32[]{:S(2)}) collective-permute-start(bf16[256,512]{1,0:T(8,128)(2,1)} %get-tuple-element.22), channel_id=1, source_target_pairs={{0,3},{1,7},{2,67},{3,71},{4,0},{5,4},{6,64},{7,68},{8,11},{9,15},... | collective-permute-start | bytes 786440 | tf_op jit(solution)/shard_map/ppermute | solution.py:53
  16.6 20.5 %collective-permute-start.5 = (bf16[256,512]{1,0:T(8,128)(2,1)}, bf16[256,512]{1,0:T(8,128)(2,1)}, u32[]{:S(2)}, u32[]{:S(2)}) collective-permute-start(bf16[256,512]{1,0:T(8,128)(2,1)} %get-tuple-element.22), channel_id=1, source_target_pairs={{0,2},{1,6},{2,66},{3,70},{4,3},{5,7},{6,67},{7,71},{8,10},{9,14},... | collective-permute-start | bytes 786440 | tf_op jit(solution)/shard_map/ppermute | solution.py:53
  17.0 62.3 %collective-permute-start = (bf16[256,1280]{1,0:T(8,128)(2,1)}, bf16[256,1280]{1,0:T(8,128)(2,1)}, u32[]{:S(2)}, u32[]{:S(2)}) collective-permute-start(bf16[256,1280]{1,0:T(8,128)(2,1)} %o0.3), channel_id=1, source_target_pairs={{0,4},{1,5},{2,6},{3,7},{4,0},{5,1},{6,2},{7,3},{8,12},{9,13},{10,... | collective-permute-start | bytes 1966088 | tf_op jit(solution)/shard_map/ppermute | solution.py:53
  28.8 50.6 %collective-permute-start.2 = (bf16[256,1280]{1,0:T(8,128)(2,1)}, bf16[256,1280]{1,0:T(8,128)(2,1)}, u32[]{:S(2)}, u32[]{:S(2)}) collective-permute-start(bf16[256,1280]{1,0:T(8,128)(2,1)} %collective-permute-done.1.o2), channel_id=1, source_target_pairs={{0,4},{1,5},{2,6},{3,7},{4,0},{5,1},{6,2},{7,3},{8,12},{9,13},{10,... | collective-permute-start | bytes 1966088 | tf_op jit(solution)/shard_map/ppermute | solution.py:53
  31.2 58.2 %collective-permute-start.8 = (bf16[8,80,512]{2,1,0:T(8,128)(2,1)S(1)}, bf16[8,80,512]{2,1,0:T(8,128)(2,1)}, u32[]{:S(2)}, u32[]{:S(2)}) collective-permute-start(bf16[8,80,512]{2,1,0:T(8,128)(2,1)S(1)} %all-to-all-done), channel_id=1, source_target_pairs={{0,128},{1,132},{2,192},{3,196},{4,0},{5,4},{6,64},{7,68},{8,136},... | collective-permute-start | bytes 1966088 | tf_op jit(solution)/shard_map/ppermute | solution.py:53
  34.2 45.2 %copy-start.2 = (bf16[256,512]{1,0:T(8,128)(2,1)}, bf16[256,512]{1,0:T(8,128)(2,1)S(1)}, u32[]{:S(2)}) copy-start(bf16[256,512]{1,0:T(8,128)(2,1)S(1)} %collective-permute-done.6.r3) | copy-start | bytes 786436
  34.2 55.1 %collective-permute-start.7 = (bf16[8,80,512]{2,1,0:T(8,128)(2,1)S(1)}, bf16[8,80,512]{2,1,0:T(8,128)(2,1)}, u32[]{:S(2)}, u32[]{:S(2)}) collective-permute-start(bf16[8,80,512]{2,1,0:T(8,128)(2,1)S(1)} %all-to-all-done), channel_id=1, source_target_pairs={{0,0},{1,4},{2,64},{3,68},{4,128},{5,132},{6,192},{7,196},{8,8},{9... | collective-permute-start | bytes 1966088 | tf_op jit(solution)/shard_map/ppermute | solution.py:53
  37.1 34.3 %collective-permute-start.4 = (bf16[256,512]{1,0:T(8,128)(2,1)}, bf16[256,512]{1,0:T(8,128)(2,1)}, u32[]{:S(2)}, u32[]{:S(2)}) collective-permute-start(bf16[256,512]{1,0:T(8,128)(2,1)} %get-tuple-element.22), channel_id=1, source_target_pairs={{0,1},{1,5},{2,65},{3,69},{4,2},{5,6},{6,66},{7,70},{8,9},{9,13},{... | collective-permute-start | bytes 786440 | tf_op jit(solution)/shard_map/ppermute | solution.py:53
  71.3 8.0 %collective-permute-start.3 = (bf16[256,512]{1,0:T(8,128)(2,1)}, bf16[256,512]{1,0:T(8,128)(2,1)}, u32[]{:S(2)}, u32[]{:S(2)}) collective-permute-start(bf16[256,512]{1,0:T(8,128)(2,1)} %get-tuple-element.22), channel_id=1, source_target_pairs={{0,0},{1,4},{2,64},{3,68},{4,1},{5,5},{6,65},{7,69},{8,8},{9,12},{... | collective-permute-start | bytes 786440 | tf_op jit(solution)/shard_map/ppermute | solution.py:53
  84.0 34.4 %all-to-all-start.1 = ((bf16[8,160,512]{2,1,0:T(8,128)(2,1)}), bf16[8,160,512]{2,1,0:T(8,128)(2,1)}, u32[]{:S(2)}, u32[]{:S(2)}) async-start(bf16[8,160,512]{2,1,0:T(8,128)(2,1)} %bitcast.18), calls=%async_computation.1 | async-start | bytes 2621440 | tf_op jit(solution)/shard_map/all_to_all | solution.py:57
  94.7 3.2 %collective-permute-start.9 = (bf16[2,256,1280]{2,1,0:T(8,128)(2,1)}, bf16[2,256,1280]{2,1,0:T(8,128)(2,1)S(1)}, u32[]{:S(2)}, u32[]{:S(2)}) collective-permute-start(bf16[2,256,1280]{2,1,0:T(8,128)(2,1)} %get-tuple-element.25), channel_id=1, source_target_pairs={{0,4},{1,5},{2,6},{3,7},{4,0},{5,1},{6,2},{7,3},{8,12},{9,13},{10,... | collective-permute-start | bytes 3932168 | tf_op jit(solution)/shard_map/ppermute | solution.py:53
  97.9 1.9 %copy-start = (bf16[2,256,1280]{2,1,0:T(8,128)(2,1)}, bf16[2,256,1280]{2,1,0:T(8,128)(2,1)S(1)}, u32[]{:S(2)}) copy-start(bf16[2,256,1280]{2,1,0:T(8,128)(2,1)S(1)} %collective-permute-done.9) | copy-start | bytes 3932164
  99.9 46.3 %collective-permute-start.10 = (bf16[256,1280]{1,0:T(8,128)(2,1)S(1)}, bf16[256,1280]{1,0:T(8,128)(2,1)}, u32[]{:S(2)}, u32[]{:S(2)}) collective-permute-start(bf16[256,1280]{1,0:T(8,128)(2,1)S(1)} %fusion), channel_id=1, source_target_pairs={{0,64},{1,65},{2,66},{3,67},{4,68},{5,69},{6,70},{7,71},{8,72},{9,... | collective-permute-start | bytes 1966088 | tf_op jit(solution)/shard_map/ppermute | solution.py:53
  110.7 11.8 %collective-permute-start.11 = (bf16[256,512]{1,0:T(8,128)(2,1)}, bf16[256,512]{1,0:T(8,128)(2,1)S(1)}, u32[]{:S(2)}, u32[]{:S(2)}) collective-permute-start(bf16[256,512]{1,0:T(8,128)(2,1)} %get-tuple-element.28), channel_id=1, source_target_pairs={{0,0},{1,4},{2,64},{3,68},{4,1},{5,5},{6,65},{7,69},{8,8},{9,12},{... | collective-permute-start | bytes 786440 | tf_op jit(solution)/shard_map/ppermute | solution.py:53
  117.0 20.4 %collective-permute-start.12 = (bf16[256,512]{1,0:T(8,128)(2,1)}, bf16[256,512]{1,0:T(8,128)(2,1)}, u32[]{:S(2)}, u32[]{:S(2)}) collective-permute-start(bf16[256,512]{1,0:T(8,128)(2,1)} %get-tuple-element.29), channel_id=1, source_target_pairs={{0,4},{1,64},{2,68},{3,0},{4,5},{5,65},{6,69},{7,1},{8,12},{9,72},... | collective-permute-start | bytes 786440 | tf_op jit(solution)/shard_map/ppermute | solution.py:53
  117.8 19.7 %collective-permute-start.13 = (bf16[256,512]{1,0:T(8,128)(2,1)}, bf16[256,512]{1,0:T(8,128)(2,1)}, u32[]{:S(2)}, u32[]{:S(2)}) collective-permute-start(bf16[256,512]{1,0:T(8,128)(2,1)} %get-tuple-element.30), channel_id=1, source_target_pairs={{0,64},{1,68},{2,0},{3,4},{4,65},{5,69},{6,1},{7,5},{8,72},{9,76},... | collective-permute-start | bytes 786440 | tf_op jit(solution)/shard_map/ppermute | solution.py:53
  117.8 19.7 %collective-permute-start.14 = (bf16[256,512]{1,0:T(8,128)(2,1)}, bf16[256,512]{1,0:T(8,128)(2,1)}, u32[]{:S(2)}, u32[]{:S(2)}) collective-permute-start(bf16[256,512]{1,0:T(8,128)(2,1)} %get-tuple-element.31), channel_id=1, source_target_pairs={{0,68},{1,0},{2,4},{3,64},{4,69},{5,1},{6,5},{7,65},{8,76},{9,8},{... | collective-permute-start | bytes 786440 | tf_op jit(solution)/shard_map/ppermute | solution.py:53
  122.5 15.0 %copy-start.1 = (bf16[256,512]{1,0:T(8,128)(2,1)}, bf16[256,512]{1,0:T(8,128)(2,1)S(1)}, u32[]{:S(2)}) copy-start(bf16[256,512]{1,0:T(8,128)(2,1)S(1)} %collective-permute-done.11.a0) | copy-start | bytes 786436
  122.5 19.0 %collective-permute-start.15 = (bf16[80,512]{1,0:T(8,128)(2,1)}, bf16[80,512]{1,0:T(8,128)(2,1)}, u32[]{:S(2)}, u32[]{:S(2)}) collective-permute-start(bf16[80,512]{1,0:T(8,128)(2,1)} %get-tuple-element.37), channel_id=1, source_target_pairs={{0,0},{1,64},{2,128},{3,192},{4,1},{5,65},{6,129},{7,193},{8,8},{9... | collective-permute-start | bytes 245768 | tf_op jit(solution)/shard_map/ppermute | solution.py:53
  137.4 7.1 %collective-permute-start.16 = (bf16[80,512]{1,0:T(8,128)(2,1)}, bf16[80,512]{1,0:T(8,128)(2,1)}, u32[]{:S(2)}, u32[]{:S(2)}) collective-permute-start(bf16[80,512]{1,0:T(8,128)(2,1)} %get-tuple-element.38), channel_id=1, source_target_pairs={{0,4},{1,68},{2,132},{3,196},{4,5},{5,69},{6,133},{7,197},{8,12},{... | collective-permute-start | bytes 245768 | tf_op jit(solution)/shard_map/ppermute | solution.py:53
where the time goes:
time: 150 us; the launch traced here: 149 us
  waiting for transfers between devices  61.4 us (41%)
  starting transfers between devices  54.3 us (36%)
  Pallas kernels  23.7 us (16%)
  other arithmetic  6.91 us (5%)
  local copies, waits for them, and re-layouts  1.79 us (1%)
    ppermute x17, waiting for transfers between devices, send(): return lax.ppermute(value, AXES, pairs)  59 us
    ppermute x17, starting transfers between devices, send(): return lax.ppermute(value, AXES, pairs)  40.5 us
    pallas_call x6, Pallas kernels, run(): pl.pallas_call(body, out_shape=outs, grid=(1,), in_specs=[pl.BlockSpec(me...  23.7 us
    all_to_all x2, starting transfers between devices, exchange(): lax.all_to_all(blocks, 'dp', 0, 0, axis_index_groups=groups, tiled=True)  13.8 us
  transfers between devices with their start and end apart: 19, of which 9 were waited for; matrix products, arithmetic and copies ran while one was open for 3% of the time, Pallas kernels for 16%

commit v1 on v0

--- a/solution.py
+++ b/solution.py
@@ -30,20 +30,27 @@
     return pairs
 
 
+def low_of(x):
+    return (x + x // 2) % 2
+
+
+def chip(high, low):
+    return 3 - low if high else low
+
+
 SWAP = route(lambda x, z, c, y: (x, z, 1 - c, y))
 ACROSS = route(lambda x, z, c, y: (x ^ 1, z, c, y))
-TO_PLANE = [
-    route(lambda x, z, c, y, k=k: (2 * ((c + k) % 2) + y // 2, z, y % 2, x)) for k in range(2)
-]
+OTHER = route(lambda x, z, c, y: (3 - x, z, c, y))
+TO_PLANE = route(lambda x, z, c, y: (chip(c, y // 2), z, y % 2, x))
 TO_OWNER = [
-    route(lambda x, z, c, y, k=k: (y, z, (x // 2 + k) % 2, 2 * (x % 2) + c)) for k in range(2)
+    route(lambda x, z, c, y, k=k: (y, z, (x // 2 + k) % 2, 2 * low_of(x) + c)) for k in range(2)
 ]
 HEADS_OUT = [
-    route(lambda x, z, c, y, k=k: (x // 2 * 2 + y // 2, z, y % 2, (2 * (x % 2) + c + k) % 4))
+    route(lambda x, z, c, y, k=k: (chip(x // 2, y // 2), z, y % 2, (2 * low_of(x) + c + k) % 4))
     for k in range(4)
 ]
 HEADS_BACK = [
-    route(lambda x, z, c, y, k=k: (x // 2 * 2 + (y + k) % 4 // 2, z, (y + k) % 2, 2 * (x % 2) + c))
+    route(lambda x, z, c, y, k=k: (chip(x // 2, (y + k) % 4 // 2), z, (y + k) % 2, 2 * low_of(x) + c))
     for k in range(4)
 ]
 Z_GROUPS = [[(x * NZ + z) * NC + c for z in range(NZ)] for x in range(NX) for c in range(NC)]
@@ -66,7 +73,7 @@
     return pl.BlockSpec(dims, lambda i: (0,) * len(dims), pipeline_mode=pl.Buffered(1))
 
 
-def call(body, outs, scratch=(), flops=0, moved=0, limit=63):
+def call(body, outs, scratch=(), flops=0, moved=0, limit=12):
     def run(scalars, *operands):
         return pl.pallas_call(
             body,
@@ -129,28 +136,39 @@
     dv_ref[...] = value_sum.astype(BF)
 
 
-def weight_grad_body(place, o0, o1, o2, o3, r0, r1, r2, r3, grad_ref, att_ref):
+def weight_grad_body(place, o0, o1, o2, o3, r0, r1, r2, r3, grad_ref, att):
     g, y = place[0], place[1]
     for k, ref in enumerate((r0, r1, r2, r3)):
-        att_ref[jnp.bitwise_xor((y + 4 - k) % 4, g)] = ref[...]
+        att[jnp.bitwise_xor((y + 4 - k) % 4, g)] = ref[...]
     for i in range(COLS // 256):
         at = slice(i * 256, (i + 1) * 256)
-        total = dot(o0[:, at], att_ref[0], ((0,), (0,)))
+        total = dot(o0[:, at], att[0], ((0,), (0,)))
         for r, ref in ((1, o1), (2, o2), (3, o3)):
-            total = total + dot(ref[:, at], att_ref[r], ((0,), (0,)))
+            total = total + dot(ref[:, at], att[r], ((0,), (0,)))
         grad_ref[at, :] = total.astype(BF)
 
 
-def layer_out_body(place, att, w0, w1, mine_ref, across_ref, pair_ref, wt_ref):
-    high = place[2]
+def layer_pair_body(place, r0, r1, r2, r3, w0, w1, pair_ref, att_ref, wt_ref, att):
+    g, y, high = place[0], place[1], place[2]
+    for k, ref in enumerate((r0, r1, r2, r3)):
+        att[jnp.bitwise_xor((y + 4 - k) % 4, g)] = ref[...]
     for k, ref in enumerate((w0, w1)):
         c = (high + k) % 2
         for z in range(NZ):
             wt_ref[pl.ds(pl.multiple_of(z * 160 + c * SHARD, 16), SHARD), :] = ref[z]
-    pair_ref[0] = dot(att[1], wt_ref[...], ((1,), (1,))).astype(BF)
-    pair_ref[1] = dot(att[3], wt_ref[...], ((1,), (1,))).astype(BF)
-    across_ref[...] = dot(att[2], wt_ref[...], ((1,), (1,)))
-    mine_ref[...] = dot(att[0], wt_ref[...], ((1,), (1,)))
+    for i in range(2):
+        pair_ref[i] = dot(att[2 * i + 1], wt_ref[...], ((1,), (1,))).astype(BF)
+        att_ref[i] = att[2 * i]
+
+
+def layer_across_body(_, att, wt, pair, out):
+    out[...] = (dot(att[1], wt[...], ((1,), (1,))) + pair[1].astype(F32)).astype(BF)
+
+
+def layer_sum_body(_, att, wt, pair, across, out):
+    out[...] = (
+        dot(att[0], wt[...], ((1,), (1,))) + pair[0].astype(F32) + across[...].astype(F32)
+    ).astype(BF)
 
 
 def attn_grad_body(place, o0, o1, o2, o3, wt, g0, g1, g2, g3, og):
@@ -175,13 +193,13 @@
 def per_device(query_rows, key_rows, value_matrix, out_weight, out_grad, doc_lengths):
     dp, y = lax.axis_index("dp"), lax.axis_index("mp")
     x = dp // (NZ * NC)
-    place = jnp.stack([2 * (x % 2) + dp % NC, y, x // 2]).astype(jnp.int32)
+    place = jnp.stack([2 * low_of(x) + dp % NC, y, x // 2]).astype(jnp.int32)
     across_grad = send(out_grad, ACROSS)
     cols = [out_grad, send(out_grad, SWAP), across_grad, send(across_grad, SWAP)]
 
-    wt = jnp.broadcast_to(out_weight.T[None], (NZ, SHARD, GROUP))
-    wt = exchange(wt, Z_GROUPS)
-    blocks = [send(wt, pairs) for pairs in TO_PLANE]
+    wt = send(out_weight.T, TO_PLANE)
+    wt = exchange(jnp.broadcast_to(wt[None], (NZ, SHARD, GROUP)), Z_GROUPS)
+    blocks = [wt, send(wt, OTHER)]
 
     attended, prob = call(
         forward_body,
@@ -192,21 +210,30 @@
     heads = [send(attended, pairs) for pairs in HEADS_OUT]
 
     big = 2 * 4 * TOK * COLS * GROUP
-    grad_part, attended_all = call(
-        weight_grad_body, (shape(COLS, GROUP), shape(4, TOK, GROUP)), flops=big, moved=6 << 20
+    grad_part = call(
+        weight_grad_body,
+        shape(COLS, GROUP),
+        scratch=(pltpu.VMEM((4, TOK, GROUP), BF),),
+        flops=big,
+        moved=6 << 20,
     )(place, *cols, *heads)
     grad_rows = exchange(grad_part.reshape(NZ, 2 * SHARD, GROUP), Z_GROUPS)
 
-    mine, across, pair, wt_all = call(
-        layer_out_body,
-        (shape(TOK, COLS, dtype=F32), shape(TOK, COLS, dtype=F32), shape(2, TOK, COLS), shape(COLS, GROUP)),
-        flops=big,
-        moved=8 << 20,
-    )(place, attended_all, *blocks)
+    pair, attended_two, wt_all = call(
+        layer_pair_body,
+        (shape(2, TOK, COLS), shape(2, TOK, GROUP), shape(COLS, GROUP)),
+        scratch=(pltpu.VMEM((4, TOK, GROUP), BF),),
+        flops=big // 2,
+        moved=6 << 20,
+    )(place, *heads, *blocks)
     pair = send(pair, SWAP)
-    across = (across + pair[1].astype(F32)).astype(BF)
+    across = call(
+        layer_across_body, shape(TOK, COLS), flops=big // 4, moved=3 << 20
+    )(place, attended_two, wt_all, pair)
     across = send(across, ACROSS)
-    layer_out = (mine + pair[0].astype(F32) + across.astype(F32)).astype(BF)
+    layer_out = call(
+        layer_sum_body, shape(TOK, COLS), flops=big // 4, moved=4 << 20
+    )(place, attended_two, wt_all, pair, across)
 
     partials = call(
         attn_grad_body,

time: 150 us -> 125 us (0.83)
  the two profiles are of different devices: /device:TPU:8 before, /device:TPU:6 now
where the time goes in v1:
time: 125 us
  starting transfers between devices  51.1 us (41%)
  waiting for transfers between devices  46 us (37%)
  Pallas kernels  21.5 us (17%)
  local copies, waits for them, and re-layouts  4.47 us (4%)
    ppermute x17, starting transfers between devices, send(): return lax.ppermute(value, AXES, pairs)  34 us
    ppermute x17, waiting for transfers between devices, send(): return lax.ppermute(value, AXES, pairs)  30.5 us
    pallas_call x8, Pallas kernels, run(): pl.pallas_call(body, out_shape=outs, grid=(1,), in_specs=[pl.BlockSpec(me...  21.5 us
    all_to_all x2, starting transfers between devices, exchange(): lax.all_to_all(blocks, 'dp', 0, 0, axis_index_groups=groups, tiled=True)  17.1 us
    all_to_all x2, waiting for transfers between devices, exchange(): lax.all_to_all(blocks, 'dp', 0, 0, axis_index_groups=groups, tiled=True)  15.5 us
    unnamed x38, local copies, waits for them, and re-layouts  3.58 us
  transfers between devices with their start and end apart: 19, of which 8 were waited for; matrix products, arithmetic and copies ran while one was open for 1% of the time, Pallas kernels for 15%

profile of v1, /device:TPU:6, one launch (start us, length us, event | category | flops | bytes accessed | tf_op | source)
XLA Modules:
  0.0 124.7 jit_solution(5734369614890939268)
XLA Ops:
  0.6 0.0 copy-start.2
  0.6 0.0 copy-start.18
  0.7 0.0 copy-start.12
  0.7 5.0 %collective-permute-start.4 = (bf16[80,512]{1,0:T(8,128)(2,1)}, bf16[80,512]{1,0:T(8,128)(2,1)S(1)}, u32[]{:S(2)}, u32[]{:S(2)}) collective-permute-start(bf16[80,512]{1,0:T(8,128)(2,1)} %bitcast.9), channel_id=1, source_target_pairs={{0,0},{1,4},{2,64},{3,68},{4,192},{5,196},{6,128},{7,132},{8,8},{9... | collective-permute-start | bytes 245768 | tf_op jit(solution)/shard_map/ppermute | solution.py:60
  5.6 1.1 collective-permute-start.9
  6.8 1.5 %collective-permute-done.4 = bf16[80,512]{1,0:T(8,128)(2,1)S(1)} collective-permute-done((bf16[80,512]{1,0:T(8,128)(2,1)}, bf16[80,512]{1,0:T(8,128)(2,1)S(1)}, u32[]{:S(2)}, u32[]{:S(2)}) %collective-permute-start.4) | collective-permute-done | bytes 81952 | tf_op jit(solution)/shard_map/ppermute | solution.py:60
  8.3 0.9 broadcast_in_dim.2
  9.2 8.5 %all-to-all-start = ((bf16[8,80,512]{2,1,0:T(8,128)(2,1)}), bf16[8,80,512]{2,1,0:T(8,128)(2,1)S(1)}, u32[]{:S(2)}, u32[]{:S(2)}) async-start(bf16[8,80,512]{2,1,0:T(8,128)(2,1)} %broadcast_in_dim.2), calls=%async_computation | async-start | bytes 1310720 | tf_op jit(solution)/shard_map/all_to_all | solution.py:64
  17.6 0.0 copy-done.2
  17.6 0.1 collective-permute-start.8
  17.8 6.3 %collective-permute-done.9.o2 = bf16[256,1280]{1,0:T(8,128)(2,1)S(1)} collective-permute-done((bf16[256,1280]{1,0:T(8,128)(2,1)}, bf16[256,1280]{1,0:T(8,128)(2,1)S(1)}, u32[]{:S(2)}, u32[]{:S(2)}) %collective-permute-start.9) | collective-permute-done | bytes 655392 | tf_op jit(solution)/shard_map/ppermute | solution.py:60
  24.1 0.1 collective-permute-start.10
  24.2 0.0 copy-done.18
  24.2 0.0 copy-done.12
  24.2 0.8 copy-done.14
  25.0 0.8 copy-done.16
  25.9 2.4 %shard_map.101 = (bf16[256,512]{1,0:T(8,128)(2,1)}, f32[4,256,256]{2,1,0:T(8,128)S(1)}) custom-call(s32[8]{0:T(128)S(1)} %bitcast.8, bf16[256,512]{1,0:T(8,128)(2,1)S(1)} %copy-done.12, bf16[256,128]{1,0:T(8,128)(2,1)S(1)} %copy-done.14, bf16[256,128]{1,0:T(8,128)(2,1)S(1)} %copy-done.16), custom_call_target="tpu_custom_call" | custom-call | flops 134217728 | bytes 2097152 | tf_op jit(solution)/shard_map/pallas_call | solution.py:78
  28.3 1.0 copy-done
  29.3 1.6 %collective-permute-start = (bf16[256,512]{1,0:T(8,128)(2,1)}, bf16[256,512]{1,0:T(8,128)(2,1)S(1)}, u32[]{:S(2)}, u32[]{:S(2)}) collective-permute-start(bf16[256,512]{1,0:T(8,128)(2,1)} %get-tuple-element.19), channel_id=1, source_target_pairs={{0,0},{1,4},{2,64},{3,68},{4,1},{5,5},{6,65},{7,69},{8,8},{9,12},{... | collective-permute-start | bytes 786440 | tf_op jit(solution)/shard_map/ppermute | solution.py:60
  30.9 2.4 %collective-permute-start.1 = (bf16[256,512]{1,0:T(8,128)(2,1)}, bf16[256,512]{1,0:T(8,128)(2,1)}, u32[]{:S(2)}, u32[]{:S(2)}) collective-permute-start(bf16[256,512]{1,0:T(8,128)(2,1)} %get-tuple-element.19), channel_id=1, source_target_pairs={{0,1},{1,5},{2,65},{3,69},{4,2},{5,6},{6,66},{7,70},{8,9},{9,13},{... | collective-permute-start | bytes 786440 | tf_op jit(solution)/shard_map/ppermute | solution.py:60
  33.3 1.3 %collective-permute-start.2 = (bf16[256,512]{1,0:T(8,128)(2,1)}, bf16[256,512]{1,0:T(8,128)(2,1)}, u32[]{:S(2)}, u32[]{:S(2)}) collective-permute-start(bf16[256,512]{1,0:T(8,128)(2,1)} %get-tuple-element.19), channel_id=1, source_target_pairs={{0,2},{1,6},{2,66},{3,70},{4,3},{5,7},{6,67},{7,71},{8,10},{9,14},... | collective-permute-start | bytes 786440 | tf_op jit(solution)/shard_map/ppermute | solution.py:60
  34.6 0.0 collective-permute-done.r0
  34.6 6.7 %collective-permute-start.3 = (bf16[256,512]{1,0:T(8,128)(2,1)}, bf16[256,512]{1,0:T(8,128)(2,1)}, u32[]{:S(2)}, u32[]{:S(2)}) collective-permute-start(bf16[256,512]{1,0:T(8,128)(2,1)} %get-tuple-element.19), channel_id=1, source_target_pairs={{0,3},{1,7},{2,67},{3,71},{4,0},{5,4},{6,64},{7,68},{8,11},{9,15},... | collective-permute-start | bytes 786440 | tf_op jit(solution)/shard_map/ppermute | solution.py:60
  41.3 1.9 %collective-permute-done.1.r1 = bf16[256,512]{1,0:T(8,128)(2,1)} collective-permute-done((bf16[256,512]{1,0:T(8,128)(2,1)}, bf16[256,512]{1,0:T(8,128)(2,1)}, u32[]{:S(2)}, u32[]{:S(2)}) %collective-permute-start.1) | collective-permute-done | bytes 262176 | tf_op jit(solution)/shard_map/ppermute | solution.py:60
  43.3 0.0 all-to-all-done.w0
  43.3 1.4 %collective-permute-start.5 = (bf16[8,80,512]{2,1,0:T(8,128)(2,1)S(1)}, bf16[8,80,512]{2,1,0:T(8,128)(2,1)}, u32[]{:S(2)}, u32[]{:S(2)}) collective-permute-start(bf16[8,80,512]{2,1,0:T(8,128)(2,1)S(1)} %all-to-all-done.w0), channel_id=1, source_target_pairs={{0,192},{1,193},{2,194},{3,195},{4,196},{5,197},{6,198},{7,199},{8... | collective-permute-start | bytes 1966088 | tf_op jit(solution)/shard_map/ppermute | solution.py:60
  44.7 0.1 pad_add_fusion.place._
  44.8 11.6 %collective-permute-done.2.r2 = bf16[256,512]{1,0:T(8,128)(2,1)} collective-permute-done((bf16[256,512]{1,0:T(8,128)(2,1)}, bf16[256,512]{1,0:T(8,128)(2,1)}, u32[]{:S(2)}, u32[]{:S(2)}) %collective-permute-start.2) | collective-permute-done | bytes 262176 | tf_op jit(solution)/shard_map/ppermute | solution.py:60
  56.4 0.0 collective-permute-done.3.r3
  56.4 0.0 collective-permute-done.8.o1
  56.4 0.0 collective-permute-done.10.o3
  56.4 0.0 copy-start.8
  56.4 4.3 %shard_map.107 = bf16[1280,512]{1,0:T(8,128)(2,1)} custom-call(s32[3]{0:T(128)S(1)} %pad_add_fusion.place._, bf16[256,1280]{1,0:T(8,128)(2,1)S(1)} %copy-done.2, bf16[256,1280]{1,0:T(8,128)(2,1)S(1)} %collective-permute-done.8.o1, bf16[256,1280]{1,0:T(8,128)(2,1)S(1)} %collective-permute-done.9.o2, bf16[256,1280]{1,0:T(8,128)(2,1)S(1)} %collective-permute-done.10.o3, ...), custom_call_target="tpu_custom_call" | custom-call | flops 1342177280 | bytes 6291456 | tf_op jit(solution)/shard_map/pallas_call | solution.py:78
  60.7 0.0 copy-done.10
  60.8 0.8 copy-done.4
  61.6 8.6 %all-to-all-start.1 = ((bf16[8,160,512]{2,1,0:T(8,128)(2,1)}), bf16[8,160,512]{2,1,0:T(8,128)(2,1)}, u32[]{:S(2)}, u32[]{:S(2)}) async-start(bf16[8,160,512]{2,1,0:T(8,128)(2,1)} %bitcast.5), calls=%async_computation.1 | async-start | bytes 2621440 | tf_op jit(solution)/shard_map/all_to_all | solution.py:64
  70.2 0.0 collective-permute-done.5.w1
  70.2 2.4 %shard_map.102 = (bf16[2,256,1280]{2,1,0:T(8,128)(2,1)S(1)}, bf16[2,256,512]{2,1,0:T(8,128)(2,1)S(1)}, bf16[1280,512]{1,0:T(8,128)(2,1)S(1)}) custom-call(s32[3]{0:T(128)S(1)} %pad_add_fusion.place._, bf16[256,512]{1,0:T(8,128)(2,1)S(1)} %collective-permute-done.r0, bf16[256,512]{1,0:T(8,128)(2,1)} %collective-permute-done.1.r1, ...), custom_call_target="tpu_custom_call" | custom-call | flops 671088640 | bytes 6291456 | tf_op jit(solution)/shard_map/pallas_call | solution.py:78
  72.6 1.3 %collective-permute-start.6 = (bf16[2,256,1280]{2,1,0:T(8,128)(2,1)S(1)}, bf16[2,256,1280]{2,1,0:T(8,128)(2,1)S(1)}, u32[]{:S(2)}, u32[]{:S(2)}) collective-permute-start(bf16[2,256,1280]{2,1,0:T(8,128)(2,1)S(1)} %get-tuple-element.22), channel_id=1, source_target_pairs={{0,4},{1,5},{2,6},{3,7},{4,0},{5,1},{6,2},{7,3},{8,12},{9,13},{10,... | collective-permute-start | bytes 3932168 | tf_op jit(solution)/shard_map/ppermute | solution.py:60
  73.9 2.7 %collective-permute-done.6.pair = bf16[2,256,1280]{2,1,0:T(8,128)(2,1)S(1)} collective-permute-done((bf16[2,256,1280]{2,1,0:T(8,128)(2,1)S(1)}, bf16[2,256,1280]{2,1,0:T(8,128)(2,1)S(1)}, u32[]{:S(2)}, u32[]{:S(2)}) %collective-permute-start.6) | collective-permute-done | bytes 1310752 | tf_op jit(solution)/shard_map/ppermute | solution.py:60
  76.6 1.9 %shard_map.103 = bf16[256,1280]{1,0:T(8,128)(2,1)} custom-call(s32[3]{0:T(128)S(1)} %pad_add_fusion.place._, bf16[2,256,512]{2,1,0:T(8,128)(2,1)S(1)} %get-tuple-element.20.att, bf16[1280,512]{1,0:T(8,128)(2,1)S(1)} %get-tuple-element.21.wt, bf16[2,256,1280]{2,1,0:T(8,128)(2,1)S(1)} %collective-permute-done.6.pair), custom_call_target="tpu_custom_call" | custom-call | flops 335544320 | bytes 3145728 | tf_op jit(solution)/shard_map/pallas_call | solution.py:78
  78.5 1.8 %collective-permute-start.7 = (bf16[256,1280]{1,0:T(8,128)(2,1)}, bf16[256,1280]{1,0:T(8,128)(2,1)}, u32[]{:S(2)}, u32[]{:S(2)}) collective-permute-start(bf16[256,1280]{1,0:T(8,128)(2,1)} %shard_map.103), channel_id=1, source_target_pairs={{0,64},{1,65},{2,66},{3,67},{4,68},{5,69},{6,70},{7,71},{8,72},{9,... | collective-permute-start | bytes 1966088 | tf_op jit(solution)/shard_map/ppermute | solution.py:60
  80.3 0.0 copy-done.9
  80.3 0.0 copy-start.15
  80.3 0.0 copy-start.17
  80.3 2.9 %shard_map.105 = (bf16[256,512]{1,0:T(8,128)(2,1)}, bf16[256,512]{1,0:T(8,128)(2,1)}, bf16[256,512]{1,0:T(8,128)(2,1)}, bf16[256,512]{1,0:T(8,128)(2,1)}) custom-call(s32[3]{0:T(128)S(1)} %pad_add_fusion.place._, bf16[256,1280]{1,0:T(8,128)(2,1)S(1)} %copy-done.3, bf16[256,1280]{1,0:T(8,128)(2,1)S(1)} %copy-done.7, bf16[256,1280]{1,0:T(8,128)(2,1)S(1)} %copy-done.5, ...), custom_call_target="tpu_custom_call" | custom-call | flops 1342177280 | bytes 6291456 | tf_op jit(solution)/shard_map/pallas_call | solution.py:78
  83.2 3.7 %collective-permute-start.11 = (bf16[256,512]{1,0:T(8,128)(2,1)}, bf16[256,512]{1,0:T(8,128)(2,1)}, u32[]{:S(2)}, u32[]{:S(2)}) collective-permute-start(bf16[256,512]{1,0:T(8,128)(2,1)} %get-tuple-element.23), channel_id=1, source_target_pairs={{0,0},{1,4},{2,64},{3,68},{4,1},{5,5},{6,65},{7,69},{8,8},{9,12},{... | collective-permute-start | bytes 786440 | tf_op jit(solution)/shard_map/ppermute | solution.py:60
  87.0 0.0 collective-permute-start.12
  87.0 2.8 %collective-permute-start.13 = (bf16[256,512]{1,0:T(8,128)(2,1)}, bf16[256,512]{1,0:T(8,128)(2,1)}, u32[]{:S(2)}, u32[]{:S(2)}) collective-permute-start(bf16[256,512]{1,0:T(8,128)(2,1)} %get-tuple-element.25), channel_id=1, source_target_pairs={{0,64},{1,68},{2,0},{3,4},{4,65},{5,69},{6,1},{7,5},{8,72},{9,76},... | collective-permute-start | bytes 786440 | tf_op jit(solution)/shard_map/ppermute | solution.py:60
  89.7 0.8 collective-permute-start.14
  90.5 15.5 %all-to-all-done.1.blocks = bf16[8,160,512]{2,1,0:T(8,128)(2,1)} async-done(((bf16[8,160,512]{2,1,0:T(8,128)(2,1)}), bf16[8,160,512]{2,1,0:T(8,128)(2,1)}, u32[]{:S(2)}, u32[]{:S(2)}) %all-to-all-start.1) | async-done | bytes 1310752 | tf_op jit(solution)/shard_map/all_to_all | solution.py:64
  106.1 1.6 %shard_map.108 = (bf16[80,512]{1,0:T(8,128)(2,1)S(1)}, bf16[80,512]{1,0:T(8,128)(2,1)S(1)}) custom-call(s32[3]{0:T(128)S(1)} %pad_add_fusion.place._, bf16[8,160,512]{2,1,0:T(8,128)(2,1)} %all-to-all-done.1.blocks), custom_call_target="tpu_custom_call" | custom-call | bytes 2097152 | tf_op jit(solution)/shard_map/pallas_call | solution.py:78
  107.7 0.0 collective-permute-done.11.a0
  107.7 1.9 %collective-permute-start.16 = (bf16[80,512]{1,0:T(8,128)(2,1)S(1)}, bf16[80,512]{1,0:T(8,128)(2,1)S(1)}, u32[]{:S(2)}, u32[]{:S(2)}) collective-permute-start(bf16[80,512]{1,0:T(8,128)(2,1)S(1)} %get-tuple-element.32), channel_id=1, source_target_pairs={{0,4},{1,68},{2,132},{3,196},{4,5},{5,69},{6,133},{7,197},{8,12},{... | collective-permute-start | bytes 245768 | tf_op jit(solution)/shard_map/ppermute | solution.py:60
  109.6 0.0 collective-permute-done.12.a1
  109.6 1.9 %collective-permute-start.15 = (bf16[80,512]{1,0:T(8,128)(2,1)S(1)}, bf16[80,512]{1,0:T(8,128)(2,1)S(1)}, u32[]{:S(2)}, u32[]{:S(2)}) collective-permute-start(bf16[80,512]{1,0:T(8,128)(2,1)S(1)} %get-tuple-element.31), channel_id=1, source_target_pairs={{0,0},{1,64},{2,128},{3,192},{4,1},{5,65},{6,129},{7,193},{8,8},{9... | collective-permute-start | bytes 245768 | tf_op jit(solution)/shard_map/ppermute | solution.py:60
  111.5 0.0 collective-permute-done.13.a2
  111.5 0.0 collective-permute-done.14.a3
  111.6 3.5 %shard_map.106 = (bf16[256,512]{1,0:T(8,128)(2,1)}, bf16[256,128]{1,0:T(8,128)(2,1)}, bf16[256,128]{1,0:T(8,128)(2,1)}) custom-call(s32[3]{0:T(128)S(1)} %pad_add_fusion.place._, bf16[256,512]{1,0:T(8,128)(2,1)} %collective-permute-done.11.a0, bf16[256,512]{1,0:T(8,128)(2,1)} %collective-permute-done.12.a1, bf16[256,512]{1,0:T(8,128)(2,1)} %collective-permute-done.13.a2, ...), custom_call_target="tpu_custom_call" | custom-call | flops 335544320 | bytes 3145728 | tf_op jit(solution)/shard_map/pallas_call | solution.py:78
  115.1 0.1 collective-permute-done.16
  115.2 6.4 %collective-permute-done.15 = bf16[80,512]{1,0:T(8,128)(2,1)S(1)} collective-permute-done((bf16[80,512]{1,0:T(8,128)(2,1)S(1)}, bf16[80,512]{1,0:T(8,128)(2,1)S(1)}, u32[]{:S(2)}, u32[]{:S(2)}) %collective-permute-start.15) | collective-permute-done | bytes 81952 | tf_op jit(solution)/shard_map/ppermute | solution.py:60
  121.6 0.7 add_bitcast_fusion
  122.2 0.0 collective-permute-done.7.across
  122.3 2.5 %shard_map.104 = bf16[256,1280]{1,0:T(8,128)(2,1)} custom-call(s32[3]{0:T(128)S(1)} %pad_add_fusion.place._, bf16[2,256,512]{2,1,0:T(8,128)(2,1)S(1)} %get-tuple-element.20.att, bf16[1280,512]{1,0:T(8,128)(2,1)S(1)} %get-tuple-element.21.wt, bf16[2,256,1280]{2,1,0:T(8,128)(2,1)S(1)} %collective-permute-done.6.pair, ...), custom_call_target="tpu_custom_call" | custom-call | flops 335544320 | bytes 4194304 | tf_op jit(solution)/shard_map/pallas_call | solution.py:78
  (23 shorter events, 0.0 us)
Async XLA Ops:
  0.6 17.0 %copy-start.2 = (bf16[256,1280]{1,0:T(8,128)(2,1)S(1)}, bf16[256,1280]{1,0:T(8,128)(2,1)}, u32[]{:S(2)}) copy-start(bf16[256,1280]{1,0:T(8,128)(2,1)} %o0.3) | copy-start | bytes 1966084
  0.6 23.6 %copy-start.18 = (s32[1,8]{1,0:T(1,128)S(1)}, s32[1,8]{1,0:T(1,128)}, u32[]{:S(2)}) copy-start(s32[1,8]{1,0:T(1,128)} %param.11) | copy-start | bytes 100
  0.7 23.6 %copy-start.12 = (bf16[256,512]{1,0:T(8,128)(2,1)S(1)}, bf16[256,512]{1,0:T(8,128)(2,1)}, u32[]{:S(2)}) copy-start(bf16[256,512]{1,0:T(8,128)(2,1)} %q_ref.3) | copy-start | bytes 786436
  0.7 7.6 %collective-permute-start.4 = (bf16[80,512]{1,0:T(8,128)(2,1)}, bf16[80,512]{1,0:T(8,128)(2,1)S(1)}, u32[]{:S(2)}, u32[]{:S(2)}) collective-permute-start(bf16[80,512]{1,0:T(8,128)(2,1)} %bitcast.9), channel_id=1, source_target_pairs={{0,0},{1,4},{2,64},{3,68},{4,192},{5,196},{6,128},{7,132},{8,8},{9... | collective-permute-start | bytes 245768 | tf_op jit(solution)/shard_map/ppermute | solution.py:60
  5.6 18.4 %collective-permute-start.9 = (bf16[256,1280]{1,0:T(8,128)(2,1)}, bf16[256,1280]{1,0:T(8,128)(2,1)S(1)}, u32[]{:S(2)}, u32[]{:S(2)}) collective-permute-start(bf16[256,1280]{1,0:T(8,128)(2,1)} %o0.3), channel_id=1, source_target_pairs={{0,64},{1,65},{2,66},{3,67},{4,68},{5,69},{6,70},{7,71},{8,72},{9,... | collective-permute-start | bytes 1966088 | tf_op jit(solution)/shard_map/ppermute | solution.py:60
  9.2 34.1 %all-to-all-start = ((bf16[8,80,512]{2,1,0:T(8,128)(2,1)}), bf16[8,80,512]{2,1,0:T(8,128)(2,1)S(1)}, u32[]{:S(2)}, u32[]{:S(2)}) async-start(bf16[8,80,512]{2,1,0:T(8,128)(2,1)} %broadcast_in_dim.2), calls=%async_computation | async-start | bytes 1310720 | tf_op jit(solution)/shard_map/all_to_all | solution.py:64
  17.6 38.8 %collective-permute-start.8 = (bf16[256,1280]{1,0:T(8,128)(2,1)S(1)}, bf16[256,1280]{1,0:T(8,128)(2,1)S(1)}, u32[]{:S(2)}, u32[]{:S(2)}) collective-permute-start(bf16[256,1280]{1,0:T(8,128)(2,1)S(1)} %copy-done.2), channel_id=1, source_target_pairs={{0,4},{1,5},{2,6},{3,7},{4,0},{5,1},{6,2},{7,3},{8,12},{9,13},{10,... | collective-permute-start | bytes 1966088 | tf_op jit(solution)/shard_map/ppermute | solution.py:60
  24.1 32.3 %collective-permute-start.10 = (bf16[256,1280]{1,0:T(8,128)(2,1)S(1)}, bf16[256,1280]{1,0:T(8,128)(2,1)S(1)}, u32[]{:S(2)}, u32[]{:S(2)}) collective-permute-start(bf16[256,1280]{1,0:T(8,128)(2,1)S(1)} %collective-permute-done.9.o2), channel_id=1, source_target_pairs={{0,4},{1,5},{2,6},{3,7},{4,0},{5,1},{6,2},{7,3},{8,12},{9,13},{10,... | collective-permute-start | bytes 1966088 | tf_op jit(solution)/shard_map/ppermute | solution.py:60
  24.2 0.8 copy-start.14
  25.0 0.8 copy-start.16
  28.3 1.0 copy-start
  29.3 5.3 %collective-permute-start = (bf16[256,512]{1,0:T(8,128)(2,1)}, bf16[256,512]{1,0:T(8,128)(2,1)S(1)}, u32[]{:S(2)}, u32[]{:S(2)}) collective-permute-start(bf16[256,512]{1,0:T(8,128)(2,1)} %get-tuple-element.19), channel_id=1, source_target_pairs={{0,0},{1,4},{2,64},{3,68},{4,1},{5,5},{6,65},{7,69},{8,8},{9,12},{... | collective-permute-start | bytes 786440 | tf_op jit(solution)/shard_map/ppermute | solution.py:60
  30.9 12.4 %collective-permute-start.1 = (bf16[256,512]{1,0:T(8,128)(2,1)}, bf16[256,512]{1,0:T(8,128)(2,1)}, u32[]{:S(2)}, u32[]{:S(2)}) collective-permute-start(bf16[256,512]{1,0:T(8,128)(2,1)} %get-tuple-element.19), channel_id=1, source_target_pairs={{0,1},{1,5},{2,65},{3,69},{4,2},{5,6},{6,66},{7,70},{8,9},{9,13},{... | collective-permute-start | bytes 786440 | tf_op jit(solution)/shard_map/ppermute | solution.py:60
  33.3 23.1 %collective-permute-start.2 = (bf16[256,512]{1,0:T(8,128)(2,1)}, bf16[256,512]{1,0:T(8,128)(2,1)}, u32[]{:S(2)}, u32[]{:S(2)}) collective-permute-start(bf16[256,512]{1,0:T(8,128)(2,1)} %get-tuple-element.19), channel_id=1, source_target_pairs={{0,2},{1,6},{2,66},{3,70},{4,3},{5,7},{6,67},{7,71},{8,10},{9,14},... | collective-permute-start | bytes 786440 | tf_op jit(solution)/shard_map/ppermute | solution.py:60
  34.6 21.8 %collective-permute-start.3 = (bf16[256,512]{1,0:T(8,128)(2,1)}, bf16[256,512]{1,0:T(8,128)(2,1)}, u32[]{:S(2)}, u32[]{:S(2)}) collective-permute-start(bf16[256,512]{1,0:T(8,128)(2,1)} %get-tuple-element.19), channel_id=1, source_target_pairs={{0,3},{1,7},{2,67},{3,71},{4,0},{5,4},{6,64},{7,68},{8,11},{9,15},... | collective-permute-start | bytes 786440 | tf_op jit(solution)/shard_map/ppermute | solution.py:60
  43.3 17.5 %copy-start.10 = (bf16[8,80,512]{2,1,0:T(8,128)(2,1)}, bf16[8,80,512]{2,1,0:T(8,128)(2,1)S(1)}, u32[]{:S(2)}) copy-start(bf16[8,80,512]{2,1,0:T(8,128)(2,1)S(1)} %all-to-all-done.w0) | copy-start | bytes 1966084
  43.3 26.9 %collective-permute-start.5 = (bf16[8,80,512]{2,1,0:T(8,128)(2,1)S(1)}, bf16[8,80,512]{2,1,0:T(8,128)(2,1)}, u32[]{:S(2)}, u32[]{:S(2)}) collective-permute-start(bf16[8,80,512]{2,1,0:T(8,128)(2,1)S(1)} %all-to-all-done.w0), channel_id=1, source_target_pairs={{0,192},{1,193},{2,194},{3,195},{4,196},{5,197},{6,198},{7,199},{8... | collective-permute-start | bytes 1966088 | tf_op jit(solution)/shard_map/ppermute | solution.py:60
  56.4 4.3 %copy-start.6 = (bf16[256,1280]{1,0:T(8,128)(2,1)}, bf16[256,1280]{1,0:T(8,128)(2,1)S(1)}, u32[]{:S(2)}) copy-start(bf16[256,1280]{1,0:T(8,128)(2,1)S(1)} %collective-permute-done.8.o1) | copy-start | bytes 1966084
  56.4 4.3 %copy-start.8 = (bf16[256,1280]{1,0:T(8,128)(2,1)}, bf16[256,1280]{1,0:T(8,128)(2,1)S(1)}, u32[]{:S(2)}) copy-start(bf16[256,1280]{1,0:T(8,128)(2,1)S(1)} %collective-permute-done.10.o3) | copy-start | bytes 1966084
  60.7 0.8 copy-start.4
  61.6 8.6 %copy-start.11 = (bf16[8,80,512]{2,1,0:T(8,128)(2,1)S(1)}, bf16[8,80,512]{2,1,0:T(8,128)(2,1)}, u32[]{:S(2)}) copy-start(bf16[8,80,512]{2,1,0:T(8,128)(2,1)} %copy-done.10) | copy-start | bytes 1966084
  61.6 44.5 %all-to-all-start.1 = ((bf16[8,160,512]{2,1,0:T(8,128)(2,1)}), bf16[8,160,512]{2,1,0:T(8,128)(2,1)}, u32[]{:S(2)}, u32[]{:S(2)}) async-start(bf16[8,160,512]{2,1,0:T(8,128)(2,1)} %bitcast.5), calls=%async_computation.1 | async-start | bytes 2621440 | tf_op jit(solution)/shard_map/all_to_all | solution.py:64
  72.6 3.9 %collective-permute-start.6 = (bf16[2,256,1280]{2,1,0:T(8,128)(2,1)S(1)}, bf16[2,256,1280]{2,1,0:T(8,128)(2,1)S(1)}, u32[]{:S(2)}, u32[]{:S(2)}) collective-permute-start(bf16[2,256,1280]{2,1,0:T(8,128)(2,1)S(1)} %get-tuple-element.22), channel_id=1, source_target_pairs={{0,4},{1,5},{2,6},{3,7},{4,0},{5,1},{6,2},{7,3},{8,12},{9,13},{10,... | collective-permute-start | bytes 3932168 | tf_op jit(solution)/shard_map/ppermute | solution.py:60
  76.6 3.7 %copy-start.3 = (bf16[256,1280]{1,0:T(8,128)(2,1)S(1)}, bf16[256,1280]{1,0:T(8,128)(2,1)}, u32[]{:S(2)}) copy-start(bf16[256,1280]{1,0:T(8,128)(2,1)} %o0.3) | copy-start | bytes 1966084
  76.6 3.7 %copy-start.5 = (bf16[256,1280]{1,0:T(8,128)(2,1)S(1)}, bf16[256,1280]{1,0:T(8,128)(2,1)}, u32[]{:S(2)}) copy-start(bf16[256,1280]{1,0:T(8,128)(2,1)} %copy-done.4) | copy-start | bytes 1966084
  76.6 3.7 %copy-start.7 = (bf16[256,1280]{1,0:T(8,128)(2,1)S(1)}, bf16[256,1280]{1,0:T(8,128)(2,1)}, u32[]{:S(2)}) copy-start(bf16[256,1280]{1,0:T(8,128)(2,1)} %copy-done.6) | copy-start | bytes 1966084
  76.6 3.7 %copy-start.9 = (bf16[256,1280]{1,0:T(8,128)(2,1)S(1)}, bf16[256,1280]{1,0:T(8,128)(2,1)}, u32[]{:S(2)}) copy-start(bf16[256,1280]{1,0:T(8,128)(2,1)} %copy-done.8) | copy-start | bytes 1966084
  78.5 43.7 %collective-permute-start.7 = (bf16[256,1280]{1,0:T(8,128)(2,1)}, bf16[256,1280]{1,0:T(8,128)(2,1)}, u32[]{:S(2)}, u32[]{:S(2)}) collective-permute-start(bf16[256,1280]{1,0:T(8,128)(2,1)} %shard_map.103), channel_id=1, source_target_pairs={{0,64},{1,65},{2,66},{3,67},{4,68},{5,69},{6,70},{7,71},{8,72},{9,... | collective-permute-start | bytes 1966088 | tf_op jit(solution)/shard_map/ppermute | solution.py:60
  80.3 31.3 %copy-start.15 = (bf16[256,128]{1,0:T(8,128)(2,1)S(1)}, bf16[256,128]{1,0:T(8,128)(2,1)}, u32[]{:S(2)}) copy-start(bf16[256,128]{1,0:T(8,128)(2,1)} %k_ref.3) | copy-start | bytes 196612
  80.3 31.3 %copy-start.17 = (bf16[256,128]{1,0:T(8,128)(2,1)S(1)}, bf16[256,128]{1,0:T(8,128)(2,1)}, u32[]{:S(2)}) copy-start(bf16[256,128]{1,0:T(8,128)(2,1)} %v_ref.3) | copy-start | bytes 196612
  83.2 28.3 %copy-start.13 = (bf16[256,512]{1,0:T(8,128)(2,1)S(1)}, bf16[256,512]{1,0:T(8,128)(2,1)}, u32[]{:S(2)}) copy-start(bf16[256,512]{1,0:T(8,128)(2,1)} %q_ref.3) | copy-start | bytes 786436
  83.2 24.4 %collective-permute-start.11 = (bf16[256,512]{1,0:T(8,128)(2,1)}, bf16[256,512]{1,0:T(8,128)(2,1)}, u32[]{:S(2)}, u32[]{:S(2)}) collective-permute-start(bf16[256,512]{1,0:T(8,128)(2,1)} %get-tuple-element.23), channel_id=1, source_target_pairs={{0,0},{1,4},{2,64},{3,68},{4,1},{5,5},{6,65},{7,69},{8,8},{9,12},{... | collective-permute-start | bytes 786440 | tf_op jit(solution)/shard_map/ppermute | solution.py:60
  87.0 22.6 %collective-permute-start.12 = (bf16[256,512]{1,0:T(8,128)(2,1)}, bf16[256,512]{1,0:T(8,128)(2,1)}, u32[]{:S(2)}, u32[]{:S(2)}) collective-permute-start(bf16[256,512]{1,0:T(8,128)(2,1)} %get-tuple-element.24), channel_id=1, source_target_pairs={{0,4},{1,64},{2,68},{3,0},{4,5},{5,65},{6,69},{7,1},{8,12},{9,72},... | collective-permute-start | bytes 786440 | tf_op jit(solution)/shard_map/ppermute | solution.py:60
  87.0 24.6 %collective-permute-start.13 = (bf16[256,512]{1,0:T(8,128)(2,1)}, bf16[256,512]{1,0:T(8,128)(2,1)}, u32[]{:S(2)}, u32[]{:S(2)}) collective-permute-start(bf16[256,512]{1,0:T(8,128)(2,1)} %get-tuple-element.25), channel_id=1, source_target_pairs={{0,64},{1,68},{2,0},{3,4},{4,65},{5,69},{6,1},{7,5},{8,72},{9,76},... | collective-permute-start | bytes 786440 | tf_op jit(solution)/shard_map/ppermute | solution.py:60
  89.7 21.8 %collective-permute-start.14 = (bf16[256,512]{1,0:T(8,128)(2,1)}, bf16[256,512]{1,0:T(8,128)(2,1)}, u32[]{:S(2)}, u32[]{:S(2)}) collective-permute-start(bf16[256,512]{1,0:T(8,128)(2,1)} %get-tuple-element.26), channel_id=1, source_target_pairs={{0,68},{1,0},{2,4},{3,64},{4,69},{5,1},{6,5},{7,65},{8,76},{9,8},{... | collective-permute-start | bytes 786440 | tf_op jit(solution)/shard_map/ppermute | solution.py:60
  106.1 5.5 %copy-start.1 = (f32[4,256,256]{2,1,0:T(8,128)S(1)}, f32[4,256,256]{2,1,0:T(8,128)}, u32[]{:S(2)}) copy-start(f32[4,256,256]{2,1,0:T(8,128)} %copy-done) | copy-start | bytes 3145732
  107.7 7.5 %collective-permute-start.16 = (bf16[80,512]{1,0:T(8,128)(2,1)S(1)}, bf16[80,512]{1,0:T(8,128)(2,1)S(1)}, u32[]{:S(2)}, u32[]{:S(2)}) collective-permute-start(bf16[80,512]{1,0:T(8,128)(2,1)S(1)} %get-tuple-element.32), channel_id=1, source_target_pairs={{0,4},{1,68},{2,132},{3,196},{4,5},{5,69},{6,133},{7,197},{8,12},{... | collective-permute-start | bytes 245768 | tf_op jit(solution)/shard_map/ppermute | solution.py:60
  109.6 12.0 %collective-permute-start.15 = (bf16[80,512]{1,0:T(8,128)(2,1)S(1)}, bf16[80,512]{1,0:T(8,128)(2,1)S(1)}, u32[]{:S(2)}, u32[]{:S(2)}) collective-permute-start(bf16[80,512]{1,0:T(8,128)(2,1)S(1)} %get-tuple-element.31), channel_id=1, source_target_pairs={{0,0},{1,64},{2,128},{3,192},{4,1},{5,65},{6,129},{7,193},{8,8},{9... | collective-permute-start | bytes 245768 | tf_op jit(solution)/shard_map/ppermute | solution.py:60

commit v2 on v1

--- a/solution.py
+++ b/solution.py
@@ -45,14 +45,8 @@
 TO_OWNER = [
     route(lambda x, z, c, y, k=k: (y, z, (x // 2 + k) % 2, 2 * low_of(x) + c)) for k in range(2)
 ]
-HEADS_OUT = [
-    route(lambda x, z, c, y, k=k: (chip(x // 2, y // 2), z, y % 2, (2 * low_of(x) + c + k) % 4))
-    for k in range(4)
-]
-HEADS_BACK = [
-    route(lambda x, z, c, y, k=k: (chip(x // 2, (y + k) % 4 // 2), z, (y + k) % 2, 2 * low_of(x) + c))
-    for k in range(4)
-]
+TURN = route(lambda x, z, c, y: (chip(x // 2, y // 2), z, y % 2, 2 * low_of(x) + c))
+ALONG_Y = [route(lambda x, z, c, y, k=k: (x, z, c, (y + k) % 4)) for k in range(1, 4)]
 Z_GROUPS = [[(x * NZ + z) * NC + c for z in range(NZ)] for x in range(NX) for c in range(NC)]
 
 
@@ -116,15 +110,18 @@
         att_ref[:, at] = dot(prob.astype(BF), v_ref[...], ((1,), (0,))).astype(BF)
 
 
-def backward_body(_, a0, a1, a2, a3, q_ref, k_ref, v_ref, prob_ref, dq_ref, dk_ref, dv_ref):
+def sum_four_body(_, a0, a1, a2, a3, out):
+    out[...] = (
+        (a0[...].astype(F32) + a1[...].astype(F32)) + (a2[...].astype(F32) + a3[...].astype(F32))
+    ).astype(BF)
+
+
+def backward_body(_, up_ref, q_ref, k_ref, v_ref, prob_ref, dq_ref, dk_ref, dv_ref):
     key_sum = jnp.zeros((TOK, HEAD), F32)
     value_sum = jnp.zeros((TOK, HEAD), F32)
     for h in range(HEADS):
         at = slice(h * HEAD, (h + 1) * HEAD)
-        up = (
-            (a0[:, at].astype(F32) + a1[:, at].astype(F32))
-            + (a2[:, at].astype(F32) + a3[:, at].astype(F32))
-        ).astype(BF)
+        up = up_ref[:, at]
         prob = prob_ref[h]
         prob_grad = dot(up, v_ref[...], ((1,), (1,)))
         delta = jnp.sum(prob * prob_grad, axis=-1, keepdims=True)
@@ -207,7 +204,8 @@
         flops=4 * 4 * TOK * TOK * HEAD,
         moved=2 << 20,
     )(doc_lengths[0], query_rows, key_rows, value_matrix)
-    heads = [send(attended, pairs) for pairs in HEADS_OUT]
+    heads = send(attended, TURN)
+    heads = [heads] + [send(heads, pairs) for pairs in ALONG_Y]
 
     big = 2 * 4 * TOK * COLS * GROUP
     grad_part = call(
@@ -242,14 +240,16 @@
         flops=big,
         moved=6 << 20,
     )(place, *cols, wt_all)
-    upstream = [send(partial, pairs) for partial, pairs in zip(partials, HEADS_BACK)]
+    partials = [partials[0]] + [send(p, pairs) for p, pairs in zip(partials[1:], ALONG_Y)]
+    upstream = call(sum_four_body, shape(TOK, GROUP), moved=1 << 20)(place, *partials)
+    upstream = send(upstream, TURN)
 
     query_grad, key_grad, value_grad = call(
         backward_body,
         (shape(TOK, GROUP), shape(TOK, HEAD), shape(TOK, HEAD)),
         flops=5 * 4 * 2 * TOK * TOK * HEAD,
         moved=3 << 20,
-    )(place, *upstream, query_rows, key_rows, value_matrix, prob)
+    )(place, upstream, query_rows, key_rows, value_matrix, prob)
 
     pieces = call(sum_z_body, (shape(SHARD, GROUP),) * 2, moved=2 << 20)(place, grad_rows)
     pieces = [send(piece, pairs).astype(F32) for piece, pairs in zip(pieces, TO_OWNER)]

time: 125 us -> 130 us (1.040)
  the two profiles are of different devices: /device:TPU:6 before, /device:TPU:17 now
where the time goes in v2:
time: 130 us; the launch traced here: 129 us
  starting transfers between devices  64.6 us (50%)
  waiting for transfers between devices  35.7 us (27%)
  Pallas kernels  21.5 us (17%)
  local copies, waits for them, and re-layouts  5.55 us (4%)
    ppermute x17, starting transfers between devices, send(): return lax.ppermute(value, AXES, pairs)  49.5 us
    ppermute x17, waiting for transfers between devices, send(): return lax.ppermute(value, AXES, pairs)  35.2 us
    pallas_call x9, Pallas kernels, run(): pl.pallas_call(body, out_shape=outs, grid=(1,), in_specs=[pl.BlockSpec(me...  21.5 us
    all_to_all x2, starting transfers between devices, exchange(): lax.all_to_all(blocks, 'dp', 0, 0, axis_index_groups=groups, tiled=True)  15.1 us
    unnamed x36, local copies, waits for them, and re-layouts  4.66 us
  transfers between devices with their start and end apart: 19, of which 7 were waited for; matrix products, arithmetic and copies ran while one was open for 1% of the time, Pallas kernels for 15%

profile of v2, /device:TPU:17, one launch (start us, length us, event | category | flops | bytes accessed | tf_op | source)
XLA Modules:
  0.0 129.1 jit_solution(16232493310704195062)
XLA Ops:
  0.6 0.0 copy-start.2
  0.6 0.0 copy-start.17
  0.7 0.0 copy-start.12
  0.7 1.3 %collective-permute-start.9 = (bf16[256,1280]{1,0:T(8,128)(2,1)}, bf16[256,1280]{1,0:T(8,128)(2,1)S(1)}, u32[]{:S(2)}, u32[]{:S(2)}) collective-permute-start(bf16[256,1280]{1,0:T(8,128)(2,1)} %o0.3), channel_id=1, source_target_pairs={{0,64},{1,65},{2,66},{3,67},{4,68},{5,69},{6,70},{7,71},{8,72},{9,... | collective-permute-start | bytes 1966088 | tf_op jit(solution)/shard_map/ppermute | solution.py:54
  2.0 5.0 %collective-permute-start.4 = (bf16[80,512]{1,0:T(8,128)(2,1)}, bf16[80,512]{1,0:T(8,128)(2,1)S(1)}, u32[]{:S(2)}, u32[]{:S(2)}) collective-permute-start(bf16[80,512]{1,0:T(8,128)(2,1)} %bitcast.9), channel_id=1, source_target_pairs={{0,0},{1,4},{2,64},{3,68},{4,192},{5,196},{6,128},{7,132},{8,8},{9... | collective-permute-start | bytes 245768 | tf_op jit(solution)/shard_map/ppermute | solution.py:54
  6.9 15.1 %collective-permute-done.4 = bf16[80,512]{1,0:T(8,128)(2,1)S(1)} collective-permute-done((bf16[80,512]{1,0:T(8,128)(2,1)}, bf16[80,512]{1,0:T(8,128)(2,1)S(1)}, u32[]{:S(2)}, u32[]{:S(2)}) %collective-permute-start.4) | collective-permute-done | bytes 81952 | tf_op jit(solution)/shard_map/ppermute | solution.py:54
  22.0 0.9 broadcast_in_dim.2
  22.9 8.2 %all-to-all-start = ((bf16[8,80,512]{2,1,0:T(8,128)(2,1)}), bf16[8,80,512]{2,1,0:T(8,128)(2,1)S(1)}, u32[]{:S(2)}, u32[]{:S(2)}) async-start(bf16[8,80,512]{2,1,0:T(8,128)(2,1)} %broadcast_in_dim.2), calls=%async_computation | async-start | bytes 1310720 | tf_op jit(solution)/shard_map/all_to_all | solution.py:58
  31.1 0.9 collective-permute-start.8
  32.0 0.0 collective-permute-done.9.o2
  32.0 0.1 collective-permute-start.10
  32.2 0.8 copy-done.13
  33.0 0.8 copy-done.15
  33.8 1.7 %shard_map.101 = (bf16[256,512]{1,0:T(8,128)(2,1)S(1)}, f32[4,256,256]{2,1,0:T(8,128)S(1)}) custom-call(s32[8]{0:T(128)S(1)} %bitcast.8, bf16[256,512]{1,0:T(8,128)(2,1)S(1)} %copy-done.12, bf16[256,128]{1,0:T(8,128)(2,1)S(1)} %copy-done.13, bf16[256,128]{1,0:T(8,128)(2,1)S(1)} %copy-done.15), custom_call_target="tpu_custom_call" | custom-call | flops 134217728 | bytes 2097152 | tf_op jit(solution)/shard_map/pallas_call | solution.py:72
  35.5 0.0 copy-start
  35.5 1.0 copy-done
  36.5 1.9 %collective-permute-start = (bf16[256,512]{1,0:T(8,128)(2,1)S(1)}, bf16[256,512]{1,0:T(8,128)(2,1)}, u32[]{:S(2)}, u32[]{:S(2)}) collective-permute-start(bf16[256,512]{1,0:T(8,128)(2,1)S(1)} %get-tuple-element.19), channel_id=1, source_target_pairs={{0,0},{1,4},{2,64},{3,68},{4,1},{5,5},{6,65},{7,69},{8,8},{9,12},{... | collective-permute-start | bytes 786440 | tf_op jit(solution)/shard_map/ppermute | solution.py:54
  38.4 7.2 %collective-permute-done.r0 = bf16[256,512]{1,0:T(8,128)(2,1)} collective-permute-done((bf16[256,512]{1,0:T(8,128)(2,1)S(1)}, bf16[256,512]{1,0:T(8,128)(2,1)}, u32[]{:S(2)}, u32[]{:S(2)}) %collective-permute-start) | collective-permute-done | bytes 262176 | tf_op jit(solution)/shard_map/ppermute | solution.py:54
  45.6 0.0 collective-permute-start.1
  45.6 0.0 collective-permute-start.2
  45.6 1.5 %collective-permute-start.3 = (bf16[256,512]{1,0:T(8,128)(2,1)}, bf16[256,512]{1,0:T(8,128)(2,1)}, u32[]{:S(2)}, u32[]{:S(2)}) collective-permute-start(bf16[256,512]{1,0:T(8,128)(2,1)} %collective-permute-done.r0), channel_id=1, source_target_pairs={{0,3},{1,0},{2,1},{3,2},{4,7},{5,4},{6,5},{7,6},{8,11},{9,8},{10,9... | collective-permute-start | bytes 786440 | tf_op jit(solution)/shard_map/ppermute | solution.py:54
  47.1 0.1 pad_add_fusion.place._
  47.2 4.2 %collective-permute-done.1.r1 = bf16[256,512]{1,0:T(8,128)(2,1)} collective-permute-done((bf16[256,512]{1,0:T(8,128)(2,1)}, bf16[256,512]{1,0:T(8,128)(2,1)}, u32[]{:S(2)}, u32[]{:S(2)}) %collective-permute-start.1) | collective-permute-done | bytes 262176 | tf_op jit(solution)/shard_map/ppermute | solution.py:54
  51.4 0.5 all-to-all-done.w0
  51.9 7.2 %collective-permute-start.5 = (bf16[8,80,512]{2,1,0:T(8,128)(2,1)S(1)}, bf16[8,80,512]{2,1,0:T(8,128)(2,1)}, u32[]{:S(2)}, u32[]{:S(2)}) collective-permute-start(bf16[8,80,512]{2,1,0:T(8,128)(2,1)S(1)} %all-to-all-done.w0), channel_id=1, source_target_pairs={{0,192},{1,193},{2,194},{3,195},{4,196},{5,197},{6,198},{7,199},{8... | collective-permute-start | bytes 1966088 | tf_op jit(solution)/shard_map/ppermute | solution.py:54
  59.1 0.0 collective-permute-done.2.r2
  59.1 0.0 collective-permute-done.3.r3
  59.1 0.0 collective-permute-done.8.o1
  59.1 0.0 collective-permute-done.10.o3
  59.1 4.4 %shard_map.108 = bf16[1280,512]{1,0:T(8,128)(2,1)} custom-call(s32[3]{0:T(128)S(1)} %pad_add_fusion.place._, bf16[256,1280]{1,0:T(8,128)(2,1)S(1)} %copy-done.2, bf16[256,1280]{1,0:T(8,128)(2,1)S(1)} %collective-permute-done.8.o1, bf16[256,1280]{1,0:T(8,128)(2,1)S(1)} %collective-permute-done.9.o2, bf16[256,1280]{1,0:T(8,128)(2,1)S(1)} %collective-permute-done.10.o3, ...), custom_call_target="tpu_custom_call" | custom-call | flops 1342177280 | bytes 6291456 | tf_op jit(solution)/shard_map/pallas_call | solution.py:72
  63.5 0.0 copy-done.10
  63.5 0.8 copy-done.4
  64.4 7.0 %all-to-all-start.1 = ((bf16[8,160,512]{2,1,0:T(8,128)(2,1)}), bf16[8,160,512]{2,1,0:T(8,128)(2,1)}, u32[]{:S(2)}, u32[]{:S(2)}) async-start(bf16[8,160,512]{2,1,0:T(8,128)(2,1)} %bitcast.5), calls=%async_computation.1 | async-start | bytes 2621440 | tf_op jit(solution)/shard_map/all_to_all | solution.py:58
  71.4 0.0 collective-permute-done.5.w1
  71.4 0.0 copy-done.11
  71.4 2.6 %shard_map.102 = (bf16[2,256,1280]{2,1,0:T(8,128)(2,1)S(1)}, bf16[2,256,512]{2,1,0:T(8,128)(2,1)S(1)}, bf16[1280,512]{1,0:T(8,128)(2,1)S(1)}) custom-call(s32[3]{0:T(128)S(1)} %pad_add_fusion.place._, bf16[256,512]{1,0:T(8,128)(2,1)} %collective-permute-done.r0, bf16[256,512]{1,0:T(8,128)(2,1)} %collective-permute-done.1.r1, ...), custom_call_target="tpu_custom_call" | custom-call | flops 671088640 | bytes 6291456 | tf_op jit(solution)/shard_map/pallas_call | solution.py:72
  74.0 3.5 %collective-permute-start.6 = (bf16[2,256,1280]{2,1,0:T(8,128)(2,1)S(1)}, bf16[2,256,1280]{2,1,0:T(8,128)(2,1)S(1)}, u32[]{:S(2)}, u32[]{:S(2)}) collective-permute-start(bf16[2,256,1280]{2,1,0:T(8,128)(2,1)S(1)} %get-tuple-element.22), channel_id=1, source_target_pairs={{0,4},{1,5},{2,6},{3,7},{4,0},{5,1},{6,2},{7,3},{8,12},{9,13},{10,... | collective-permute-start | bytes 3932168 | tf_op jit(solution)/shard_map/ppermute | solution.py:54
  77.6 1.1 copy-done.9
  78.6 2.2 %shard_map.105 = (bf16[256,512]{1,0:T(8,128)(2,1)S(1)}, bf16[256,512]{1,0:T(8,128)(2,1)S(1)}, bf16[256,512]{1,0:T(8,128)(2,1)S(1)}, bf16[256,512]{1,0:T(8,128)(2,1)S(1)}) custom-call(s32[3]{0:T(128)S(1)} %pad_add_fusion.place._, bf16[256,1280]{1,0:T(8,128)(2,1)S(1)} %copy-done.3, bf16[256,1280]{1,0:T(8,128)(2,1)S(1)} %copy-done.7, ...), custom_call_target="tpu_custom_call" | custom-call | flops 1342177280 | bytes 6291456 | tf_op jit(solution)/shard_map/pallas_call | solution.py:72
  80.9 0.1 collective-permute-start.11
  80.9 0.7 collective-permute-start.12
  81.6 0.9 collective-permute-start.13
  82.5 0.0 collective-permute-done.6.pair
  82.5 1.9 %shard_map.103 = bf16[256,1280]{1,0:T(8,128)(2,1)} custom-call(s32[3]{0:T(128)S(1)} %pad_add_fusion.place._, bf16[2,256,512]{2,1,0:T(8,128)(2,1)S(1)} %get-tuple-element.20.att, bf16[1280,512]{1,0:T(8,128)(2,1)S(1)} %get-tuple-element.21.wt, bf16[2,256,1280]{2,1,0:T(8,128)(2,1)S(1)} %collective-permute-done.6.pair), custom_call_target="tpu_custom_call" | custom-call | flops 335544320 | bytes 3145728 | tf_op jit(solution)/shard_map/pallas_call | solution.py:72
  84.5 6.9 %collective-permute-start.7 = (bf16[256,1280]{1,0:T(8,128)(2,1)}, bf16[256,1280]{1,0:T(8,128)(2,1)}, u32[]{:S(2)}, u32[]{:S(2)}) collective-permute-start(bf16[256,1280]{1,0:T(8,128)(2,1)} %shard_map.103), channel_id=1, source_target_pairs={{0,64},{1,65},{2,66},{3,67},{4,68},{5,69},{6,70},{7,71},{8,72},{9,... | collective-permute-start | bytes 1966088 | tf_op jit(solution)/shard_map/ppermute | solution.py:54
  91.4 3.1 %collective-permute-done.11.a1 = bf16[256,512]{1,0:T(8,128)(2,1)S(1)} collective-permute-done((bf16[256,512]{1,0:T(8,128)(2,1)S(1)}, bf16[256,512]{1,0:T(8,128)(2,1)S(1)}, u32[]{:S(2)}, u32[]{:S(2)}) %collective-permute-start.11) | collective-permute-done | bytes 262176 | tf_op jit(solution)/shard_map/ppermute | solution.py:54
  94.5 0.0 collective-permute-done.12.a2
  94.5 1.5 %collective-permute-done.13.a3 = bf16[256,512]{1,0:T(8,128)(2,1)S(1)} collective-permute-done((bf16[256,512]{1,0:T(8,128)(2,1)S(1)}, bf16[256,512]{1,0:T(8,128)(2,1)S(1)}, u32[]{:S(2)}, u32[]{:S(2)}) %collective-permute-start.13) | collective-permute-done | bytes 262176 | tf_op jit(solution)/shard_map/ppermute | solution.py:54
  96.0 1.4 %shard_map.106 = bf16[256,512]{1,0:T(8,128)(2,1)} custom-call(s32[3]{0:T(128)S(1)} %pad_add_fusion.place._, bf16[256,512]{1,0:T(8,128)(2,1)S(1)} %get-tuple-element.23.a0, bf16[256,512]{1,0:T(8,128)(2,1)S(1)} %collective-permute-done.11.a1, bf16[256,512]{1,0:T(8,128)(2,1)S(1)} %collective-permute-done.12.a2, bf16[256,512]{1,0:T(8,128)(2,1)S(1)} %collective-permute-done.13.a3), custom_call_target="tpu_custom_call" | custom-call | bytes 1048576 | tf_op jit(solution)/shard_map/pallas_call | solution.py:72
  97.4 7.8 %collective-permute-start.14 = (bf16[256,512]{1,0:T(8,128)(2,1)}, bf16[256,512]{1,0:T(8,128)(2,1)}, u32[]{:S(2)}, u32[]{:S(2)}) collective-permute-start(bf16[256,512]{1,0:T(8,128)(2,1)} %shard_map.106), channel_id=1, source_target_pairs={{0,0},{1,4},{2,64},{3,68},{4,1},{5,5},{6,65},{7,69},{8,8},{9,12},{... | collective-permute-start | bytes 786440 | tf_op jit(solution)/shard_map/ppermute | solution.py:54
  105.2 0.0 all-to-all-done.1.blocks
  105.2 1.6 %shard_map.109 = (bf16[80,512]{1,0:T(8,128)(2,1)S(1)}, bf16[80,512]{1,0:T(8,128)(2,1)S(1)}) custom-call(s32[3]{0:T(128)S(1)} %pad_add_fusion.place._, bf16[8,160,512]{2,1,0:T(8,128)(2,1)} %all-to-all-done.1.blocks), custom_call_target="tpu_custom_call" | custom-call | bytes 2097152 | tf_op jit(solution)/shard_map/pallas_call | solution.py:72
  106.8 9.4 %collective-permute-start.16 = (bf16[80,512]{1,0:T(8,128)(2,1)S(1)}, bf16[80,512]{1,0:T(8,128)(2,1)S(1)}, u32[]{:S(2)}, u32[]{:S(2)}) collective-permute-start(bf16[80,512]{1,0:T(8,128)(2,1)S(1)} %get-tuple-element.32), channel_id=1, source_target_pairs={{0,4},{1,68},{2,132},{3,196},{4,5},{5,69},{6,133},{7,197},{8,12},{... | collective-permute-start | bytes 245768 | tf_op jit(solution)/shard_map/ppermute | solution.py:54
  116.2 2.3 %collective-permute-start.15 = (bf16[80,512]{1,0:T(8,128)(2,1)S(1)}, bf16[80,512]{1,0:T(8,128)(2,1)S(1)}, u32[]{:S(2)}, u32[]{:S(2)}) collective-permute-start(bf16[80,512]{1,0:T(8,128)(2,1)S(1)} %get-tuple-element.31), channel_id=1, source_target_pairs={{0,0},{1,64},{2,128},{3,192},{4,1},{5,65},{6,129},{7,193},{8,8},{9... | collective-permute-start | bytes 245768 | tf_op jit(solution)/shard_map/ppermute | solution.py:54
  118.5 0.0 collective-permute-done.14.up_ref
  118.5 0.0 copy-done.14
  118.6 0.0 copy-done.16
  118.6 0.0 copy-done.1
  118.6 3.3 %shard_map.107 = (bf16[256,512]{1,0:T(8,128)(2,1)}, bf16[256,128]{1,0:T(8,128)(2,1)}, bf16[256,128]{1,0:T(8,128)(2,1)}) custom-call(s32[3]{0:T(128)S(1)} %pad_add_fusion.place._, bf16[256,512]{1,0:T(8,128)(2,1)} %collective-permute-done.14.up_ref, bf16[256,512]{1,0:T(8,128)(2,1)S(1)} %copy-done.12, bf16[256,128]{1,0:T(8,128)(2,1)S(1)} %copy-done.14, ...), custom_call_target="tpu_custom_call" | custom-call | flops 335544320 | bytes 3145728 | tf_op jit(solution)/shard_map/pallas_call | solution.py:72
  121.8 0.0 collective-permute-done.16
  121.9 4.0 %collective-permute-done.15 = bf16[80,512]{1,0:T(8,128)(2,1)S(1)} collective-permute-done((bf16[80,512]{1,0:T(8,128)(2,1)S(1)}, bf16[80,512]{1,0:T(8,128)(2,1)S(1)}, u32[]{:S(2)}, u32[]{:S(2)}) %collective-permute-start.15) | collective-permute-done | bytes 81952 | tf_op jit(solution)/shard_map/ppermute | solution.py:54
  125.9 0.7 add_bitcast_fusion
  126.6 0.0 collective-permute-done.7.across
  126.6 2.5 %shard_map.104 = bf16[256,1280]{1,0:T(8,128)(2,1)} custom-call(s32[3]{0:T(128)S(1)} %pad_add_fusion.place._, bf16[2,256,512]{2,1,0:T(8,128)(2,1)S(1)} %get-tuple-element.20.att, bf16[1280,512]{1,0:T(8,128)(2,1)S(1)} %get-tuple-element.21.wt, bf16[2,256,1280]{2,1,0:T(8,128)(2,1)S(1)} %collective-permute-done.6.pair, ...), custom_call_target="tpu_custom_call" | custom-call | flops 335544320 | bytes 4194304 | tf_op jit(solution)/shard_map/pallas_call | solution.py:72
  (22 shorter events, 0.0 us)
Async XLA Ops:
  0.6 30.5 %copy-start.2 = (bf16[256,1280]{1,0:T(8,128)(2,1)S(1)}, bf16[256,1280]{1,0:T(8,128)(2,1)}, u32[]{:S(2)}) copy-start(bf16[256,1280]{1,0:T(8,128)(2,1)} %o0.3) | copy-start | bytes 1966084
  0.6 31.5 %copy-start.17 = (s32[1,8]{1,0:T(1,128)S(1)}, s32[1,8]{1,0:T(1,128)}, u32[]{:S(2)}) copy-start(s32[1,8]{1,0:T(1,128)} %param.11) | copy-start | bytes 100
  0.7 31.5 %copy-start.12 = (bf16[256,512]{1,0:T(8,128)(2,1)S(1)}, bf16[256,512]{1,0:T(8,128)(2,1)}, u32[]{:S(2)}) copy-start(bf16[256,512]{1,0:T(8,128)(2,1)} %q_ref.3) | copy-start | bytes 786436
  0.7 31.4 %collective-permute-start.9 = (bf16[256,1280]{1,0:T(8,128)(2,1)}, bf16[256,1280]{1,0:T(8,128)(2,1)S(1)}, u32[]{:S(2)}, u32[]{:S(2)}) collective-permute-start(bf16[256,1280]{1,0:T(8,128)(2,1)} %o0.3), channel_id=1, source_target_pairs={{0,64},{1,65},{2,66},{3,67},{4,68},{5,69},{6,70},{7,71},{8,72},{9,... | collective-permute-start | bytes 1966088 | tf_op jit(solution)/shard_map/ppermute | solution.py:54
  2.0 20.1 %collective-permute-start.4 = (bf16[80,512]{1,0:T(8,128)(2,1)}, bf16[80,512]{1,0:T(8,128)(2,1)S(1)}, u32[]{:S(2)}, u32[]{:S(2)}) collective-permute-start(bf16[80,512]{1,0:T(8,128)(2,1)} %bitcast.9), channel_id=1, source_target_pairs={{0,0},{1,4},{2,64},{3,68},{4,192},{5,196},{6,128},{7,132},{8,8},{9... | collective-permute-start | bytes 245768 | tf_op jit(solution)/shard_map/ppermute | solution.py:54
  22.9 29.0 %all-to-all-start = ((bf16[8,80,512]{2,1,0:T(8,128)(2,1)}), bf16[8,80,512]{2,1,0:T(8,128)(2,1)S(1)}, u32[]{:S(2)}, u32[]{:S(2)}) async-start(bf16[8,80,512]{2,1,0:T(8,128)(2,1)} %broadcast_in_dim.2), calls=%async_computation | async-start | bytes 1310720 | tf_op jit(solution)/shard_map/all_to_all | solution.py:58
  31.1 28.0 %collective-permute-start.8 = (bf16[256,1280]{1,0:T(8,128)(2,1)S(1)}, bf16[256,1280]{1,0:T(8,128)(2,1)S(1)}, u32[]{:S(2)}, u32[]{:S(2)}) collective-permute-start(bf16[256,1280]{1,0:T(8,128)(2,1)S(1)} %copy-done.2), channel_id=1, source_target_pairs={{0,4},{1,5},{2,6},{3,7},{4,0},{5,1},{6,2},{7,3},{8,12},{9,13},{10,... | collective-permute-start | bytes 1966088 | tf_op jit(solution)/shard_map/ppermute | solution.py:54
  32.0 27.1 %collective-permute-start.10 = (bf16[256,1280]{1,0:T(8,128)(2,1)S(1)}, bf16[256,1280]{1,0:T(8,128)(2,1)S(1)}, u32[]{:S(2)}, u32[]{:S(2)}) collective-permute-start(bf16[256,1280]{1,0:T(8,128)(2,1)S(1)} %collective-permute-done.9.o2), channel_id=1, source_target_pairs={{0,4},{1,5},{2,6},{3,7},{4,0},{5,1},{6,2},{7,3},{8,12},{9,13},{10,... | collective-permute-start | bytes 1966088 | tf_op jit(solution)/shard_map/ppermute | solution.py:54
  32.2 0.8 copy-start.13
  33.0 0.8 copy-start.15
  35.5 1.0 copy-start
  36.5 9.1 %collective-permute-start = (bf16[256,512]{1,0:T(8,128)(2,1)S(1)}, bf16[256,512]{1,0:T(8,128)(2,1)}, u32[]{:S(2)}, u32[]{:S(2)}) collective-permute-start(bf16[256,512]{1,0:T(8,128)(2,1)S(1)} %get-tuple-element.19), channel_id=1, source_target_pairs={{0,0},{1,4},{2,64},{3,68},{4,1},{5,5},{6,65},{7,69},{8,8},{9,12},{... | collective-permute-start | bytes 786440 | tf_op jit(solution)/shard_map/ppermute | solution.py:54
  45.6 5.7 %collective-permute-start.1 = (bf16[256,512]{1,0:T(8,128)(2,1)}, bf16[256,512]{1,0:T(8,128)(2,1)}, u32[]{:S(2)}, u32[]{:S(2)}) collective-permute-start(bf16[256,512]{1,0:T(8,128)(2,1)} %collective-permute-done.r0), channel_id=1, source_target_pairs={{0,1},{1,2},{2,3},{3,0},{4,5},{5,6},{6,7},{7,4},{8,9},{9,10},{10,1... | collective-permute-start | bytes 786440 | tf_op jit(solution)/shard_map/ppermute | solution.py:54
  45.6 13.5 %collective-permute-start.2 = (bf16[256,512]{1,0:T(8,128)(2,1)}, bf16[256,512]{1,0:T(8,128)(2,1)}, u32[]{:S(2)}, u32[]{:S(2)}) collective-permute-start(bf16[256,512]{1,0:T(8,128)(2,1)} %collective-permute-done.r0), channel_id=1, source_target_pairs={{0,2},{1,3},{2,0},{3,1},{4,6},{5,7},{6,4},{7,5},{8,10},{9,11},{10,... | collective-permute-start | bytes 786440 | tf_op jit(solution)/shard_map/ppermute | solution.py:54
  45.6 13.5 %collective-permute-start.3 = (bf16[256,512]{1,0:T(8,128)(2,1)}, bf16[256,512]{1,0:T(8,128)(2,1)}, u32[]{:S(2)}, u32[]{:S(2)}) collective-permute-start(bf16[256,512]{1,0:T(8,128)(2,1)} %collective-permute-done.r0), channel_id=1, source_target_pairs={{0,3},{1,0},{2,1},{3,2},{4,7},{5,4},{6,5},{7,6},{8,11},{9,8},{10,9... | collective-permute-start | bytes 786440 | tf_op jit(solution)/shard_map/ppermute | solution.py:54
  51.9 11.6 %copy-start.10 = (bf16[8,80,512]{2,1,0:T(8,128)(2,1)}, bf16[8,80,512]{2,1,0:T(8,128)(2,1)S(1)}, u32[]{:S(2)}) copy-start(bf16[8,80,512]{2,1,0:T(8,128)(2,1)S(1)} %all-to-all-done.w0) | copy-start | bytes 1966084
  51.9 19.5 %collective-permute-start.5 = (bf16[8,80,512]{2,1,0:T(8,128)(2,1)S(1)}, bf16[8,80,512]{2,1,0:T(8,128)(2,1)}, u32[]{:S(2)}, u32[]{:S(2)}) collective-permute-start(bf16[8,80,512]{2,1,0:T(8,128)(2,1)S(1)} %all-to-all-done.w0), channel_id=1, source_target_pairs={{0,192},{1,193},{2,194},{3,195},{4,196},{5,197},{6,198},{7,199},{8... | collective-permute-start | bytes 1966088 | tf_op jit(solution)/shard_map/ppermute | solution.py:54
  59.1 4.4 %copy-start.6 = (bf16[256,1280]{1,0:T(8,128)(2,1)}, bf16[256,1280]{1,0:T(8,128)(2,1)S(1)}, u32[]{:S(2)}) copy-start(bf16[256,1280]{1,0:T(8,128)(2,1)S(1)} %collective-permute-done.8.o1) | copy-start | bytes 1966084
  59.1 4.4 %copy-start.8 = (bf16[256,1280]{1,0:T(8,128)(2,1)}, bf16[256,1280]{1,0:T(8,128)(2,1)S(1)}, u32[]{:S(2)}) copy-start(bf16[256,1280]{1,0:T(8,128)(2,1)S(1)} %collective-permute-done.10.o3) | copy-start | bytes 1966084
  63.5 0.9 copy-start.4
  64.4 7.0 %copy-start.11 = (bf16[8,80,512]{2,1,0:T(8,128)(2,1)S(1)}, bf16[8,80,512]{2,1,0:T(8,128)(2,1)}, u32[]{:S(2)}) copy-start(bf16[8,80,512]{2,1,0:T(8,128)(2,1)} %copy-done.10) | copy-start | bytes 1966084
  64.4 40.9 %all-to-all-start.1 = ((bf16[8,160,512]{2,1,0:T(8,128)(2,1)}), bf16[8,160,512]{2,1,0:T(8,128)(2,1)}, u32[]{:S(2)}, u32[]{:S(2)}) async-start(bf16[8,160,512]{2,1,0:T(8,128)(2,1)} %bitcast.5), calls=%async_computation.1 | async-start | bytes 2621440 | tf_op jit(solution)/shard_map/all_to_all | solution.py:58
  71.3 6.2 %copy-start.3 = (bf16[256,1280]{1,0:T(8,128)(2,1)S(1)}, bf16[256,1280]{1,0:T(8,128)(2,1)}, u32[]{:S(2)}) copy-start(bf16[256,1280]{1,0:T(8,128)(2,1)} %o0.3) | copy-start | bytes 1966084
  71.3 6.2 %copy-start.5 = (bf16[256,1280]{1,0:T(8,128)(2,1)S(1)}, bf16[256,1280]{1,0:T(8,128)(2,1)}, u32[]{:S(2)}) copy-start(bf16[256,1280]{1,0:T(8,128)(2,1)} %copy-done.4) | copy-start | bytes 1966084
  71.3 6.2 %copy-start.7 = (bf16[256,1280]{1,0:T(8,128)(2,1)S(1)}, bf16[256,1280]{1,0:T(8,128)(2,1)}, u32[]{:S(2)}) copy-start(bf16[256,1280]{1,0:T(8,128)(2,1)} %copy-done.6) | copy-start | bytes 1966084
  74.0 8.5 %collective-permute-start.6 = (bf16[2,256,1280]{2,1,0:T(8,128)(2,1)S(1)}, bf16[2,256,1280]{2,1,0:T(8,128)(2,1)S(1)}, u32[]{:S(2)}, u32[]{:S(2)}) collective-permute-start(bf16[2,256,1280]{2,1,0:T(8,128)(2,1)S(1)} %get-tuple-element.22), channel_id=1, source_target_pairs={{0,4},{1,5},{2,6},{3,7},{4,0},{5,1},{6,2},{7,3},{8,12},{9,13},{10,... | collective-permute-start | bytes 3932168 | tf_op jit(solution)/shard_map/ppermute | solution.py:54
  77.5 1.1 copy-start.9
  80.9 13.6 %collective-permute-start.11 = (bf16[256,512]{1,0:T(8,128)(2,1)S(1)}, bf16[256,512]{1,0:T(8,128)(2,1)S(1)}, u32[]{:S(2)}, u32[]{:S(2)}) collective-permute-start(bf16[256,512]{1,0:T(8,128)(2,1)S(1)} %get-tuple-element.24), channel_id=1, source_target_pairs={{0,1},{1,2},{2,3},{3,0},{4,5},{5,6},{6,7},{7,4},{8,9},{9,10},{10,1... | collective-permute-start | bytes 786440 | tf_op jit(solution)/shard_map/ppermute | solution.py:54
  80.9 13.5 %collective-permute-start.12 = (bf16[256,512]{1,0:T(8,128)(2,1)S(1)}, bf16[256,512]{1,0:T(8,128)(2,1)S(1)}, u32[]{:S(2)}, u32[]{:S(2)}) collective-permute-start(bf16[256,512]{1,0:T(8,128)(2,1)S(1)} %get-tuple-element.25), channel_id=1, source_target_pairs={{0,2},{1,3},{2,0},{3,1},{4,6},{5,7},{6,4},{7,5},{8,10},{9,11},{10,... | collective-permute-start | bytes 786440 | tf_op jit(solution)/shard_map/ppermute | solution.py:54
  81.6 14.4 %collective-permute-start.13 = (bf16[256,512]{1,0:T(8,128)(2,1)S(1)}, bf16[256,512]{1,0:T(8,128)(2,1)S(1)}, u32[]{:S(2)}, u32[]{:S(2)}) collective-permute-start(bf16[256,512]{1,0:T(8,128)(2,1)S(1)} %get-tuple-element.26), channel_id=1, source_target_pairs={{0,3},{1,0},{2,1},{3,2},{4,7},{5,4},{6,5},{7,6},{8,11},{9,8},{10,9... | collective-permute-start | bytes 786440 | tf_op jit(solution)/shard_map/ppermute | solution.py:54
  84.5 42.1 %collective-permute-start.7 = (bf16[256,1280]{1,0:T(8,128)(2,1)}, bf16[256,1280]{1,0:T(8,128)(2,1)}, u32[]{:S(2)}, u32[]{:S(2)}) collective-permute-start(bf16[256,1280]{1,0:T(8,128)(2,1)} %shard_map.103), channel_id=1, source_target_pairs={{0,64},{1,65},{2,66},{3,67},{4,68},{5,69},{6,70},{7,71},{8,72},{9,... | collective-permute-start | bytes 1966088 | tf_op jit(solution)/shard_map/ppermute | solution.py:54
  96.0 22.5 %copy-start.14 = (bf16[256,128]{1,0:T(8,128)(2,1)S(1)}, bf16[256,128]{1,0:T(8,128)(2,1)}, u32[]{:S(2)}) copy-start(bf16[256,128]{1,0:T(8,128)(2,1)} %k_ref.3) | copy-start | bytes 196612
  96.0 22.5 %copy-start.16 = (bf16[256,128]{1,0:T(8,128)(2,1)S(1)}, bf16[256,128]{1,0:T(8,128)(2,1)}, u32[]{:S(2)}) copy-start(bf16[256,128]{1,0:T(8,128)(2,1)} %v_ref.3) | copy-start | bytes 196612
  97.4 21.1 %collective-permute-start.14 = (bf16[256,512]{1,0:T(8,128)(2,1)}, bf16[256,512]{1,0:T(8,128)(2,1)}, u32[]{:S(2)}, u32[]{:S(2)}) collective-permute-start(bf16[256,512]{1,0:T(8,128)(2,1)} %shard_map.106), channel_id=1, source_target_pairs={{0,0},{1,4},{2,64},{3,68},{4,1},{5,5},{6,65},{7,69},{8,8},{9,12},{... | collective-permute-start | bytes 786440 | tf_op jit(solution)/shard_map/ppermute | solution.py:54
  105.2 13.3 %copy-start.1 = (f32[4,256,256]{2,1,0:T(8,128)S(1)}, f32[4,256,256]{2,1,0:T(8,128)}, u32[]{:S(2)}) copy-start(f32[4,256,256]{2,1,0:T(8,128)} %copy-done) | copy-start | bytes 3145732
  106.8 15.0 %collective-permute-start.16 = (bf16[80,512]{1,0:T(8,128)(2,1)S(1)}, bf16[80,512]{1,0:T(8,128)(2,1)S(1)}, u32[]{:S(2)}, u32[]{:S(2)}) collective-permute-start(bf16[80,512]{1,0:T(8,128)(2,1)S(1)} %get-tuple-element.32), channel_id=1, source_target_pairs={{0,4},{1,68},{2,132},{3,196},{4,5},{5,69},{6,133},{7,197},{8,12},{... | collective-permute-start | bytes 245768 | tf_op jit(solution)/shard_map/ppermute | solution.py:54
  116.2 9.7 %collective-permute-start.15 = (bf16[80,512]{1,0:T(8,128)(2,1)S(1)}, bf16[80,512]{1,0:T(8,128)(2,1)S(1)}, u32[]{:S(2)}, u32[]{:S(2)}) collective-permute-start(bf16[80,512]{1,0:T(8,128)(2,1)S(1)} %get-tuple-element.31), channel_id=1, source_target_pairs={{0,0},{1,64},{2,128},{3,192},{4,1},{5,65},{6,129},{7,193},{8,8},{9... | collective-permute-start | bytes 245768 | tf_op jit(solution)/shard_map/ppermute | solution.py:54

commit v3 on v2

--- a/solution.py
+++ b/solution.py
@@ -145,36 +145,36 @@
         grad_ref[at, :] = total.astype(BF)
 
 
-def layer_pair_body(place, r0, r1, r2, r3, w0, w1, pair_ref, att_ref, wt_ref, att):
-    g, y, high = place[0], place[1], place[2]
+def layer_pair_body(place, r0, r1, r2, r3, wt, pair_ref, att_ref, att):
+    g, y = place[0], place[1]
     for k, ref in enumerate((r0, r1, r2, r3)):
         att[jnp.bitwise_xor((y + 4 - k) % 4, g)] = ref[...]
+    for i in range(2):
+        pair_ref[i] = dot(att[2 * i + 1], wt[...], ((1,), (1,))).astype(BF)
+        att_ref[i] = att[2 * i]
+
+
+def layer_across_body(_, att, wt, pair, out):
+    out[...] = (dot(att[1], wt[...], ((1,), (1,))) + pair[1].astype(F32)).astype(BF)
+
+
+def layer_sum_body(_, att, wt, pair, across, out):
+    out[...] = (
+        dot(att[0], wt[...], ((1,), (1,))) + pair[0].astype(F32) + across[...].astype(F32)
+    ).astype(BF)
+
+
+def attn_grad_body(place, o0, o1, o2, o3, w0, w1, g0, g1, g2, g3, wt_ref, og):
+    g, y, high = place[0], place[1], place[2]
     for k, ref in enumerate((w0, w1)):
         c = (high + k) % 2
         for z in range(NZ):
             wt_ref[pl.ds(pl.multiple_of(z * 160 + c * SHARD, 16), SHARD), :] = ref[z]
-    for i in range(2):
-        pair_ref[i] = dot(att[2 * i + 1], wt_ref[...], ((1,), (1,))).astype(BF)
-        att_ref[i] = att[2 * i]
-
-
-def layer_across_body(_, att, wt, pair, out):
-    out[...] = (dot(att[1], wt[...], ((1,), (1,))) + pair[1].astype(F32)).astype(BF)
-
-
-def layer_sum_body(_, att, wt, pair, across, out):
-    out[...] = (
-        dot(att[0], wt[...], ((1,), (1,))) + pair[0].astype(F32) + across[...].astype(F32)
-    ).astype(BF)
-
-
-def attn_grad_body(place, o0, o1, o2, o3, wt, g0, g1, g2, g3, og):
-    g, y = place[0], place[1]
     for r, ref in enumerate((o0, o1, o2, o3)):
         og[r] = ref[...]
     for k, ref in enumerate((g0, g1, g2, g3)):
         at = jnp.bitwise_xor((y + k) % 4, g)
-        ref[...] = dot(og[at], wt[...], ((1,), (0,))).astype(BF)
+        ref[...] = dot(og[at], wt_ref[...], ((1,), (0,))).astype(BF)
 
 
 def sum_z_body(place, blocks, o0, o1):
@@ -203,6 +203,7 @@
         (shape(TOK, GROUP), shape(HEADS, TOK, TOK, dtype=F32)),
         flops=4 * 4 * TOK * TOK * HEAD,
         moved=2 << 20,
+        limit=63,
     )(doc_lengths[0], query_rows, key_rows, value_matrix)
     heads = send(attended, TURN)
     heads = [heads] + [send(heads, pairs) for pairs in ALONG_Y]
@@ -217,13 +218,21 @@
     )(place, *cols, *heads)
     grad_rows = exchange(grad_part.reshape(NZ, 2 * SHARD, GROUP), Z_GROUPS)
 
-    pair, attended_two, wt_all = call(
+    *partials, wt_all = call(
+        attn_grad_body,
+        (shape(TOK, GROUP),) * 4 + (shape(COLS, GROUP),),
+        scratch=(pltpu.VMEM((4, TOK, COLS), BF),),
+        flops=big,
+        moved=6 << 20,
+    )(place, *cols, *blocks)
+
+    pair, attended_two = call(
         layer_pair_body,
-        (shape(2, TOK, COLS), shape(2, TOK, GROUP), shape(COLS, GROUP)),
+        (shape(2, TOK, COLS), shape(2, TOK, GROUP)),
         scratch=(pltpu.VMEM((4, TOK, GROUP), BF),),
         flops=big // 2,
-        moved=6 << 20,
-    )(place, *heads, *blocks)
+        moved=4 << 20,
+    )(place, *heads, wt_all)
     pair = send(pair, SWAP)
     across = call(
         layer_across_body, shape(TOK, COLS), flops=big // 4, moved=3 << 20
@@ -233,13 +242,6 @@
         layer_sum_body, shape(TOK, COLS), flops=big // 4, moved=4 << 20
     )(place, attended_two, wt_all, pair, across)
 
-    partials = call(
-        attn_grad_body,
-        (shape(TOK, GROUP),) * 4,
-        scratch=(pltpu.VMEM((4, TOK, COLS), BF),),
-        flops=big,
-        moved=6 << 20,
-    )(place, *cols, wt_all)
     partials = [partials[0]] + [send(p, pairs) for p, pairs in zip(partials[1:], ALONG_Y)]
     upstream = call(sum_four_body, shape(TOK, GROUP), moved=1 << 20)(place, *partials)
     upstream = send(upstream, TURN)

time: 130 us -> 123 us (0.946)
  the two profiles are of different devices: /device:TPU:17 before, /device:TPU:16 now
where the time goes in v3:
time: 123 us
  starting transfers between devices  50.2 us (41%)
  waiting for transfers between devices  45.2 us (37%)
  Pallas kernels  22.7 us (18%)
  local copies, waits for them, and re-layouts  2.83 us (2%)
    ppermute x17, waiting for transfers between devices, send(): return lax.ppermute(value, AXES, pairs)  40.3 us
    ppermute x17, starting transfers between devices, send(): return lax.ppermute(value, AXES, pairs)  33.6 us
    pallas_call x9, Pallas kernels, run(): pl.pallas_call(body, out_shape=outs, grid=(1,), in_specs=[pl.BlockSpec(me...  22.7 us
    all_to_all x2, starting transfers between devices, exchange(): lax.all_to_all(blocks, 'dp', 0, 0, axis_index_groups=groups, tiled=True)  16.6 us
    all_to_all x2, waiting for transfers between devices, exchange(): lax.all_to_all(blocks, 'dp', 0, 0, axis_index_groups=groups, tiled=True)  4.93 us
  transfers between devices with their start and end apart: 19, of which 9 were waited for; matrix products, arithmetic and copies ran while one was open for 1% of the time, Pallas kernels for 17%

profile of v3, /device:TPU:16, one launch (start us, length us, event | category | flops | bytes accessed | tf_op | source)
XLA Modules:
  0.0 122.5 jit_solution(16794817458629474219)
XLA Ops:
  0.6 0.0 copy-start.1
  0.6 3.3 %collective-permute-start.7 = (bf16[80,512]{1,0:T(8,128)(2,1)}, bf16[80,512]{1,0:T(8,128)(2,1)S(1)}, u32[]{:S(2)}, u32[]{:S(2)}) collective-permute-start(bf16[80,512]{1,0:T(8,128)(2,1)} %bitcast.8), channel_id=1, source_target_pairs={{0,0},{1,4},{2,64},{3,68},{4,192},{5,196},{6,128},{7,132},{8,8},{9... | collective-permute-start | bytes 245768 | tf_op jit(solution)/shard_map/ppermute | solution.py:54
  4.0 0.8 collective-permute-start.5
  4.7 7.3 %collective-permute-done.7 = bf16[80,512]{1,0:T(8,128)(2,1)S(1)} collective-permute-done((bf16[80,512]{1,0:T(8,128)(2,1)}, bf16[80,512]{1,0:T(8,128)(2,1)S(1)}, u32[]{:S(2)}, u32[]{:S(2)}) %collective-permute-start.7) | collective-permute-done | bytes 81952 | tf_op jit(solution)/shard_map/ppermute | solution.py:54
  12.0 0.9 broadcast_in_dim.2
  12.9 8.5 %all-to-all-start = ((bf16[8,80,512]{2,1,0:T(8,128)(2,1)}), bf16[8,80,512]{2,1,0:T(8,128)(2,1)}, u32[]{:S(2)}, u32[]{:S(2)}) async-start(bf16[8,80,512]{2,1,0:T(8,128)(2,1)} %broadcast_in_dim.2), calls=%async_computation | async-start | bytes 1310720 | tf_op jit(solution)/shard_map/all_to_all | solution.py:58
  21.3 0.0 copy-done.1
  21.3 0.1 collective-permute-start.4
  21.4 0.0 collective-permute-done.5.o2
  21.5 0.5 collective-permute-start.6
  21.9 3.1 %shard_map.101 = (bf16[256,512]{1,0:T(8,128)(2,1)}, f32[4,256,256]{2,1,0:T(8,128)}) custom-call(s32[8]{0:T(128)} %bitcast.9, bf16[256,512]{1,0:T(8,128)(2,1)} %q_ref.3, bf16[256,128]{1,0:T(8,128)(2,1)} %k_ref.3, bf16[256,128]{1,0:T(8,128)(2,1)} %v_ref.3), custom_call_target="tpu_custom_call" | custom-call | flops 134217728 | bytes 2097152 | tf_op jit(solution)/shard_map/pallas_call | solution.py:72
  25.0 3.3 %collective-permute-start = (bf16[256,512]{1,0:T(8,128)(2,1)}, bf16[256,512]{1,0:T(8,128)(2,1)S(1)}, u32[]{:S(2)}, u32[]{:S(2)}) collective-permute-start(bf16[256,512]{1,0:T(8,128)(2,1)} %get-tuple-element.19), channel_id=1, source_target_pairs={{0,0},{1,4},{2,64},{3,68},{4,1},{5,5},{6,65},{7,69},{8,8},{9,12},{... | collective-permute-start | bytes 786440 | tf_op jit(solution)/shard_map/ppermute | solution.py:54
  28.3 9.5 %collective-permute-done.r0 = bf16[256,512]{1,0:T(8,128)(2,1)S(1)} collective-permute-done((bf16[256,512]{1,0:T(8,128)(2,1)}, bf16[256,512]{1,0:T(8,128)(2,1)S(1)}, u32[]{:S(2)}, u32[]{:S(2)}) %collective-permute-start) | collective-permute-done | bytes 262176 | tf_op jit(solution)/shard_map/ppermute | solution.py:54
  37.8 0.0 collective-permute-start.3
  37.8 2.5 %collective-permute-start.2 = (bf16[256,512]{1,0:T(8,128)(2,1)S(1)}, bf16[256,512]{1,0:T(8,128)(2,1)S(1)}, u32[]{:S(2)}, u32[]{:S(2)}) collective-permute-start(bf16[256,512]{1,0:T(8,128)(2,1)S(1)} %collective-permute-done.r0), channel_id=1, source_target_pairs={{0,2},{1,3},{2,0},{3,1},{4,6},{5,7},{6,4},{7,5},{8,10},{9,11},{10,... | collective-permute-start | bytes 786440 | tf_op jit(solution)/shard_map/ppermute | solution.py:54
  40.3 0.0 collective-permute-start.1
  40.3 6.7 %collective-permute-done.3.r3 = bf16[256,512]{1,0:T(8,128)(2,1)S(1)} collective-permute-done((bf16[256,512]{1,0:T(8,128)(2,1)S(1)}, bf16[256,512]{1,0:T(8,128)(2,1)S(1)}, u32[]{:S(2)}, u32[]{:S(2)}) %collective-permute-start.3) | collective-permute-done | bytes 262176 | tf_op jit(solution)/shard_map/ppermute | solution.py:54
  47.0 0.0 all-to-all-done.w0
  47.0 2.4 %collective-permute-start.8 = (bf16[8,80,512]{2,1,0:T(8,128)(2,1)}, bf16[8,80,512]{2,1,0:T(8,128)(2,1)S(1)}, u32[]{:S(2)}, u32[]{:S(2)}) collective-permute-start(bf16[8,80,512]{2,1,0:T(8,128)(2,1)} %all-to-all-done.w0), channel_id=1, source_target_pairs={{0,192},{1,193},{2,194},{3,195},{4,196},{5,197},{6,198},{7,199},{8... | collective-permute-start | bytes 1966088 | tf_op jit(solution)/shard_map/ppermute | solution.py:54
  49.4 0.1 pad_add_fusion.place._
  49.5 0.0 collective-permute-done.2.r2
  49.5 2.7 %collective-permute-done.1.r1 = bf16[256,512]{1,0:T(8,128)(2,1)S(1)} collective-permute-done((bf16[256,512]{1,0:T(8,128)(2,1)S(1)}, bf16[256,512]{1,0:T(8,128)(2,1)S(1)}, u32[]{:S(2)}, u32[]{:S(2)}) %collective-permute-start.1) | collective-permute-done | bytes 262176 | tf_op jit(solution)/shard_map/ppermute | solution.py:54
  52.2 0.0 collective-permute-done.4.o1
  52.2 0.0 collective-permute-done.6.o3
  52.2 4.2 %shard_map.108 = bf16[1280,512]{1,0:T(8,128)(2,1)} custom-call(s32[3]{0:T(128)S(1)} %pad_add_fusion.place._, bf16[256,1280]{1,0:T(8,128)(2,1)S(1)} %copy-done.1, bf16[256,1280]{1,0:T(8,128)(2,1)} %collective-permute-done.4.o1, bf16[256,1280]{1,0:T(8,128)(2,1)} %collective-permute-done.5.o2, bf16[256,1280]{1,0:T(8,128)(2,1)} %collective-permute-done.6.o3, ...), custom_call_target="tpu_custom_call" | custom-call | flops 1342177280 | bytes 6291456 | tf_op jit(solution)/shard_map/pallas_call | solution.py:72
  56.4 8.1 %all-to-all-start.1 = ((bf16[8,160,512]{2,1,0:T(8,128)(2,1)}), bf16[8,160,512]{2,1,0:T(8,128)(2,1)}, u32[]{:S(2)}, u32[]{:S(2)}) async-start(bf16[8,160,512]{2,1,0:T(8,128)(2,1)} %bitcast.5), calls=%async_computation.1 | async-start | bytes 2621440 | tf_op jit(solution)/shard_map/all_to_all | solution.py:58
  64.5 0.0 collective-permute-done.8.w1
  64.5 0.0 copy-start.5
  64.5 0.8 copy-done.5
  65.4 0.0 copy-start.6
  65.4 1.1 copy-done.6
  66.4 3.4 %shard_map.102 = (bf16[256,512]{1,0:T(8,128)(2,1)S(1)}, bf16[256,512]{1,0:T(8,128)(2,1)S(1)}, bf16[256,512]{1,0:T(8,128)(2,1)S(1)}, bf16[256,512]{1,0:T(8,128)(2,1)S(1)}, bf16[1280,512]{1,0:T(8,128)(2,1)S(1)}) custom-call(s32[3]{0:T(128)S(1)} %pad_add_fusion.place._, bf16[256,1280]{1,0:T(8,128)(2,1)S(1)} %copy-done.1, ...), custom_call_target="tpu_custom_call" | custom-call | flops 1342177280 | bytes 6291456 | tf_op jit(solution)/shard_map/pallas_call | solution.py:72
  69.9 1.4 %shard_map.103 = (bf16[2,256,1280]{2,1,0:T(8,128)(2,1)S(1)}, bf16[2,256,512]{2,1,0:T(8,128)(2,1)S(1)}) custom-call(s32[3]{0:T(128)S(1)} %pad_add_fusion.place._, bf16[256,512]{1,0:T(8,128)(2,1)S(1)} %collective-permute-done.r0, bf16[256,512]{1,0:T(8,128)(2,1)S(1)} %collective-permute-done.1.r1, bf16[256,512]{1,0:T(8,128)(2,1)S(1)} %collective-permute-done.2.r2, ...), custom_call_target="tpu_custom_call" | custom-call | flops 671088640 | bytes 4194304 | tf_op jit(solution)/shard_map/pallas_call | solution.py:72
  71.3 0.1 collective-permute-start.9
  71.4 6.3 %collective-permute-start.11 = (bf16[256,512]{1,0:T(8,128)(2,1)S(1)}, bf16[256,512]{1,0:T(8,128)(2,1)S(1)}, u32[]{:S(2)}, u32[]{:S(2)}) collective-permute-start(bf16[256,512]{1,0:T(8,128)(2,1)S(1)} %get-tuple-element.24), channel_id=1, source_target_pairs={{0,1},{1,2},{2,3},{3,0},{4,5},{5,6},{6,7},{7,4},{8,9},{9,10},{10,1... | collective-permute-start | bytes 786440 | tf_op jit(solution)/shard_map/ppermute | solution.py:54
  77.7 0.0 collective-permute-start.12
  77.7 1.6 %collective-permute-start.13 = (bf16[256,512]{1,0:T(8,128)(2,1)S(1)}, bf16[256,512]{1,0:T(8,128)(2,1)S(1)}, u32[]{:S(2)}, u32[]{:S(2)}) collective-permute-start(bf16[256,512]{1,0:T(8,128)(2,1)S(1)} %get-tuple-element.26), channel_id=1, source_target_pairs={{0,3},{1,0},{2,1},{3,2},{4,7},{5,4},{6,5},{7,6},{8,11},{9,8},{10,9... | collective-permute-start | bytes 786440 | tf_op jit(solution)/shard_map/ppermute | solution.py:54
  79.2 0.0 collective-permute-done.9.pair
  79.2 1.9 %shard_map.104 = bf16[256,1280]{1,0:T(8,128)(2,1)} custom-call(s32[3]{0:T(128)S(1)} %pad_add_fusion.place._, bf16[2,256,512]{2,1,0:T(8,128)(2,1)S(1)} %get-tuple-element.21.att, bf16[1280,512]{1,0:T(8,128)(2,1)S(1)} %get-tuple-element.20.wt, bf16[2,256,1280]{2,1,0:T(8,128)(2,1)S(1)} %collective-permute-done.9.pair), custom_call_target="tpu_custom_call" | custom-call | flops 335544320 | bytes 3145728 | tf_op jit(solution)/shard_map/pallas_call | solution.py:72
  81.2 0.0 collective-permute-start.10
  81.2 3.2 %collective-permute-done.11.a1 = bf16[256,512]{1,0:T(8,128)(2,1)S(1)} collective-permute-done((bf16[256,512]{1,0:T(8,128)(2,1)S(1)}, bf16[256,512]{1,0:T(8,128)(2,1)S(1)}, u32[]{:S(2)}, u32[]{:S(2)}) %collective-permute-start.11) | collective-permute-done | bytes 262176 | tf_op jit(solution)/shard_map/ppermute | solution.py:54
  84.4 5.1 %collective-permute-done.12.a2 = bf16[256,512]{1,0:T(8,128)(2,1)S(1)} collective-permute-done((bf16[256,512]{1,0:T(8,128)(2,1)S(1)}, bf16[256,512]{1,0:T(8,128)(2,1)S(1)}, u32[]{:S(2)}, u32[]{:S(2)}) %collective-permute-start.12) | collective-permute-done | bytes 262176 | tf_op jit(solution)/shard_map/ppermute | solution.py:54
  89.5 0.8 collective-permute-done.13.a3
  90.2 0.0 copy-start.2
  90.2 0.0 copy-start.3
  90.2 0.0 copy-start.4
  90.2 1.4 %shard_map.106 = bf16[256,512]{1,0:T(8,128)(2,1)} custom-call(s32[3]{0:T(128)S(1)} %pad_add_fusion.place._, bf16[256,512]{1,0:T(8,128)(2,1)S(1)} %get-tuple-element.23.a0, bf16[256,512]{1,0:T(8,128)(2,1)S(1)} %collective-permute-done.11.a1, bf16[256,512]{1,0:T(8,128)(2,1)S(1)} %collective-permute-done.12.a2, bf16[256,512]{1,0:T(8,128)(2,1)S(1)} %collective-permute-done.13.a3), custom_call_target="tpu_custom_call" | custom-call | bytes 1048576 | tf_op jit(solution)/shard_map/pallas_call | solution.py:72
  91.6 2.6 %collective-permute-start.14 = (bf16[256,512]{1,0:T(8,128)(2,1)}, bf16[256,512]{1,0:T(8,128)(2,1)}, u32[]{:S(2)}, u32[]{:S(2)}) collective-permute-start(bf16[256,512]{1,0:T(8,128)(2,1)} %shard_map.106), channel_id=1, source_target_pairs={{0,0},{1,4},{2,64},{3,68},{4,1},{5,5},{6,65},{7,69},{8,8},{9,12},{... | collective-permute-start | bytes 786440 | tf_op jit(solution)/shard_map/ppermute | solution.py:54
  94.2 4.9 %all-to-all-done.1.blocks = bf16[8,160,512]{2,1,0:T(8,128)(2,1)} async-done(((bf16[8,160,512]{2,1,0:T(8,128)(2,1)}), bf16[8,160,512]{2,1,0:T(8,128)(2,1)}, u32[]{:S(2)}, u32[]{:S(2)}) %all-to-all-start.1) | async-done | bytes 1310752 | tf_op jit(solution)/shard_map/all_to_all | solution.py:58
  99.1 0.0 copy-start
  99.1 1.6 %shard_map.109 = (bf16[80,512]{1,0:T(8,128)(2,1)S(1)}, bf16[80,512]{1,0:T(8,128)(2,1)S(1)}) custom-call(s32[3]{0:T(128)S(1)} %pad_add_fusion.place._, bf16[8,160,512]{2,1,0:T(8,128)(2,1)} %all-to-all-done.1.blocks), custom_call_target="tpu_custom_call" | custom-call | bytes 2097152 | tf_op jit(solution)/shard_map/pallas_call | solution.py:72
  100.7 8.4 %collective-permute-start.15 = (bf16[80,512]{1,0:T(8,128)(2,1)S(1)}, bf16[80,512]{1,0:T(8,128)(2,1)S(1)}, u32[]{:S(2)}, u32[]{:S(2)}) collective-permute-start(bf16[80,512]{1,0:T(8,128)(2,1)S(1)} %get-tuple-element.31), channel_id=1, source_target_pairs={{0,0},{1,64},{2,128},{3,192},{4,1},{5,65},{6,129},{7,193},{8,8},{9... | collective-permute-start | bytes 245768 | tf_op jit(solution)/shard_map/ppermute | solution.py:54
  109.1 1.9 %collective-permute-start.16 = (bf16[80,512]{1,0:T(8,128)(2,1)S(1)}, bf16[80,512]{1,0:T(8,128)(2,1)S(1)}, u32[]{:S(2)}, u32[]{:S(2)}) collective-permute-start(bf16[80,512]{1,0:T(8,128)(2,1)S(1)} %get-tuple-element.32), channel_id=1, source_target_pairs={{0,4},{1,68},{2,132},{3,196},{4,5},{5,69},{6,133},{7,197},{8,12},{... | collective-permute-start | bytes 245768 | tf_op jit(solution)/shard_map/ppermute | solution.py:54
  111.1 0.0 collective-permute-done.14.up_ref
  111.1 0.0 copy-done.2
  111.1 0.0 copy-done.3
  111.1 0.0 copy-done.4
  111.1 0.0 copy-done
  111.1 3.3 %shard_map.107 = (bf16[256,512]{1,0:T(8,128)(2,1)}, bf16[256,128]{1,0:T(8,128)(2,1)}, bf16[256,128]{1,0:T(8,128)(2,1)}) custom-call(s32[3]{0:T(128)S(1)} %pad_add_fusion.place._, bf16[256,512]{1,0:T(8,128)(2,1)} %collective-permute-done.14.up_ref, bf16[256,512]{1,0:T(8,128)(2,1)S(1)} %copy-done.2, bf16[256,128]{1,0:T(8,128)(2,1)S(1)} %copy-done.3, ...), custom_call_target="tpu_custom_call" | custom-call | flops 335544320 | bytes 3145728 | tf_op jit(solution)/shard_map/pallas_call | solution.py:72
  114.4 0.0 collective-permute-done.15
  114.4 5.0 %collective-permute-done.16 = bf16[80,512]{1,0:T(8,128)(2,1)S(1)} collective-permute-done((bf16[80,512]{1,0:T(8,128)(2,1)S(1)}, bf16[80,512]{1,0:T(8,128)(2,1)S(1)}, u32[]{:S(2)}, u32[]{:S(2)}) %collective-permute-start.16) | collective-permute-done | bytes 81952 | tf_op jit(solution)/shard_map/ppermute | solution.py:54
  119.4 0.7 add_bitcast_fusion
  120.1 0.0 collective-permute-done.10.across
  120.1 2.5 %shard_map.105 = bf16[256,1280]{1,0:T(8,128)(2,1)} custom-call(s32[3]{0:T(128)S(1)} %pad_add_fusion.place._, bf16[2,256,512]{2,1,0:T(8,128)(2,1)S(1)} %get-tuple-element.21.att, bf16[1280,512]{1,0:T(8,128)(2,1)S(1)} %get-tuple-element.20.wt, bf16[2,256,1280]{2,1,0:T(8,128)(2,1)S(1)} %collective-permute-done.9.pair, ...), custom_call_target="tpu_custom_call" | custom-call | flops 335544320 | bytes 4194304 | tf_op jit(solution)/shard_map/pallas_call | solution.py:72
Async XLA Ops:
  0.6 20.7 %copy-start.1 = (bf16[256,1280]{1,0:T(8,128)(2,1)S(1)}, bf16[256,1280]{1,0:T(8,128)(2,1)}, u32[]{:S(2)}) copy-start(bf16[256,1280]{1,0:T(8,128)(2,1)} %o0.3) | copy-start | bytes 1966084
  0.6 11.3 %collective-permute-start.7 = (bf16[80,512]{1,0:T(8,128)(2,1)}, bf16[80,512]{1,0:T(8,128)(2,1)S(1)}, u32[]{:S(2)}, u32[]{:S(2)}) collective-permute-start(bf16[80,512]{1,0:T(8,128)(2,1)} %bitcast.8), channel_id=1, source_target_pairs={{0,0},{1,4},{2,64},{3,68},{4,192},{5,196},{6,128},{7,132},{8,8},{9... | collective-permute-start | bytes 245768 | tf_op jit(solution)/shard_map/ppermute | solution.py:54
  4.0 17.5 %collective-permute-start.5 = (bf16[256,1280]{1,0:T(8,128)(2,1)}, bf16[256,1280]{1,0:T(8,128)(2,1)}, u32[]{:S(2)}, u32[]{:S(2)}) collective-permute-start(bf16[256,1280]{1,0:T(8,128)(2,1)} %o0.3), channel_id=1, source_target_pairs={{0,64},{1,65},{2,66},{3,67},{4,68},{5,69},{6,70},{7,71},{8,72},{9,... | collective-permute-start | bytes 1966088 | tf_op jit(solution)/shard_map/ppermute | solution.py:54
  12.9 34.1 %all-to-all-start = ((bf16[8,80,512]{2,1,0:T(8,128)(2,1)}), bf16[8,80,512]{2,1,0:T(8,128)(2,1)}, u32[]{:S(2)}, u32[]{:S(2)}) async-start(bf16[8,80,512]{2,1,0:T(8,128)(2,1)} %broadcast_in_dim.2), calls=%async_computation | async-start | bytes 1310720 | tf_op jit(solution)/shard_map/all_to_all | solution.py:58
  21.3 30.8 %collective-permute-start.4 = (bf16[256,1280]{1,0:T(8,128)(2,1)S(1)}, bf16[256,1280]{1,0:T(8,128)(2,1)}, u32[]{:S(2)}, u32[]{:S(2)}) collective-permute-start(bf16[256,1280]{1,0:T(8,128)(2,1)S(1)} %copy-done.1), channel_id=1, source_target_pairs={{0,4},{1,5},{2,6},{3,7},{4,0},{5,1},{6,2},{7,3},{8,12},{9,13},{10,... | collective-permute-start | bytes 1966088 | tf_op jit(solution)/shard_map/ppermute | solution.py:54
  21.5 30.7 %collective-permute-start.6 = (bf16[256,1280]{1,0:T(8,128)(2,1)}, bf16[256,1280]{1,0:T(8,128)(2,1)}, u32[]{:S(2)}, u32[]{:S(2)}) collective-permute-start(bf16[256,1280]{1,0:T(8,128)(2,1)} %collective-permute-done.5.o2), channel_id=1, source_target_pairs={{0,4},{1,5},{2,6},{3,7},{4,0},{5,1},{6,2},{7,3},{8,12},{9,13},{10,... | collective-permute-start | bytes 1966088 | tf_op jit(solution)/shard_map/ppermute | solution.py:54
  25.0 12.8 %collective-permute-start = (bf16[256,512]{1,0:T(8,128)(2,1)}, bf16[256,512]{1,0:T(8,128)(2,1)S(1)}, u32[]{:S(2)}, u32[]{:S(2)}) collective-permute-start(bf16[256,512]{1,0:T(8,128)(2,1)} %get-tuple-element.19), channel_id=1, source_target_pairs={{0,0},{1,4},{2,64},{3,68},{4,1},{5,5},{6,65},{7,69},{8,8},{9,12},{... | collective-permute-start | bytes 786440 | tf_op jit(solution)/shard_map/ppermute | solution.py:54
  37.8 9.2 %collective-permute-start.3 = (bf16[256,512]{1,0:T(8,128)(2,1)S(1)}, bf16[256,512]{1,0:T(8,128)(2,1)S(1)}, u32[]{:S(2)}, u32[]{:S(2)}) collective-permute-start(bf16[256,512]{1,0:T(8,128)(2,1)S(1)} %collective-permute-done.r0), channel_id=1, source_target_pairs={{0,3},{1,0},{2,1},{3,2},{4,7},{5,4},{6,5},{7,6},{8,11},{9,8},{10,9... | collective-permute-start | bytes 786440 | tf_op jit(solution)/shard_map/ppermute | solution.py:54
  37.8 11.7 %collective-permute-start.2 = (bf16[256,512]{1,0:T(8,128)(2,1)S(1)}, bf16[256,512]{1,0:T(8,128)(2,1)S(1)}, u32[]{:S(2)}, u32[]{:S(2)}) collective-permute-start(bf16[256,512]{1,0:T(8,128)(2,1)S(1)} %collective-permute-done.r0), channel_id=1, source_target_pairs={{0,2},{1,3},{2,0},{3,1},{4,6},{5,7},{6,4},{7,5},{8,10},{9,11},{10,... | collective-permute-start | bytes 786440 | tf_op jit(solution)/shard_map/ppermute | solution.py:54
  40.3 11.9 %collective-permute-start.1 = (bf16[256,512]{1,0:T(8,128)(2,1)S(1)}, bf16[256,512]{1,0:T(8,128)(2,1)S(1)}, u32[]{:S(2)}, u32[]{:S(2)}) collective-permute-start(bf16[256,512]{1,0:T(8,128)(2,1)S(1)} %collective-permute-done.r0), channel_id=1, source_target_pairs={{0,1},{1,2},{2,3},{3,0},{4,5},{5,6},{6,7},{7,4},{8,9},{9,10},{10,1... | collective-permute-start | bytes 786440 | tf_op jit(solution)/shard_map/ppermute | solution.py:54
  47.0 17.5 %collective-permute-start.8 = (bf16[8,80,512]{2,1,0:T(8,128)(2,1)}, bf16[8,80,512]{2,1,0:T(8,128)(2,1)S(1)}, u32[]{:S(2)}, u32[]{:S(2)}) collective-permute-start(bf16[8,80,512]{2,1,0:T(8,128)(2,1)} %all-to-all-done.w0), channel_id=1, source_target_pairs={{0,192},{1,193},{2,194},{3,195},{4,196},{5,197},{6,198},{7,199},{8... | collective-permute-start | bytes 1966088 | tf_op jit(solution)/shard_map/ppermute | solution.py:54
  56.4 42.8 %all-to-all-start.1 = ((bf16[8,160,512]{2,1,0:T(8,128)(2,1)}), bf16[8,160,512]{2,1,0:T(8,128)(2,1)}, u32[]{:S(2)}, u32[]{:S(2)}) async-start(bf16[8,160,512]{2,1,0:T(8,128)(2,1)} %bitcast.5), calls=%async_computation.1 | async-start | bytes 2621440 | tf_op jit(solution)/shard_map/all_to_all | solution.py:58
  64.5 0.8 copy-start.5
  65.4 1.1 copy-start.6
  71.3 7.9 %collective-permute-start.9 = (bf16[2,256,1280]{2,1,0:T(8,128)(2,1)S(1)}, bf16[2,256,1280]{2,1,0:T(8,128)(2,1)S(1)}, u32[]{:S(2)}, u32[]{:S(2)}) collective-permute-start(bf16[2,256,1280]{2,1,0:T(8,128)(2,1)S(1)} %get-tuple-element.22), channel_id=1, source_target_pairs={{0,4},{1,5},{2,6},{3,7},{4,0},{5,1},{6,2},{7,3},{8,12},{9,13},{10,... | collective-permute-start | bytes 3932168 | tf_op jit(solution)/shard_map/ppermute | solution.py:54
  71.4 13.0 %collective-permute-start.11 = (bf16[256,512]{1,0:T(8,128)(2,1)S(1)}, bf16[256,512]{1,0:T(8,128)(2,1)S(1)}, u32[]{:S(2)}, u32[]{:S(2)}) collective-permute-start(bf16[256,512]{1,0:T(8,128)(2,1)S(1)} %get-tuple-element.24), channel_id=1, source_target_pairs={{0,1},{1,2},{2,3},{3,0},{4,5},{5,6},{6,7},{7,4},{8,9},{9,10},{10,1... | collective-permute-start | bytes 786440 | tf_op jit(solution)/shard_map/ppermute | solution.py:54
  77.7 11.8 %collective-permute-start.12 = (bf16[256,512]{1,0:T(8,128)(2,1)S(1)}, bf16[256,512]{1,0:T(8,128)(2,1)S(1)}, u32[]{:S(2)}, u32[]{:S(2)}) collective-permute-start(bf16[256,512]{1,0:T(8,128)(2,1)S(1)} %get-tuple-element.25), channel_id=1, source_target_pairs={{0,2},{1,3},{2,0},{3,1},{4,6},{5,7},{6,4},{7,5},{8,10},{9,11},{10,... | collective-permute-start | bytes 786440 | tf_op jit(solution)/shard_map/ppermute | solution.py:54
  77.7 12.5 %collective-permute-start.13 = (bf16[256,512]{1,0:T(8,128)(2,1)S(1)}, bf16[256,512]{1,0:T(8,128)(2,1)S(1)}, u32[]{:S(2)}, u32[]{:S(2)}) collective-permute-start(bf16[256,512]{1,0:T(8,128)(2,1)S(1)} %get-tuple-element.26), channel_id=1, source_target_pairs={{0,3},{1,0},{2,1},{3,2},{4,7},{5,4},{6,5},{7,6},{8,11},{9,8},{10,9... | collective-permute-start | bytes 786440 | tf_op jit(solution)/shard_map/ppermute | solution.py:54
  81.2 38.9 %collective-permute-start.10 = (bf16[256,1280]{1,0:T(8,128)(2,1)}, bf16[256,1280]{1,0:T(8,128)(2,1)}, u32[]{:S(2)}, u32[]{:S(2)}) collective-permute-start(bf16[256,1280]{1,0:T(8,128)(2,1)} %shard_map.104), channel_id=1, source_target_pairs={{0,64},{1,65},{2,66},{3,67},{4,68},{5,69},{6,70},{7,71},{8,72},{9,... | collective-permute-start | bytes 1966088 | tf_op jit(solution)/shard_map/ppermute | solution.py:54
  90.2 20.8 %copy-start.2 = (bf16[256,512]{1,0:T(8,128)(2,1)S(1)}, bf16[256,512]{1,0:T(8,128)(2,1)}, u32[]{:S(2)}) copy-start(bf16[256,512]{1,0:T(8,128)(2,1)} %q_ref.3) | copy-start | bytes 786436
  90.2 20.8 %copy-start.3 = (bf16[256,128]{1,0:T(8,128)(2,1)S(1)}, bf16[256,128]{1,0:T(8,128)(2,1)}, u32[]{:S(2)}) copy-start(bf16[256,128]{1,0:T(8,128)(2,1)} %k_ref.3) | copy-start | bytes 196612
  90.2 20.8 %copy-start.4 = (bf16[256,128]{1,0:T(8,128)(2,1)S(1)}, bf16[256,128]{1,0:T(8,128)(2,1)}, u32[]{:S(2)}) copy-start(bf16[256,128]{1,0:T(8,128)(2,1)} %v_ref.3) | copy-start | bytes 196612
  91.6 19.4 %collective-permute-start.14 = (bf16[256,512]{1,0:T(8,128)(2,1)}, bf16[256,512]{1,0:T(8,128)(2,1)}, u32[]{:S(2)}, u32[]{:S(2)}) collective-permute-start(bf16[256,512]{1,0:T(8,128)(2,1)} %shard_map.106), channel_id=1, source_target_pairs={{0,0},{1,4},{2,64},{3,68},{4,1},{5,5},{6,65},{7,69},{8,8},{9,12},{... | collective-permute-start | bytes 786440 | tf_op jit(solution)/shard_map/ppermute | solution.py:54
  99.1 11.9 %copy-start = (f32[4,256,256]{2,1,0:T(8,128)S(1)}, f32[4,256,256]{2,1,0:T(8,128)}, u32[]{:S(2)}) copy-start(f32[4,256,256]{2,1,0:T(8,128)} %get-tuple-element.27.prob_ref) | copy-start | bytes 3145732
  100.7 13.6 %collective-permute-start.15 = (bf16[80,512]{1,0:T(8,128)(2,1)S(1)}, bf16[80,512]{1,0:T(8,128)(2,1)S(1)}, u32[]{:S(2)}, u32[]{:S(2)}) collective-permute-start(bf16[80,512]{1,0:T(8,128)(2,1)S(1)} %get-tuple-element.31), channel_id=1, source_target_pairs={{0,0},{1,64},{2,128},{3,192},{4,1},{5,65},{6,129},{7,193},{8,8},{9... | collective-permute-start | bytes 245768 | tf_op jit(solution)/shard_map/ppermute | solution.py:54
  109.1 10.2 %collective-permute-start.16 = (bf16[80,512]{1,0:T(8,128)(2,1)S(1)}, bf16[80,512]{1,0:T(8,128)(2,1)S(1)}, u32[]{:S(2)}, u32[]{:S(2)}) collective-permute-start(bf16[80,512]{1,0:T(8,128)(2,1)S(1)} %get-tuple-element.32), channel_id=1, source_target_pairs={{0,4},{1,68},{2,132},{3,196},{4,5},{5,69},{6,133},{7,197},{8,12},{... | collective-permute-start | bytes 245768 | tf_op jit(solution)/shard_map/ppermute | solution.py:54

commit v4 on v3

--- a/solution.py
+++ b/solution.py
@@ -158,10 +158,8 @@
     out[...] = (dot(att[1], wt[...], ((1,), (1,))) + pair[1].astype(F32)).astype(BF)
 
 
-def layer_sum_body(_, att, wt, pair, across, out):
-    out[...] = (
-        dot(att[0], wt[...], ((1,), (1,))) + pair[0].astype(F32) + across[...].astype(F32)
-    ).astype(BF)
+def layer_own_body(_, att, wt, pair, out):
+    out[...] = (dot(att[0], wt[...], ((1,), (1,))) + pair[0].astype(F32)).astype(BF)
 
 
 def attn_grad_body(place, o0, o1, o2, o3, w0, w1, g0, g1, g2, g3, wt_ref, og):
@@ -238,9 +236,10 @@
         layer_across_body, shape(TOK, COLS), flops=big // 4, moved=3 << 20
     )(place, attended_two, wt_all, pair)
     across = send(across, ACROSS)
-    layer_out = call(
-        layer_sum_body, shape(TOK, COLS), flops=big // 4, moved=4 << 20
-    )(place, attended_two, wt_all, pair, across)
+    own = call(layer_own_body, shape(TOK, COLS), flops=big // 4, moved=4 << 20)(
+        place, attended_two, wt_all, pair
+    )
+    layer_out = (own.astype(F32) + across.astype(F32)).astype(BF)
 
     partials = [partials[0]] + [send(p, pairs) for p, pairs in zip(partials[1:], ALONG_Y)]
     upstream = call(sum_four_body, shape(TOK, GROUP), moved=1 << 20)(place, *partials)

time: 123 us -> 122 us (level)
  the two profiles are of different devices: /device:TPU:16 before, /device:TPU:4 now
where the time goes in v4:
time: 122 us
  starting transfers between devices  47.7 us (39%)
  waiting for transfers between devices  47.3 us (39%)
  Pallas kernels  20.8 us (17%)
  other arithmetic  2.84 us (2%)
  local copies, waits for them, and re-layouts  2.16 us (2%)
    ppermute x17, waiting for transfers between devices, send(): return lax.ppermute(value, AXES, pairs)  39 us
    ppermute x17, starting transfers between devices, send(): return lax.ppermute(value, AXES, pairs)  30.8 us
    pallas_call x9, Pallas kernels, run(): pl.pallas_call(body, out_shape=outs, grid=(1,), in_specs=[pl.BlockSpec(me...  20.8 us
    all_to_all x2, starting transfers between devices, exchange(): lax.all_to_all(blocks, 'dp', 0, 0, axis_index_groups=groups, tiled=True)  16.9 us
    all_to_all x2, waiting for transfers between devices, exchange(): lax.all_to_all(blocks, 'dp', 0, 0, axis_index_groups=groups, tiled=True)  8.28 us
  transfers between devices with their start and end apart: 19, of which 9 were waited for; matrix products, arithmetic and copies ran while one was open for 1% of the time, Pallas kernels for 17%

profile of v4, /device:TPU:4, one launch (start us, length us, event | category | flops | bytes accessed | tf_op | source)
XLA Modules:
  0.0 121.7 jit_solution(11638941242377784543)
XLA Ops:
  0.6 0.0 copy-start.3
  0.6 5.2 %collective-permute-start.7 = (bf16[80,512]{1,0:T(8,128)(2,1)}, bf16[80,512]{1,0:T(8,128)(2,1)S(1)}, u32[]{:S(2)}, u32[]{:S(2)}) collective-permute-start(bf16[80,512]{1,0:T(8,128)(2,1)} %bitcast.8), channel_id=1, source_target_pairs={{0,0},{1,4},{2,64},{3,68},{4,192},{5,196},{6,128},{7,132},{8,8},{9... | collective-permute-start | bytes 245768 | tf_op jit(solution)/shard_map/ppermute | solution.py:54
  5.8 1.1 collective-permute-start.5
  6.9 4.6 %collective-permute-done.7 = bf16[80,512]{1,0:T(8,128)(2,1)S(1)} collective-permute-done((bf16[80,512]{1,0:T(8,128)(2,1)}, bf16[80,512]{1,0:T(8,128)(2,1)S(1)}, u32[]{:S(2)}, u32[]{:S(2)}) %collective-permute-start.7) | collective-permute-done | bytes 81952 | tf_op jit(solution)/shard_map/ppermute | solution.py:54
  11.5 0.9 broadcast_in_dim.2
  12.4 8.5 %all-to-all-start = ((bf16[8,80,512]{2,1,0:T(8,128)(2,1)}), bf16[8,80,512]{2,1,0:T(8,128)(2,1)}, u32[]{:S(2)}, u32[]{:S(2)}) async-start(bf16[8,80,512]{2,1,0:T(8,128)(2,1)} %broadcast_in_dim.2), calls=%async_computation | async-start | bytes 1310720 | tf_op jit(solution)/shard_map/all_to_all | solution.py:58
  20.9 0.0 copy-done.3
  20.9 0.1 collective-permute-start.4
  21.0 2.7 %collective-permute-done.5.o2 = bf16[256,1280]{1,0:T(8,128)(2,1)} collective-permute-done((bf16[256,1280]{1,0:T(8,128)(2,1)}, bf16[256,1280]{1,0:T(8,128)(2,1)}, u32[]{:S(2)}, u32[]{:S(2)}) %collective-permute-start.5) | collective-permute-done | bytes 655392 | tf_op jit(solution)/shard_map/ppermute | solution.py:54
  23.7 0.0 collective-permute-start.6
  23.7 3.1 %shard_map.101 = (bf16[256,512]{1,0:T(8,128)(2,1)}, f32[4,256,256]{2,1,0:T(8,128)}) custom-call(s32[8]{0:T(128)} %bitcast.9, bf16[256,512]{1,0:T(8,128)(2,1)} %q_ref.3, bf16[256,128]{1,0:T(8,128)(2,1)} %k_ref.3, bf16[256,128]{1,0:T(8,128)(2,1)} %v_ref.3), custom_call_target="tpu_custom_call" | custom-call | flops 134217728 | bytes 2097152 | tf_op jit(solution)/shard_map/pallas_call | solution.py:72
  26.7 3.4 %collective-permute-start = (bf16[256,512]{1,0:T(8,128)(2,1)}, bf16[256,512]{1,0:T(8,128)(2,1)S(1)}, u32[]{:S(2)}, u32[]{:S(2)}) collective-permute-start(bf16[256,512]{1,0:T(8,128)(2,1)} %get-tuple-element.19), channel_id=1, source_target_pairs={{0,0},{1,4},{2,64},{3,68},{4,1},{5,5},{6,65},{7,69},{8,8},{9,12},{... | collective-permute-start | bytes 786440 | tf_op jit(solution)/shard_map/ppermute | solution.py:54
  30.2 9.4 %collective-permute-done.r0 = bf16[256,512]{1,0:T(8,128)(2,1)S(1)} collective-permute-done((bf16[256,512]{1,0:T(8,128)(2,1)}, bf16[256,512]{1,0:T(8,128)(2,1)S(1)}, u32[]{:S(2)}, u32[]{:S(2)}) %collective-permute-start) | collective-permute-done | bytes 262176 | tf_op jit(solution)/shard_map/ppermute | solution.py:54
  39.6 0.0 collective-permute-start.3
  39.6 0.0 collective-permute-start.2
  39.6 2.0 %collective-permute-start.1 = (bf16[256,512]{1,0:T(8,128)(2,1)S(1)}, bf16[256,512]{1,0:T(8,128)(2,1)S(1)}, u32[]{:S(2)}, u32[]{:S(2)}) collective-permute-start(bf16[256,512]{1,0:T(8,128)(2,1)S(1)} %collective-permute-done.r0), channel_id=1, source_target_pairs={{0,1},{1,2},{2,3},{3,0},{4,5},{5,6},{6,7},{7,4},{8,9},{9,10},{10,1... | collective-permute-start | bytes 786440 | tf_op jit(solution)/shard_map/ppermute | solution.py:54
  41.6 7.1 %collective-permute-done.3.r3 = bf16[256,512]{1,0:T(8,128)(2,1)S(1)} collective-permute-done((bf16[256,512]{1,0:T(8,128)(2,1)S(1)}, bf16[256,512]{1,0:T(8,128)(2,1)S(1)}, u32[]{:S(2)}, u32[]{:S(2)}) %collective-permute-start.3) | collective-permute-done | bytes 262176 | tf_op jit(solution)/shard_map/ppermute | solution.py:54
  48.8 0.0 all-to-all-done.w0
  48.8 0.0 collective-permute-start.8
  48.8 0.1 pad_add_fusion.place._
  48.8 1.5 %collective-permute-done.2.r2 = bf16[256,512]{1,0:T(8,128)(2,1)S(1)} collective-permute-done((bf16[256,512]{1,0:T(8,128)(2,1)S(1)}, bf16[256,512]{1,0:T(8,128)(2,1)S(1)}, u32[]{:S(2)}, u32[]{:S(2)}) %collective-permute-start.2) | collective-permute-done | bytes 262176 | tf_op jit(solution)/shard_map/ppermute | solution.py:54
  50.3 5.2 %collective-permute-done.1.r1 = bf16[256,512]{1,0:T(8,128)(2,1)S(1)} collective-permute-done((bf16[256,512]{1,0:T(8,128)(2,1)S(1)}, bf16[256,512]{1,0:T(8,128)(2,1)S(1)}, u32[]{:S(2)}, u32[]{:S(2)}) %collective-permute-start.1) | collective-permute-done | bytes 262176 | tf_op jit(solution)/shard_map/ppermute | solution.py:54
  55.5 0.0 collective-permute-done.4.o1
  55.5 0.0 collective-permute-done.6.o3
  55.5 4.3 %shard_map.108 = bf16[1280,512]{1,0:T(8,128)(2,1)} custom-call(s32[3]{0:T(128)S(1)} %pad_add_fusion.place._, bf16[256,1280]{1,0:T(8,128)(2,1)S(1)} %copy-done.3, bf16[256,1280]{1,0:T(8,128)(2,1)} %collective-permute-done.4.o1, bf16[256,1280]{1,0:T(8,128)(2,1)} %collective-permute-done.5.o2, bf16[256,1280]{1,0:T(8,128)(2,1)} %collective-permute-done.6.o3, ...), custom_call_target="tpu_custom_call" | custom-call | flops 1342177280 | bytes 6291456 | tf_op jit(solution)/shard_map/pallas_call | solution.py:72
  59.8 0.0 copy-done.5
  59.8 0.0 copy-done.7
  59.8 0.0 copy-done.9
  59.8 8.5 %all-to-all-start.1 = ((bf16[8,160,512]{2,1,0:T(8,128)(2,1)}), bf16[8,160,512]{2,1,0:T(8,128)(2,1)S(1)}, u32[]{:S(2)}, u32[]{:S(2)}) async-start(bf16[8,160,512]{2,1,0:T(8,128)(2,1)} %bitcast.5), calls=%async_computation.1 | async-start | bytes 2621440 | tf_op jit(solution)/shard_map/all_to_all | solution.py:58
  68.3 0.0 copy-start.8
  68.3 0.0 copy-start.10
  68.3 0.0 collective-permute-done.8.w1
  68.3 3.7 %shard_map.102 = (bf16[256,512]{1,0:T(8,128)(2,1)S(1)}, bf16[256,512]{1,0:T(8,128)(2,1)S(1)}, bf16[256,512]{1,0:T(8,128)(2,1)S(1)}, bf16[256,512]{1,0:T(8,128)(2,1)S(1)}, bf16[1280,512]{1,0:T(8,128)(2,1)S(1)}) custom-call(s32[3]{0:T(128)S(1)} %pad_add_fusion.place._, bf16[256,1280]{1,0:T(8,128)(2,1)S(1)} %copy-done.3, ...), custom_call_target="tpu_custom_call" | custom-call | flops 1342177280 | bytes 6291456 | tf_op jit(solution)/shard_map/pallas_call | solution.py:72
  72.0 0.0 copy-done.6
  72.0 0.0 copy-done.8
  72.0 0.0 copy-done.10
  72.0 1.4 %shard_map.103 = (bf16[2,256,1280]{2,1,0:T(8,128)(2,1)S(1)}, bf16[2,256,512]{2,1,0:T(8,128)(2,1)S(1)}) custom-call(s32[3]{0:T(128)S(1)} %pad_add_fusion.place._, bf16[256,512]{1,0:T(8,128)(2,1)S(1)} %collective-permute-done.r0, bf16[256,512]{1,0:T(8,128)(2,1)S(1)} %copy-done.10, bf16[256,512]{1,0:T(8,128)(2,1)S(1)} %copy-done.8, ...), custom_call_target="tpu_custom_call" | custom-call | flops 671088640 | bytes 4194304 | tf_op jit(solution)/shard_map/pallas_call | solution.py:72
  73.5 0.1 collective-permute-start.9
  73.6 0.1 collective-permute-start.11
  73.7 2.7 %collective-permute-start.12 = (bf16[256,512]{1,0:T(8,128)(2,1)S(1)}, bf16[256,512]{1,0:T(8,128)(2,1)S(1)}, u32[]{:S(2)}, u32[]{:S(2)}) collective-permute-start(bf16[256,512]{1,0:T(8,128)(2,1)S(1)} %get-tuple-element.25), channel_id=1, source_target_pairs={{0,2},{1,3},{2,0},{3,1},{4,6},{5,7},{6,4},{7,5},{8,10},{9,11},{10,... | collective-permute-start | bytes 786440 | tf_op jit(solution)/shard_map/ppermute | solution.py:54
  76.4 0.5 collective-permute-start.13
  76.9 0.0 collective-permute-done.9.pair
  76.9 1.9 %shard_map.105 = bf16[256,1280]{1,0:T(8,128)(2,1)} custom-call(s32[3]{0:T(128)S(1)} %pad_add_fusion.place._, bf16[2,256,512]{2,1,0:T(8,128)(2,1)S(1)} %get-tuple-element.21.att, bf16[1280,512]{1,0:T(8,128)(2,1)S(1)} %get-tuple-element.20.wt, bf16[2,256,1280]{2,1,0:T(8,128)(2,1)S(1)} %collective-permute-done.9.pair), custom_call_target="tpu_custom_call" | custom-call | flops 335544320 | bytes 3145728 | tf_op jit(solution)/shard_map/pallas_call | solution.py:72
  78.8 0.0 copy-done
  78.8 2.4 %collective-permute-start.10 = (bf16[256,1280]{1,0:T(8,128)(2,1)}, bf16[256,1280]{1,0:T(8,128)(2,1)}, u32[]{:S(2)}, u32[]{:S(2)}) collective-permute-start(bf16[256,1280]{1,0:T(8,128)(2,1)} %shard_map.105), channel_id=1, source_target_pairs={{0,64},{1,65},{2,66},{3,67},{4,68},{5,69},{6,70},{7,71},{8,72},{9,... | collective-permute-start | bytes 1966088 | tf_op jit(solution)/shard_map/ppermute | solution.py:54
  81.2 7.9 %collective-permute-done.11.a1 = bf16[256,512]{1,0:T(8,128)(2,1)S(1)} collective-permute-done((bf16[256,512]{1,0:T(8,128)(2,1)S(1)}, bf16[256,512]{1,0:T(8,128)(2,1)S(1)}, u32[]{:S(2)}, u32[]{:S(2)}) %collective-permute-start.11) | collective-permute-done | bytes 262176 | tf_op jit(solution)/shard_map/ppermute | solution.py:54
  89.1 0.0 collective-permute-done.12.a2
  89.1 0.6 collective-permute-done.13.a3
  89.7 1.4 %shard_map.106 = bf16[256,512]{1,0:T(8,128)(2,1)} custom-call(s32[3]{0:T(128)S(1)} %pad_add_fusion.place._, bf16[256,512]{1,0:T(8,128)(2,1)S(1)} %get-tuple-element.23.a0, bf16[256,512]{1,0:T(8,128)(2,1)S(1)} %collective-permute-done.11.a1, bf16[256,512]{1,0:T(8,128)(2,1)S(1)} %collective-permute-done.12.a2, bf16[256,512]{1,0:T(8,128)(2,1)S(1)} %collective-permute-done.13.a3), custom_call_target="tpu_custom_call" | custom-call | bytes 1048576 | tf_op jit(solution)/shard_map/pallas_call | solution.py:72
  91.1 3.4 %collective-permute-start.14 = (bf16[256,512]{1,0:T(8,128)(2,1)}, bf16[256,512]{1,0:T(8,128)(2,1)}, u32[]{:S(2)}, u32[]{:S(2)}) collective-permute-start(bf16[256,512]{1,0:T(8,128)(2,1)} %shard_map.106), channel_id=1, source_target_pairs={{0,0},{1,4},{2,64},{3,68},{4,1},{5,5},{6,65},{7,69},{8,8},{9,12},{... | collective-permute-start | bytes 786440 | tf_op jit(solution)/shard_map/ppermute | solution.py:54
  94.6 8.3 %all-to-all-done.1.blocks = bf16[8,160,512]{2,1,0:T(8,128)(2,1)S(1)} async-done(((bf16[8,160,512]{2,1,0:T(8,128)(2,1)}), bf16[8,160,512]{2,1,0:T(8,128)(2,1)S(1)}, u32[]{:S(2)}, u32[]{:S(2)}) %all-to-all-start.1) | async-done | bytes 1310752 | tf_op jit(solution)/shard_map/all_to_all | solution.py:58
  102.8 0.7 shard_map.109
  103.6 1.9 %collective-permute-start.15 = (bf16[80,512]{1,0:T(8,128)(2,1)S(1)}, bf16[80,512]{1,0:T(8,128)(2,1)S(1)}, u32[]{:S(2)}, u32[]{:S(2)}) collective-permute-start(bf16[80,512]{1,0:T(8,128)(2,1)S(1)} %get-tuple-element.31), channel_id=1, source_target_pairs={{0,0},{1,64},{2,128},{3,192},{4,1},{5,65},{6,129},{7,193},{8,8},{9... | collective-permute-start | bytes 245768 | tf_op jit(solution)/shard_map/ppermute | solution.py:54
  105.5 7.8 %collective-permute-start.16 = (bf16[80,512]{1,0:T(8,128)(2,1)S(1)}, bf16[80,512]{1,0:T(8,128)(2,1)S(1)}, u32[]{:S(2)}, u32[]{:S(2)}) collective-permute-start(bf16[80,512]{1,0:T(8,128)(2,1)S(1)} %get-tuple-element.32), channel_id=1, source_target_pairs={{0,4},{1,68},{2,132},{3,196},{4,5},{5,69},{6,133},{7,197},{8,12},{... | collective-permute-start | bytes 245768 | tf_op jit(solution)/shard_map/ppermute | solution.py:54
  113.3 0.0 collective-permute-done.14.up_ref
  113.3 0.0 copy-done.4
  113.4 1.2 copy-done.2
  114.6 3.2 %shard_map.107 = (bf16[256,512]{1,0:T(8,128)(2,1)}, bf16[256,128]{1,0:T(8,128)(2,1)}, bf16[256,128]{1,0:T(8,128)(2,1)}) custom-call(s32[3]{0:T(128)S(1)} %pad_add_fusion.place._, bf16[256,512]{1,0:T(8,128)(2,1)} %collective-permute-done.14.up_ref, bf16[256,512]{1,0:T(8,128)(2,1)S(1)} %copy-done.4, bf16[256,128]{1,0:T(8,128)(2,1)S(1)} %copy-done.11, ...), custom_call_target="tpu_custom_call" | custom-call | flops 335544320 | bytes 3145728 | tf_op jit(solution)/shard_map/pallas_call | solution.py:72
  117.8 1.1 shard_map.104
  118.9 0.0 collective-permute-done.15
  118.9 0.0 collective-permute-done.16
  118.9 0.7 add_bitcast_fusion
  119.6 0.0 collective-permute-done.10
  119.6 2.1 %add_convert_fusion = bf16[256,1280]{1,0:T(8,128)(2,1)} fusion(bf16[256,1280]{1,0:T(8,128)(2,1)} %collective-permute-done.10, bf16[256,1280]{1,0:T(8,128)(2,1)S(1)} %shard_map.104), kind=kLoop, calls=%fused_computation | loop fusion | flops 1310720 | bytes 1966080 | tf_op jit(solution)/shard_map/convert_element_type | solution.py:242
  (13 shorter events, 0.0 us)
Async XLA Ops:
  0.6 20.3 %copy-start.3 = (bf16[256,1280]{1,0:T(8,128)(2,1)S(1)}, bf16[256,1280]{1,0:T(8,128)(2,1)}, u32[]{:S(2)}) copy-start(bf16[256,1280]{1,0:T(8,128)(2,1)} %o0.3) | copy-start | bytes 1966084
  0.6 10.9 %collective-permute-start.7 = (bf16[80,512]{1,0:T(8,128)(2,1)}, bf16[80,512]{1,0:T(8,128)(2,1)S(1)}, u32[]{:S(2)}, u32[]{:S(2)}) collective-permute-start(bf16[80,512]{1,0:T(8,128)(2,1)} %bitcast.8), channel_id=1, source_target_pairs={{0,0},{1,4},{2,64},{3,68},{4,192},{5,196},{6,128},{7,132},{8,8},{9... | collective-permute-start | bytes 245768 | tf_op jit(solution)/shard_map/ppermute | solution.py:54
  5.8 17.8 %collective-permute-start.5 = (bf16[256,1280]{1,0:T(8,128)(2,1)}, bf16[256,1280]{1,0:T(8,128)(2,1)}, u32[]{:S(2)}, u32[]{:S(2)}) collective-permute-start(bf16[256,1280]{1,0:T(8,128)(2,1)} %o0.3), channel_id=1, source_target_pairs={{0,64},{1,65},{2,66},{3,67},{4,68},{5,69},{6,70},{7,71},{8,72},{9,... | collective-permute-start | bytes 1966088 | tf_op jit(solution)/shard_map/ppermute | solution.py:54
  12.4 36.3 %all-to-all-start = ((bf16[8,80,512]{2,1,0:T(8,128)(2,1)}), bf16[8,80,512]{2,1,0:T(8,128)(2,1)}, u32[]{:S(2)}, u32[]{:S(2)}) async-start(bf16[8,80,512]{2,1,0:T(8,128)(2,1)} %broadcast_in_dim.2), calls=%async_computation | async-start | bytes 1310720 | tf_op jit(solution)/shard_map/all_to_all | solution.py:58
  20.9 34.6 %collective-permute-start.4 = (bf16[256,1280]{1,0:T(8,128)(2,1)S(1)}, bf16[256,1280]{1,0:T(8,128)(2,1)}, u32[]{:S(2)}, u32[]{:S(2)}) collective-permute-start(bf16[256,1280]{1,0:T(8,128)(2,1)S(1)} %copy-done.3), channel_id=1, source_target_pairs={{0,4},{1,5},{2,6},{3,7},{4,0},{5,1},{6,2},{7,3},{8,12},{9,13},{10,... | collective-permute-start | bytes 1966088 | tf_op jit(solution)/shard_map/ppermute | solution.py:54
  23.7 31.8 %collective-permute-start.6 = (bf16[256,1280]{1,0:T(8,128)(2,1)}, bf16[256,1280]{1,0:T(8,128)(2,1)}, u32[]{:S(2)}, u32[]{:S(2)}) collective-permute-start(bf16[256,1280]{1,0:T(8,128)(2,1)} %collective-permute-done.5.o2), channel_id=1, source_target_pairs={{0,4},{1,5},{2,6},{3,7},{4,0},{5,1},{6,2},{7,3},{8,12},{9,13},{10,... | collective-permute-start | bytes 1966088 | tf_op jit(solution)/shard_map/ppermute | solution.py:54
  26.7 12.8 %collective-permute-start = (bf16[256,512]{1,0:T(8,128)(2,1)}, bf16[256,512]{1,0:T(8,128)(2,1)S(1)}, u32[]{:S(2)}, u32[]{:S(2)}) collective-permute-start(bf16[256,512]{1,0:T(8,128)(2,1)} %get-tuple-element.19), channel_id=1, source_target_pairs={{0,0},{1,4},{2,64},{3,68},{4,1},{5,5},{6,65},{7,69},{8,8},{9,12},{... | collective-permute-start | bytes 786440 | tf_op jit(solution)/shard_map/ppermute | solution.py:54
  39.6 9.2 %collective-permute-start.3 = (bf16[256,512]{1,0:T(8,128)(2,1)S(1)}, bf16[256,512]{1,0:T(8,128)(2,1)S(1)}, u32[]{:S(2)}, u32[]{:S(2)}) collective-permute-start(bf16[256,512]{1,0:T(8,128)(2,1)S(1)} %collective-permute-done.r0), channel_id=1, source_target_pairs={{0,3},{1,0},{2,1},{3,2},{4,7},{5,4},{6,5},{7,6},{8,11},{9,8},{10,9... | collective-permute-start | bytes 786440 | tf_op jit(solution)/shard_map/ppermute | solution.py:54
  39.6 10.7 %collective-permute-start.2 = (bf16[256,512]{1,0:T(8,128)(2,1)S(1)}, bf16[256,512]{1,0:T(8,128)(2,1)S(1)}, u32[]{:S(2)}, u32[]{:S(2)}) collective-permute-start(bf16[256,512]{1,0:T(8,128)(2,1)S(1)} %collective-permute-done.r0), channel_id=1, source_target_pairs={{0,2},{1,3},{2,0},{3,1},{4,6},{5,7},{6,4},{7,5},{8,10},{9,11},{10,... | collective-permute-start | bytes 786440 | tf_op jit(solution)/shard_map/ppermute | solution.py:54
  39.6 15.9 %collective-permute-start.1 = (bf16[256,512]{1,0:T(8,128)(2,1)S(1)}, bf16[256,512]{1,0:T(8,128)(2,1)S(1)}, u32[]{:S(2)}, u32[]{:S(2)}) collective-permute-start(bf16[256,512]{1,0:T(8,128)(2,1)S(1)} %collective-permute-done.r0), channel_id=1, source_target_pairs={{0,1},{1,2},{2,3},{3,0},{4,5},{5,6},{6,7},{7,4},{8,9},{9,10},{10,1... | collective-permute-start | bytes 786440 | tf_op jit(solution)/shard_map/ppermute | solution.py:54
  48.8 11.0 %copy-start.5 = (bf16[256,512]{1,0:T(8,128)(2,1)}, bf16[256,512]{1,0:T(8,128)(2,1)S(1)}, u32[]{:S(2)}) copy-start(bf16[256,512]{1,0:T(8,128)(2,1)S(1)} %collective-permute-done.3.r3) | copy-start | bytes 786436
  48.8 19.5 %collective-permute-start.8 = (bf16[8,80,512]{2,1,0:T(8,128)(2,1)}, bf16[8,80,512]{2,1,0:T(8,128)(2,1)}, u32[]{:S(2)}, u32[]{:S(2)}) collective-permute-start(bf16[8,80,512]{2,1,0:T(8,128)(2,1)} %all-to-all-done.w0), channel_id=1, source_target_pairs={{0,192},{1,193},{2,194},{3,195},{4,196},{5,197},{6,198},{7,199},{8... | collective-permute-start | bytes 1966088 | tf_op jit(solution)/shard_map/ppermute | solution.py:54
  50.3 9.5 %copy-start.7 = (bf16[256,512]{1,0:T(8,128)(2,1)}, bf16[256,512]{1,0:T(8,128)(2,1)S(1)}, u32[]{:S(2)}) copy-start(bf16[256,512]{1,0:T(8,128)(2,1)S(1)} %collective-permute-done.2.r2) | copy-start | bytes 786436
  55.5 4.3 %copy-start.9 = (bf16[256,512]{1,0:T(8,128)(2,1)}, bf16[256,512]{1,0:T(8,128)(2,1)S(1)}, u32[]{:S(2)}) copy-start(bf16[256,512]{1,0:T(8,128)(2,1)S(1)} %collective-permute-done.1.r1) | copy-start | bytes 786436
  59.8 43.0 %all-to-all-start.1 = ((bf16[8,160,512]{2,1,0:T(8,128)(2,1)}), bf16[8,160,512]{2,1,0:T(8,128)(2,1)S(1)}, u32[]{:S(2)}, u32[]{:S(2)}) async-start(bf16[8,160,512]{2,1,0:T(8,128)(2,1)} %bitcast.5), calls=%async_computation.1 | async-start | bytes 2621440 | tf_op jit(solution)/shard_map/all_to_all | solution.py:58
  68.3 3.7 %copy-start.6 = (bf16[256,512]{1,0:T(8,128)(2,1)S(1)}, bf16[256,512]{1,0:T(8,128)(2,1)}, u32[]{:S(2)}) copy-start(bf16[256,512]{1,0:T(8,128)(2,1)} %copy-done.5) | copy-start | bytes 786436
  68.3 3.7 %copy-start.8 = (bf16[256,512]{1,0:T(8,128)(2,1)S(1)}, bf16[256,512]{1,0:T(8,128)(2,1)}, u32[]{:S(2)}) copy-start(bf16[256,512]{1,0:T(8,128)(2,1)} %copy-done.7) | copy-start | bytes 786436
  68.3 3.7 %copy-start.10 = (bf16[256,512]{1,0:T(8,128)(2,1)S(1)}, bf16[256,512]{1,0:T(8,128)(2,1)}, u32[]{:S(2)}) copy-start(bf16[256,512]{1,0:T(8,128)(2,1)} %copy-done.9) | copy-start | bytes 786436
  73.5 3.4 %collective-permute-start.9 = (bf16[2,256,1280]{2,1,0:T(8,128)(2,1)S(1)}, bf16[2,256,1280]{2,1,0:T(8,128)(2,1)S(1)}, u32[]{:S(2)}, u32[]{:S(2)}) collective-permute-start(bf16[2,256,1280]{2,1,0:T(8,128)(2,1)S(1)} %get-tuple-element.22), channel_id=1, source_target_pairs={{0,4},{1,5},{2,6},{3,7},{4,0},{5,1},{6,2},{7,3},{8,12},{9,13},{10,... | collective-permute-start | bytes 3932168 | tf_op jit(solution)/shard_map/ppermute | solution.py:54
  73.6 15.5 %collective-permute-start.11 = (bf16[256,512]{1,0:T(8,128)(2,1)S(1)}, bf16[256,512]{1,0:T(8,128)(2,1)S(1)}, u32[]{:S(2)}, u32[]{:S(2)}) collective-permute-start(bf16[256,512]{1,0:T(8,128)(2,1)S(1)} %get-tuple-element.24), channel_id=1, source_target_pairs={{0,1},{1,2},{2,3},{3,0},{4,5},{5,6},{6,7},{7,4},{8,9},{9,10},{10,1... | collective-permute-start | bytes 786440 | tf_op jit(solution)/shard_map/ppermute | solution.py:54
  73.7 15.4 %collective-permute-start.12 = (bf16[256,512]{1,0:T(8,128)(2,1)S(1)}, bf16[256,512]{1,0:T(8,128)(2,1)S(1)}, u32[]{:S(2)}, u32[]{:S(2)}) collective-permute-start(bf16[256,512]{1,0:T(8,128)(2,1)S(1)} %get-tuple-element.25), channel_id=1, source_target_pairs={{0,2},{1,3},{2,0},{3,1},{4,6},{5,7},{6,4},{7,5},{8,10},{9,11},{10,... | collective-permute-start | bytes 786440 | tf_op jit(solution)/shard_map/ppermute | solution.py:54
  76.4 13.3 %collective-permute-start.13 = (bf16[256,512]{1,0:T(8,128)(2,1)S(1)}, bf16[256,512]{1,0:T(8,128)(2,1)S(1)}, u32[]{:S(2)}, u32[]{:S(2)}) collective-permute-start(bf16[256,512]{1,0:T(8,128)(2,1)S(1)} %get-tuple-element.26), channel_id=1, source_target_pairs={{0,3},{1,0},{2,1},{3,2},{4,7},{5,4},{6,5},{7,6},{8,11},{9,8},{10,9... | collective-permute-start | bytes 786440 | tf_op jit(solution)/shard_map/ppermute | solution.py:54
  76.9 1.9 %copy-start = (bf16[2,256,1280]{2,1,0:T(8,128)(2,1)}, bf16[2,256,1280]{2,1,0:T(8,128)(2,1)S(1)}, u32[]{:S(2)}) copy-start(bf16[2,256,1280]{2,1,0:T(8,128)(2,1)S(1)} %collective-permute-done.9.pair) | copy-start | bytes 3932164
  78.8 40.8 %collective-permute-start.10 = (bf16[256,1280]{1,0:T(8,128)(2,1)}, bf16[256,1280]{1,0:T(8,128)(2,1)}, u32[]{:S(2)}, u32[]{:S(2)}) collective-permute-start(bf16[256,1280]{1,0:T(8,128)(2,1)} %shard_map.105), channel_id=1, source_target_pairs={{0,64},{1,65},{2,66},{3,67},{4,68},{5,69},{6,70},{7,71},{8,72},{9,... | collective-permute-start | bytes 1966088 | tf_op jit(solution)/shard_map/ppermute | solution.py:54
  89.7 23.6 %copy-start.4 = (bf16[256,512]{1,0:T(8,128)(2,1)S(1)}, bf16[256,512]{1,0:T(8,128)(2,1)}, u32[]{:S(2)}) copy-start(bf16[256,512]{1,0:T(8,128)(2,1)} %q_ref.3) | copy-start | bytes 786436
  89.7 23.6 %copy-start.11 = (bf16[256,128]{1,0:T(8,128)(2,1)S(1)}, bf16[256,128]{1,0:T(8,128)(2,1)}, u32[]{:S(2)}) copy-start(bf16[256,128]{1,0:T(8,128)(2,1)} %k_ref.3) | copy-start | bytes 196612
  89.7 23.6 %copy-start.12 = (bf16[256,128]{1,0:T(8,128)(2,1)S(1)}, bf16[256,128]{1,0:T(8,128)(2,1)}, u32[]{:S(2)}) copy-start(bf16[256,128]{1,0:T(8,128)(2,1)} %v_ref.3) | copy-start | bytes 196612
  91.1 22.2 %collective-permute-start.14 = (bf16[256,512]{1,0:T(8,128)(2,1)}, bf16[256,512]{1,0:T(8,128)(2,1)}, u32[]{:S(2)}, u32[]{:S(2)}) collective-permute-start(bf16[256,512]{1,0:T(8,128)(2,1)} %shard_map.106), channel_id=1, source_target_pairs={{0,0},{1,4},{2,64},{3,68},{4,1},{5,5},{6,65},{7,69},{8,8},{9,12},{... | collective-permute-start | bytes 786440 | tf_op jit(solution)/shard_map/ppermute | solution.py:54
  102.8 15.0 %copy-start.1 = (bf16[2,256,1280]{2,1,0:T(8,128)(2,1)S(1)}, bf16[2,256,1280]{2,1,0:T(8,128)(2,1)}, u32[]{:S(2)}) copy-start(bf16[2,256,1280]{2,1,0:T(8,128)(2,1)} %copy-done) | copy-start | bytes 3932164
  103.6 15.4 %collective-permute-start.15 = (bf16[80,512]{1,0:T(8,128)(2,1)S(1)}, bf16[80,512]{1,0:T(8,128)(2,1)S(1)}, u32[]{:S(2)}, u32[]{:S(2)}) collective-permute-start(bf16[80,512]{1,0:T(8,128)(2,1)S(1)} %get-tuple-element.31), channel_id=1, source_target_pairs={{0,0},{1,64},{2,128},{3,192},{4,1},{5,65},{6,129},{7,193},{8,8},{9... | collective-permute-start | bytes 245768 | tf_op jit(solution)/shard_map/ppermute | solution.py:54
  105.5 13.4 %collective-permute-start.16 = (bf16[80,512]{1,0:T(8,128)(2,1)S(1)}, bf16[80,512]{1,0:T(8,128)(2,1)S(1)}, u32[]{:S(2)}, u32[]{:S(2)}) collective-permute-start(bf16[80,512]{1,0:T(8,128)(2,1)S(1)} %get-tuple-element.32), channel_id=1, source_target_pairs={{0,4},{1,68},{2,132},{3,196},{4,5},{5,69},{6,133},{7,197},{8,12},{... | collective-permute-start | bytes 245768 | tf_op jit(solution)/shard_map/ppermute | solution.py:54
  113.4 1.2 %copy-start.2 = (f32[4,256,256]{2,1,0:T(8,128)S(1)}, f32[4,256,256]{2,1,0:T(8,128)}, u32[]{:S(2)}) copy-start(f32[4,256,256]{2,1,0:T(8,128)} %get-tuple-element.27.prob_ref) | copy-start | bytes 3145732

commit v5 on v4

--- a/solution.py
+++ b/solution.py
@@ -116,7 +116,8 @@
     ).astype(BF)
 
 
-def backward_body(_, up_ref, q_ref, k_ref, v_ref, prob_ref, dq_ref, dk_ref, dv_ref):
+def backward_body(_, up_ref, q_ref, k_ref, v_ref, prob_ref, own, across, dq_ref, dk_ref, dv_ref, out):
+    out[...] = (own[...].astype(F32) + across[...].astype(F32)).astype(BF)
     key_sum = jnp.zeros((TOK, HEAD), F32)
     value_sum = jnp.zeros((TOK, HEAD), F32)
     for h in range(HEADS):
@@ -213,6 +214,7 @@
         scratch=(pltpu.VMEM((4, TOK, GROUP), BF),),
         flops=big,
         moved=6 << 20,
+        limit=63,
     )(place, *cols, *heads)
     grad_rows = exchange(grad_part.reshape(NZ, 2 * SHARD, GROUP), Z_GROUPS)
 
@@ -239,18 +241,18 @@
     own = call(layer_own_body, shape(TOK, COLS), flops=big // 4, moved=4 << 20)(
         place, attended_two, wt_all, pair
     )
-    layer_out = (own.astype(F32) + across.astype(F32)).astype(BF)
 
     partials = [partials[0]] + [send(p, pairs) for p, pairs in zip(partials[1:], ALONG_Y)]
     upstream = call(sum_four_body, shape(TOK, GROUP), moved=1 << 20)(place, *partials)
     upstream = send(upstream, TURN)
 
-    query_grad, key_grad, value_grad = call(
+    query_grad, key_grad, value_grad, layer_out = call(
         backward_body,
-        (shape(TOK, GROUP), shape(TOK, HEAD), shape(TOK, HEAD)),
+        (shape(TOK, GROUP), shape(TOK, HEAD), shape(TOK, HEAD), shape(TOK, COLS)),
         flops=5 * 4 * 2 * TOK * TOK * HEAD,
         moved=3 << 20,
-    )(place, upstream, query_rows, key_rows, value_matrix, prob)
+        limit=63,
+    )(place, upstream, query_rows, key_rows, value_matrix, prob, own, across)
 
     pieces = call(sum_z_body, (shape(SHARD, GROUP),) * 2, moved=2 << 20)(place, grad_rows)
     pieces = [send(piece, pairs).astype(F32) for piece, pairs in zip(pieces, TO_OWNER)]

time: 122 us -> 134 us (1.098)
  waiting for transfers between devices: 47.3 us -> 59 us
  Pallas kernels: 20.8 us -> 23.9 us
  starting transfers between devices: 47.7 us -> 45 us
  other arithmetic: 2.84 us -> 1.29 us
    all_to_all x2, waiting for transfers between devices: 8.28 us -> 19.3 us  [exchange(): lax.all_to_all(blocks, 'dp', 0, 0, axis_index_groups=groups, tiled=True)]
    pallas_call x9, Pallas kernels: 20.8 us -> 23.9 us  [run(): pl.pallas_call(body, out_shape=outs, grid=(1,), in_specs=[pl.BlockSpec(me...]
    ppermute x17, starting transfers between devices: 30.8 us -> 28 us  [send(): return lax.ppermute(value, AXES, pairs)]
    convert_element_type x1 -> x0, other arithmetic: 2.07 us -> none  [per_device(): layer_out = (own.astype(F32) + across.astype(F32)).astype(BF)]
  transfers between devices with their start and end apart: 19 -> 19, of which waited for: 9 -> 9; matrix products, arithmetic and copies ran while one was open for 1% -> 2% of each run, Pallas kernels for 17% -> 14%
where the time goes in v5:
time: 134 us; the launch traced here: 133 us
  waiting for transfers between devices  59 us (44%)
  starting transfers between devices  45 us (34%)
  Pallas kernels  23.9 us (18%)
  local copies, waits for them, and re-layouts  3.19 us (2%)
    ppermute x17, waiting for transfers between devices, send(): return lax.ppermute(value, AXES, pairs)  39.7 us
    ppermute x17, starting transfers between devices, send(): return lax.ppermute(value, AXES, pairs)  28 us
    pallas_call x9, Pallas kernels, run(): pl.pallas_call(body, out_shape=outs, grid=(1,), in_specs=[pl.BlockSpec(me...  23.9 us
    all_to_all x2, waiting for transfers between devices, exchange(): lax.all_to_all(blocks, 'dp', 0, 0, axis_index_groups=groups, tiled=True)  19.3 us
    all_to_all x2, starting transfers between devices, exchange(): lax.all_to_all(blocks, 'dp', 0, 0, axis_index_groups=groups, tiled=True)  17.1 us
  transfers between devices with their start and end apart: 19, of which 9 were waited for; matrix products, arithmetic and copies ran while one was open for 2% of the time, Pallas kernels for 14%

profile of v5, /device:TPU:4, one launch (start us, length us, event | category | flops | bytes accessed | tf_op | source)
XLA Modules:
  0.0 133.3 jit_solution(10856394687753483878)
XLA Ops:
  0.6 0.0 copy-start.1
  0.6 5.2 %collective-permute-start.3 = (bf16[80,512]{1,0:T(8,128)(2,1)}, bf16[80,512]{1,0:T(8,128)(2,1)S(1)}, u32[]{:S(2)}, u32[]{:S(2)}) collective-permute-start(bf16[80,512]{1,0:T(8,128)(2,1)} %bitcast.9), channel_id=1, source_target_pairs={{0,0},{1,4},{2,64},{3,68},{4,192},{5,196},{6,128},{7,132},{8,8},{9... | collective-permute-start | bytes 245768 | tf_op jit(solution)/shard_map/ppermute | solution.py:54
  5.8 1.1 collective-permute-start.1
  6.9 4.6 %collective-permute-done.3 = bf16[80,512]{1,0:T(8,128)(2,1)S(1)} collective-permute-done((bf16[80,512]{1,0:T(8,128)(2,1)}, bf16[80,512]{1,0:T(8,128)(2,1)S(1)}, u32[]{:S(2)}, u32[]{:S(2)}) %collective-permute-start.3) | collective-permute-done | bytes 81952 | tf_op jit(solution)/shard_map/ppermute | solution.py:54
  11.5 0.9 broadcast_in_dim.2
  12.4 8.5 %all-to-all-start = ((bf16[8,80,512]{2,1,0:T(8,128)(2,1)}), bf16[8,80,512]{2,1,0:T(8,128)(2,1)}, u32[]{:S(2)}, u32[]{:S(2)}) async-start(bf16[8,80,512]{2,1,0:T(8,128)(2,1)} %broadcast_in_dim.2), calls=%async_computation | async-start | bytes 1310720 | tf_op jit(solution)/shard_map/all_to_all | solution.py:58
  20.9 0.0 copy-done.1
  20.9 0.1 collective-permute-start
  21.0 2.7 %collective-permute-done.1.o2 = bf16[256,1280]{1,0:T(8,128)(2,1)} collective-permute-done((bf16[256,1280]{1,0:T(8,128)(2,1)}, bf16[256,1280]{1,0:T(8,128)(2,1)}, u32[]{:S(2)}, u32[]{:S(2)}) %collective-permute-start.1) | collective-permute-done | bytes 655392 | tf_op jit(solution)/shard_map/ppermute | solution.py:54
  23.7 0.0 collective-permute-start.2
  23.7 3.1 %shard_map.103 = (bf16[256,512]{1,0:T(8,128)(2,1)}, f32[4,256,256]{2,1,0:T(8,128)}) custom-call(s32[8]{0:T(128)} %bitcast.10, bf16[256,512]{1,0:T(8,128)(2,1)} %q_ref.3, bf16[256,128]{1,0:T(8,128)(2,1)} %k_ref.3, bf16[256,128]{1,0:T(8,128)(2,1)} %v_ref.3), custom_call_target="tpu_custom_call" | custom-call | flops 134217728 | bytes 2097152 | tf_op jit(solution)/shard_map/pallas_call | solution.py:72
  26.7 3.4 %collective-permute-start.9 = (bf16[256,512]{1,0:T(8,128)(2,1)}, bf16[256,512]{1,0:T(8,128)(2,1)S(1)}, u32[]{:S(2)}, u32[]{:S(2)}) collective-permute-start(bf16[256,512]{1,0:T(8,128)(2,1)} %get-tuple-element.25), channel_id=1, source_target_pairs={{0,0},{1,4},{2,64},{3,68},{4,1},{5,5},{6,65},{7,69},{8,8},{9,12},{... | collective-permute-start | bytes 786440 | tf_op jit(solution)/shard_map/ppermute | solution.py:54
  30.2 9.4 %collective-permute-done.9.r0 = bf16[256,512]{1,0:T(8,128)(2,1)S(1)} collective-permute-done((bf16[256,512]{1,0:T(8,128)(2,1)}, bf16[256,512]{1,0:T(8,128)(2,1)S(1)}, u32[]{:S(2)}, u32[]{:S(2)}) %collective-permute-start.9) | collective-permute-done | bytes 262176 | tf_op jit(solution)/shard_map/ppermute | solution.py:54
  39.6 0.0 collective-permute-start.12
  39.6 0.0 collective-permute-start.11
  39.6 2.0 %collective-permute-start.10 = (bf16[256,512]{1,0:T(8,128)(2,1)S(1)}, bf16[256,512]{1,0:T(8,128)(2,1)S(1)}, u32[]{:S(2)}, u32[]{:S(2)}) collective-permute-start(bf16[256,512]{1,0:T(8,128)(2,1)S(1)} %collective-permute-done.9.r0), channel_id=1, source_target_pairs={{0,1},{1,2},{2,3},{3,0},{4,5},{5,6},{6,7},{7,4},{8,9},{9,10},{10,1... | collective-permute-start | bytes 786440 | tf_op jit(solution)/shard_map/ppermute | solution.py:54
  41.6 7.1 %collective-permute-done.12.r3 = bf16[256,512]{1,0:T(8,128)(2,1)S(1)} collective-permute-done((bf16[256,512]{1,0:T(8,128)(2,1)S(1)}, bf16[256,512]{1,0:T(8,128)(2,1)S(1)}, u32[]{:S(2)}, u32[]{:S(2)}) %collective-permute-start.12) | collective-permute-done | bytes 262176 | tf_op jit(solution)/shard_map/ppermute | solution.py:54
  48.8 0.0 all-to-all-done.w0
  48.8 0.0 collective-permute-start.4
  48.8 0.6 pad_add_fusion.place._
  49.4 0.9 collective-permute-done.11.r2
  50.3 5.2 %collective-permute-done.10.r1 = bf16[256,512]{1,0:T(8,128)(2,1)S(1)} collective-permute-done((bf16[256,512]{1,0:T(8,128)(2,1)S(1)}, bf16[256,512]{1,0:T(8,128)(2,1)S(1)}, u32[]{:S(2)}, u32[]{:S(2)}) %collective-permute-start.10) | collective-permute-done | bytes 262176 | tf_op jit(solution)/shard_map/ppermute | solution.py:54
  55.5 0.0 collective-permute-done.o1
  55.5 0.0 copy-done.5
  55.5 0.0 copy-done.7
  55.5 0.7 copy-done.9
  56.2 0.0 collective-permute-done.2.o3
  56.2 0.0 copy-done.3
  56.2 4.7 %shard_map.108 = bf16[1280,512]{1,0:T(8,128)(2,1)} custom-call(s32[3]{0:T(128)} %pad_add_fusion.place._, bf16[256,1280]{1,0:T(8,128)(2,1)} %o0.3, bf16[256,1280]{1,0:T(8,128)(2,1)} %collective-permute-done.o1, bf16[256,1280]{1,0:T(8,128)(2,1)} %collective-permute-done.1.o2, bf16[256,1280]{1,0:T(8,128)(2,1)} %collective-permute-done.2.o3, ...), custom_call_target="tpu_custom_call" | custom-call | flops 1342177280 | bytes 6291456 | tf_op jit(solution)/shard_map/pallas_call | solution.py:72
  60.9 8.6 %all-to-all-start.1 = ((bf16[8,160,512]{2,1,0:T(8,128)(2,1)}), bf16[8,160,512]{2,1,0:T(8,128)(2,1)}, u32[]{:S(2)}, u32[]{:S(2)}) async-start(bf16[8,160,512]{2,1,0:T(8,128)(2,1)} %bitcast.8), calls=%async_computation.1 | async-start | bytes 2621440 | tf_op jit(solution)/shard_map/all_to_all | solution.py:58
  69.5 0.0 copy-start.6
  69.5 0.0 copy-start.8
  69.5 0.0 copy-start.10
  69.5 0.0 collective-permute-done.4.w1
  69.5 0.0 copy-done.2
  69.5 0.0 copy-done.11
  69.6 4.4 %shard_map.101 = (bf16[256,512]{1,0:T(8,128)(2,1)S(1)}, bf16[256,512]{1,0:T(8,128)(2,1)}, bf16[256,512]{1,0:T(8,128)(2,1)}, bf16[256,512]{1,0:T(8,128)(2,1)}, bf16[1280,512]{1,0:T(8,128)(2,1)S(1)}) custom-call(s32[3]{0:T(128)S(1)} %copy-done.11, bf16[256,1280]{1,0:T(8,128)(2,1)S(1)} %copy-done.2, bf16[256,1280]{1,0:T(8,128)(2,1)} %collective-permute-done.o1, ...), custom_call_target="tpu_custom_call" | custom-call | flops 1342177280 | bytes 6291456 | tf_op jit(solution)/shard_map/pallas_call | solution.py:72
  74.0 1.4 %shard_map.104 = (bf16[2,256,1280]{2,1,0:T(8,128)(2,1)S(1)}, bf16[2,256,512]{2,1,0:T(8,128)(2,1)S(1)}) custom-call(s32[3]{0:T(128)S(1)} %copy-done.11, bf16[256,512]{1,0:T(8,128)(2,1)S(1)} %copy-done.4, bf16[256,512]{1,0:T(8,128)(2,1)S(1)} %copy-done.10, bf16[256,512]{1,0:T(8,128)(2,1)S(1)} %copy-done.8, bf16[256,512]{1,0:T(8,128)(2,1)S(1)} %copy-done.6, ...), custom_call_target="tpu_custom_call" | custom-call | flops 671088640 | bytes 4194304 | tf_op jit(solution)/shard_map/pallas_call | solution.py:72
  75.4 0.1 collective-permute-start.13
  75.5 3.0 %collective-permute-done.13.pair = bf16[2,256,1280]{2,1,0:T(8,128)(2,1)S(1)} collective-permute-done((bf16[2,256,1280]{2,1,0:T(8,128)(2,1)S(1)}, bf16[2,256,1280]{2,1,0:T(8,128)(2,1)S(1)}, u32[]{:S(2)}, u32[]{:S(2)}) %collective-permute-start.13) | collective-permute-done | bytes 1310752 | tf_op jit(solution)/shard_map/ppermute | solution.py:54
  78.6 1.9 %shard_map.106 = bf16[256,1280]{1,0:T(8,128)(2,1)} custom-call(s32[3]{0:T(128)S(1)} %copy-done.11, bf16[2,256,512]{2,1,0:T(8,128)(2,1)S(1)} %get-tuple-element.27.att, bf16[1280,512]{1,0:T(8,128)(2,1)S(1)} %get-tuple-element.26.wt, bf16[2,256,1280]{2,1,0:T(8,128)(2,1)S(1)} %collective-permute-done.13.pair), custom_call_target="tpu_custom_call" | custom-call | flops 335544320 | bytes 3145728 | tf_op jit(solution)/shard_map/pallas_call | solution.py:72
  80.5 0.0 collective-permute-start.14
  80.5 0.0 collective-permute-start.5
  80.5 4.4 %collective-permute-start.6 = (bf16[256,512]{1,0:T(8,128)(2,1)}, bf16[256,512]{1,0:T(8,128)(2,1)}, u32[]{:S(2)}, u32[]{:S(2)}) collective-permute-start(bf16[256,512]{1,0:T(8,128)(2,1)} %get-tuple-element.22), channel_id=1, source_target_pairs={{0,2},{1,3},{2,0},{3,1},{4,6},{5,7},{6,4},{7,5},{8,10},{9,11},{10,... | collective-permute-start | bytes 786440 | tf_op jit(solution)/shard_map/ppermute | solution.py:54
  84.9 0.0 collective-permute-start.7
  84.9 19.3 %all-to-all-done.1.blocks = bf16[8,160,512]{2,1,0:T(8,128)(2,1)} async-done(((bf16[8,160,512]{2,1,0:T(8,128)(2,1)}), bf16[8,160,512]{2,1,0:T(8,128)(2,1)}, u32[]{:S(2)}, u32[]{:S(2)}) %all-to-all-start.1) | async-done | bytes 1310752 | tf_op jit(solution)/shard_map/all_to_all | solution.py:58
  104.2 1.5 %shard_map.109 = (bf16[80,512]{1,0:T(8,128)(2,1)S(1)}, bf16[80,512]{1,0:T(8,128)(2,1)S(1)}) custom-call(s32[3]{0:T(128)S(1)} %copy-done.11, bf16[8,160,512]{2,1,0:T(8,128)(2,1)} %all-to-all-done.1.blocks), custom_call_target="tpu_custom_call" | custom-call | bytes 2097152 | tf_op jit(solution)/shard_map/pallas_call | solution.py:72
  105.7 1.9 %collective-permute-start.15 = (bf16[80,512]{1,0:T(8,128)(2,1)S(1)}, bf16[80,512]{1,0:T(8,128)(2,1)S(1)}, u32[]{:S(2)}, u32[]{:S(2)}) collective-permute-start(bf16[80,512]{1,0:T(8,128)(2,1)S(1)} %get-tuple-element.33), channel_id=1, source_target_pairs={{0,0},{1,64},{2,128},{3,192},{4,1},{5,65},{6,129},{7,193},{8,8},{9... | collective-permute-start | bytes 245768 | tf_op jit(solution)/shard_map/ppermute | solution.py:54
  107.6 0.0 collective-permute-done.5.a1
  107.6 7.8 %collective-permute-start.16 = (bf16[80,512]{1,0:T(8,128)(2,1)S(1)}, bf16[80,512]{1,0:T(8,128)(2,1)S(1)}, u32[]{:S(2)}, u32[]{:S(2)}) collective-permute-start(bf16[80,512]{1,0:T(8,128)(2,1)S(1)} %get-tuple-element.34), channel_id=1, source_target_pairs={{0,4},{1,68},{2,132},{3,196},{4,5},{5,69},{6,133},{7,197},{8,12},{... | collective-permute-start | bytes 245768 | tf_op jit(solution)/shard_map/ppermute | solution.py:54
  115.4 0.0 collective-permute-done.6.a2
  115.5 0.0 collective-permute-done.7.a3
  115.5 1.2 shard_map.102
  116.7 1.9 %collective-permute-start.8 = (bf16[256,512]{1,0:T(8,128)(2,1)S(1)}, bf16[256,512]{1,0:T(8,128)(2,1)S(1)}, u32[]{:S(2)}, u32[]{:S(2)}) collective-permute-start(bf16[256,512]{1,0:T(8,128)(2,1)S(1)} %shard_map.102), channel_id=1, source_target_pairs={{0,0},{1,4},{2,64},{3,68},{4,1},{5,5},{6,65},{7,69},{8,8},{9,12},{... | collective-permute-start | bytes 786440 | tf_op jit(solution)/shard_map/ppermute | solution.py:54
  118.6 1.1 shard_map.105.own
  119.7 0.0 copy-start
  119.7 0.9 copy-done
  120.6 0.0 collective-permute-done.15
  120.6 0.0 collective-permute-done.16
  120.6 0.7 add_bitcast_fusion
  121.3 6.7 %collective-permute-done.8.up_ref = bf16[256,512]{1,0:T(8,128)(2,1)S(1)} collective-permute-done((bf16[256,512]{1,0:T(8,128)(2,1)S(1)}, bf16[256,512]{1,0:T(8,128)(2,1)S(1)}, u32[]{:S(2)}, u32[]{:S(2)}) %collective-permute-start.8) | collective-permute-done | bytes 262176 | tf_op jit(solution)/shard_map/ppermute | solution.py:54
  128.0 0.0 collective-permute-done.14.across
  128.0 0.7 copy-done.12
  128.7 4.6 %shard_map.107 = (bf16[256,512]{1,0:T(8,128)(2,1)}, bf16[256,128]{1,0:T(8,128)(2,1)}, bf16[256,128]{1,0:T(8,128)(2,1)}, bf16[256,1280]{1,0:T(8,128)(2,1)}) custom-call(s32[3]{0:T(128)} %pad_add_fusion.place._, bf16[256,512]{1,0:T(8,128)(2,1)} %copy-done.12, bf16[256,512]{1,0:T(8,128)(2,1)} %q_ref.3, bf16[256,128]{1,0:T(8,128)(2,1)} %k_ref.3, ...), custom_call_target="tpu_custom_call" | custom-call | flops 335544320 | bytes 3145728 | tf_op jit(solution)/shard_map/pallas_call | solution.py:72
  (12 shorter events, 0.0 us)
Async XLA Ops:
  0.6 20.3 %copy-start.1 = (bf16[256,1280]{1,0:T(8,128)(2,1)S(1)}, bf16[256,1280]{1,0:T(8,128)(2,1)}, u32[]{:S(2)}) copy-start(bf16[256,1280]{1,0:T(8,128)(2,1)} %o0.3) | copy-start | bytes 1966084
  0.6 10.9 %collective-permute-start.3 = (bf16[80,512]{1,0:T(8,128)(2,1)}, bf16[80,512]{1,0:T(8,128)(2,1)S(1)}, u32[]{:S(2)}, u32[]{:S(2)}) collective-permute-start(bf16[80,512]{1,0:T(8,128)(2,1)} %bitcast.9), channel_id=1, source_target_pairs={{0,0},{1,4},{2,64},{3,68},{4,192},{5,196},{6,128},{7,132},{8,8},{9... | collective-permute-start | bytes 245768 | tf_op jit(solution)/shard_map/ppermute | solution.py:54
  5.8 17.8 %collective-permute-start.1 = (bf16[256,1280]{1,0:T(8,128)(2,1)}, bf16[256,1280]{1,0:T(8,128)(2,1)}, u32[]{:S(2)}, u32[]{:S(2)}) collective-permute-start(bf16[256,1280]{1,0:T(8,128)(2,1)} %o0.3), channel_id=1, source_target_pairs={{0,64},{1,65},{2,66},{3,67},{4,68},{5,69},{6,70},{7,71},{8,72},{9,... | collective-permute-start | bytes 1966088 | tf_op jit(solution)/shard_map/ppermute | solution.py:54
  12.4 36.4 %all-to-all-start = ((bf16[8,80,512]{2,1,0:T(8,128)(2,1)}), bf16[8,80,512]{2,1,0:T(8,128)(2,1)}, u32[]{:S(2)}, u32[]{:S(2)}) async-start(bf16[8,80,512]{2,1,0:T(8,128)(2,1)} %broadcast_in_dim.2), calls=%async_computation | async-start | bytes 1310720 | tf_op jit(solution)/shard_map/all_to_all | solution.py:58
  20.9 34.6 %collective-permute-start = (bf16[256,1280]{1,0:T(8,128)(2,1)S(1)}, bf16[256,1280]{1,0:T(8,128)(2,1)}, u32[]{:S(2)}, u32[]{:S(2)}) collective-permute-start(bf16[256,1280]{1,0:T(8,128)(2,1)S(1)} %copy-done.1), channel_id=1, source_target_pairs={{0,4},{1,5},{2,6},{3,7},{4,0},{5,1},{6,2},{7,3},{8,12},{9,13},{10,... | collective-permute-start | bytes 1966088 | tf_op jit(solution)/shard_map/ppermute | solution.py:54
  23.7 32.5 %collective-permute-start.2 = (bf16[256,1280]{1,0:T(8,128)(2,1)}, bf16[256,1280]{1,0:T(8,128)(2,1)}, u32[]{:S(2)}, u32[]{:S(2)}) collective-permute-start(bf16[256,1280]{1,0:T(8,128)(2,1)} %collective-permute-done.1.o2), channel_id=1, source_target_pairs={{0,4},{1,5},{2,6},{3,7},{4,0},{5,1},{6,2},{7,3},{8,12},{9,13},{10,... | collective-permute-start | bytes 1966088 | tf_op jit(solution)/shard_map/ppermute | solution.py:54
  26.7 12.9 %collective-permute-start.9 = (bf16[256,512]{1,0:T(8,128)(2,1)}, bf16[256,512]{1,0:T(8,128)(2,1)S(1)}, u32[]{:S(2)}, u32[]{:S(2)}) collective-permute-start(bf16[256,512]{1,0:T(8,128)(2,1)} %get-tuple-element.25), channel_id=1, source_target_pairs={{0,0},{1,4},{2,64},{3,68},{4,1},{5,5},{6,65},{7,69},{8,8},{9,12},{... | collective-permute-start | bytes 786440 | tf_op jit(solution)/shard_map/ppermute | solution.py:54
  39.6 16.6 %copy-start.3 = (bf16[256,512]{1,0:T(8,128)(2,1)}, bf16[256,512]{1,0:T(8,128)(2,1)S(1)}, u32[]{:S(2)}) copy-start(bf16[256,512]{1,0:T(8,128)(2,1)S(1)} %collective-permute-done.9.r0) | copy-start | bytes 786436
  39.6 9.2 %collective-permute-start.12 = (bf16[256,512]{1,0:T(8,128)(2,1)S(1)}, bf16[256,512]{1,0:T(8,128)(2,1)S(1)}, u32[]{:S(2)}, u32[]{:S(2)}) collective-permute-start(bf16[256,512]{1,0:T(8,128)(2,1)S(1)} %collective-permute-done.9.r0), channel_id=1, source_target_pairs={{0,3},{1,0},{2,1},{3,2},{4,7},{5,4},{6,5},{7,6},{8,11},{9,8},{10,9... | collective-permute-start | bytes 786440 | tf_op jit(solution)/shard_map/ppermute | solution.py:54
  39.6 10.7 %collective-permute-start.11 = (bf16[256,512]{1,0:T(8,128)(2,1)S(1)}, bf16[256,512]{1,0:T(8,128)(2,1)S(1)}, u32[]{:S(2)}, u32[]{:S(2)}) collective-permute-start(bf16[256,512]{1,0:T(8,128)(2,1)S(1)} %collective-permute-done.9.r0), channel_id=1, source_target_pairs={{0,2},{1,3},{2,0},{3,1},{4,6},{5,7},{6,4},{7,5},{8,10},{9,11},{10,... | collective-permute-start | bytes 786440 | tf_op jit(solution)/shard_map/ppermute | solution.py:54
  39.6 15.9 %collective-permute-start.10 = (bf16[256,512]{1,0:T(8,128)(2,1)S(1)}, bf16[256,512]{1,0:T(8,128)(2,1)S(1)}, u32[]{:S(2)}, u32[]{:S(2)}) collective-permute-start(bf16[256,512]{1,0:T(8,128)(2,1)S(1)} %collective-permute-done.9.r0), channel_id=1, source_target_pairs={{0,1},{1,2},{2,3},{3,0},{4,5},{5,6},{6,7},{7,4},{8,9},{9,10},{10,1... | collective-permute-start | bytes 786440 | tf_op jit(solution)/shard_map/ppermute | solution.py:54
  48.8 6.7 %copy-start.5 = (bf16[256,512]{1,0:T(8,128)(2,1)}, bf16[256,512]{1,0:T(8,128)(2,1)S(1)}, u32[]{:S(2)}) copy-start(bf16[256,512]{1,0:T(8,128)(2,1)S(1)} %collective-permute-done.12.r3) | copy-start | bytes 786436
  48.8 20.7 %collective-permute-start.4 = (bf16[8,80,512]{2,1,0:T(8,128)(2,1)}, bf16[8,80,512]{2,1,0:T(8,128)(2,1)}, u32[]{:S(2)}, u32[]{:S(2)}) collective-permute-start(bf16[8,80,512]{2,1,0:T(8,128)(2,1)} %all-to-all-done.w0), channel_id=1, source_target_pairs={{0,192},{1,193},{2,194},{3,195},{4,196},{5,197},{6,198},{7,199},{8... | collective-permute-start | bytes 1966088 | tf_op jit(solution)/shard_map/ppermute | solution.py:54
  50.3 5.2 %copy-start.7 = (bf16[256,512]{1,0:T(8,128)(2,1)}, bf16[256,512]{1,0:T(8,128)(2,1)S(1)}, u32[]{:S(2)}) copy-start(bf16[256,512]{1,0:T(8,128)(2,1)S(1)} %collective-permute-done.11.r2) | copy-start | bytes 786436
  55.5 0.7 copy-start.9
  60.9 8.7 %copy-start.2 = (bf16[256,1280]{1,0:T(8,128)(2,1)S(1)}, bf16[256,1280]{1,0:T(8,128)(2,1)}, u32[]{:S(2)}) copy-start(bf16[256,1280]{1,0:T(8,128)(2,1)} %o0.3) | copy-start | bytes 1966084
  60.9 8.7 %copy-start.11 = (s32[3]{0:T(128)S(1)}, s32[3]{0:T(128)}, u32[]{:S(2)}) copy-start(s32[3]{0:T(128)} %pad_add_fusion.place._) | copy-start | bytes 40
  60.9 43.3 %all-to-all-start.1 = ((bf16[8,160,512]{2,1,0:T(8,128)(2,1)}), bf16[8,160,512]{2,1,0:T(8,128)(2,1)}, u32[]{:S(2)}, u32[]{:S(2)}) async-start(bf16[8,160,512]{2,1,0:T(8,128)(2,1)} %bitcast.8), calls=%async_computation.1 | async-start | bytes 2621440 | tf_op jit(solution)/shard_map/all_to_all | solution.py:58
  69.5 4.5 %copy-start.4 = (bf16[256,512]{1,0:T(8,128)(2,1)S(1)}, bf16[256,512]{1,0:T(8,128)(2,1)}, u32[]{:S(2)}) copy-start(bf16[256,512]{1,0:T(8,128)(2,1)} %copy-done.3) | copy-start | bytes 786436
  69.5 4.5 %copy-start.6 = (bf16[256,512]{1,0:T(8,128)(2,1)S(1)}, bf16[256,512]{1,0:T(8,128)(2,1)}, u32[]{:S(2)}) copy-start(bf16[256,512]{1,0:T(8,128)(2,1)} %copy-done.5) | copy-start | bytes 786436
  69.5 4.5 %copy-start.8 = (bf16[256,512]{1,0:T(8,128)(2,1)S(1)}, bf16[256,512]{1,0:T(8,128)(2,1)}, u32[]{:S(2)}) copy-start(bf16[256,512]{1,0:T(8,128)(2,1)} %copy-done.7) | copy-start | bytes 786436
  69.5 4.5 %copy-start.10 = (bf16[256,512]{1,0:T(8,128)(2,1)S(1)}, bf16[256,512]{1,0:T(8,128)(2,1)}, u32[]{:S(2)}) copy-start(bf16[256,512]{1,0:T(8,128)(2,1)} %copy-done.9) | copy-start | bytes 786436
  75.4 3.1 %collective-permute-start.13 = (bf16[2,256,1280]{2,1,0:T(8,128)(2,1)S(1)}, bf16[2,256,1280]{2,1,0:T(8,128)(2,1)S(1)}, u32[]{:S(2)}, u32[]{:S(2)}) collective-permute-start(bf16[2,256,1280]{2,1,0:T(8,128)(2,1)S(1)} %get-tuple-element.28), channel_id=1, source_target_pairs={{0,4},{1,5},{2,6},{3,7},{4,0},{5,1},{6,2},{7,3},{8,12},{9,13},{10,... | collective-permute-start | bytes 3932168 | tf_op jit(solution)/shard_map/ppermute | solution.py:54
  80.5 47.5 %collective-permute-start.14 = (bf16[256,1280]{1,0:T(8,128)(2,1)}, bf16[256,1280]{1,0:T(8,128)(2,1)}, u32[]{:S(2)}, u32[]{:S(2)}) collective-permute-start(bf16[256,1280]{1,0:T(8,128)(2,1)} %shard_map.106), channel_id=1, source_target_pairs={{0,64},{1,65},{2,66},{3,67},{4,68},{5,69},{6,70},{7,71},{8,72},{9,... | collective-permute-start | bytes 1966088 | tf_op jit(solution)/shard_map/ppermute | solution.py:54
  80.5 27.1 %collective-permute-start.5 = (bf16[256,512]{1,0:T(8,128)(2,1)}, bf16[256,512]{1,0:T(8,128)(2,1)}, u32[]{:S(2)}, u32[]{:S(2)}) collective-permute-start(bf16[256,512]{1,0:T(8,128)(2,1)} %get-tuple-element.21), channel_id=1, source_target_pairs={{0,1},{1,2},{2,3},{3,0},{4,5},{5,6},{6,7},{7,4},{8,9},{9,10},{10,1... | collective-permute-start | bytes 786440 | tf_op jit(solution)/shard_map/ppermute | solution.py:54
  80.5 35.0 %collective-permute-start.6 = (bf16[256,512]{1,0:T(8,128)(2,1)}, bf16[256,512]{1,0:T(8,128)(2,1)}, u32[]{:S(2)}, u32[]{:S(2)}) collective-permute-start(bf16[256,512]{1,0:T(8,128)(2,1)} %get-tuple-element.22), channel_id=1, source_target_pairs={{0,2},{1,3},{2,0},{3,1},{4,6},{5,7},{6,4},{7,5},{8,10},{9,11},{10,... | collective-permute-start | bytes 786440 | tf_op jit(solution)/shard_map/ppermute | solution.py:54
  84.9 30.6 %collective-permute-start.7 = (bf16[256,512]{1,0:T(8,128)(2,1)}, bf16[256,512]{1,0:T(8,128)(2,1)}, u32[]{:S(2)}, u32[]{:S(2)}) collective-permute-start(bf16[256,512]{1,0:T(8,128)(2,1)} %get-tuple-element.23), channel_id=1, source_target_pairs={{0,3},{1,0},{2,1},{3,2},{4,7},{5,4},{6,5},{7,6},{8,11},{9,8},{10,9... | collective-permute-start | bytes 786440 | tf_op jit(solution)/shard_map/ppermute | solution.py:54
  105.7 14.9 %collective-permute-start.15 = (bf16[80,512]{1,0:T(8,128)(2,1)S(1)}, bf16[80,512]{1,0:T(8,128)(2,1)S(1)}, u32[]{:S(2)}, u32[]{:S(2)}) collective-permute-start(bf16[80,512]{1,0:T(8,128)(2,1)S(1)} %get-tuple-element.33), channel_id=1, source_target_pairs={{0,0},{1,64},{2,128},{3,192},{4,1},{5,65},{6,129},{7,193},{8,8},{9... | collective-permute-start | bytes 245768 | tf_op jit(solution)/shard_map/ppermute | solution.py:54
  107.6 13.0 %collective-permute-start.16 = (bf16[80,512]{1,0:T(8,128)(2,1)S(1)}, bf16[80,512]{1,0:T(8,128)(2,1)S(1)}, u32[]{:S(2)}, u32[]{:S(2)}) collective-permute-start(bf16[80,512]{1,0:T(8,128)(2,1)S(1)} %get-tuple-element.34), channel_id=1, source_target_pairs={{0,4},{1,68},{2,132},{3,196},{4,5},{5,69},{6,133},{7,197},{8,12},{... | collective-permute-start | bytes 245768 | tf_op jit(solution)/shard_map/ppermute | solution.py:54
  116.7 11.2 %collective-permute-start.8 = (bf16[256,512]{1,0:T(8,128)(2,1)S(1)}, bf16[256,512]{1,0:T(8,128)(2,1)S(1)}, u32[]{:S(2)}, u32[]{:S(2)}) collective-permute-start(bf16[256,512]{1,0:T(8,128)(2,1)S(1)} %shard_map.102), channel_id=1, source_target_pairs={{0,0},{1,4},{2,64},{3,68},{4,1},{5,5},{6,65},{7,69},{8,8},{9,12},{... | collective-permute-start | bytes 786440 | tf_op jit(solution)/shard_map/ppermute | solution.py:54
  119.7 0.9 copy-start
  128.0 0.7 copy-start.12

commit v6 on v4

--- a/solution.py
+++ b/solution.py
@@ -87,7 +87,7 @@
     return jax.ShapeDtypeStruct(dims, dtype)
 
 
-def forward_body(lengths, q_ref, k_ref, v_ref, att_ref, prob_ref):
+def forward_body(place, q_ref, k_ref, v_ref, att_ref, prob_ref):
     rows = lax.broadcasted_iota(jnp.int32, (TOK, TOK), 0)
     cols = lax.broadcasted_iota(jnp.int32, (TOK, TOK), 1)
     row_at = lax.broadcasted_iota(jnp.int32, (TOK, 1), 0)
@@ -96,7 +96,7 @@
     col_seg = jnp.zeros((1, TOK), jnp.int32)
     end = jnp.int32(0)
     for i in range(8):
-        end = end + lengths[i]
+        end = end + place[3 + i]
         row_seg = row_seg + (row_at >= end).astype(jnp.int32)
         col_seg = col_seg + (col_at >= end).astype(jnp.int32)
     allowed = (row_seg == col_seg) & (rows >= cols)
@@ -189,6 +189,7 @@
     dp, y = lax.axis_index("dp"), lax.axis_index("mp")
     x = dp // (NZ * NC)
     place = jnp.stack([2 * low_of(x) + dp % NC, y, x // 2]).astype(jnp.int32)
+    place = jnp.concatenate([place, doc_lengths[0]])
     across_grad = send(out_grad, ACROSS)
     cols = [out_grad, send(out_grad, SWAP), across_grad, send(across_grad, SWAP)]
 
@@ -202,7 +203,7 @@
         flops=4 * 4 * TOK * TOK * HEAD,
         moved=2 << 20,
         limit=63,
-    )(doc_lengths[0], query_rows, key_rows, value_matrix)
+    )(place, query_rows, key_rows, value_matrix)
     heads = send(attended, TURN)
     heads = [heads] + [send(heads, pairs) for pairs in ALONG_Y]
 
@@ -222,6 +223,7 @@
         scratch=(pltpu.VMEM((4, TOK, COLS), BF),),
         flops=big,
         moved=6 << 20,
+        limit=63,
     )(place, *cols, *blocks)
 
     pair, attended_two = call(
@@ -250,6 +252,7 @@
         (shape(TOK, GROUP), shape(TOK, HEAD), shape(TOK, HEAD)),
         flops=5 * 4 * 2 * TOK * TOK * HEAD,
         moved=3 << 20,
+        limit=63,
     )(place, upstream, query_rows, key_rows, value_matrix, prob)
 
     pieces = call(sum_z_body, (shape(SHARD, GROUP),) * 2, moved=2 << 20)(place, grad_rows)

time: 122 us -> 133 us (1.090)
  starting transfers between devices: 47.7 us -> 54.6 us
  local copies, waits for them, and re-layouts: 2.16 us -> 9.02 us
  waiting for transfers between devices: 47.3 us -> 41.1 us
  Pallas kernels: 20.8 us -> 22.7 us
  other arithmetic: 2.84 us -> 4.25 us
    ppermute x17, starting transfers between devices: 30.8 us -> 39 us  [send(): return lax.ppermute(value, AXES, pairs)]
    all_to_all x2, waiting for transfers between devices: 8.28 us -> 0.74 us  [exchange(): lax.all_to_all(blocks, 'dp', 0, 0, axis_index_groups=groups, tiled=True)]
    unnamed x26 -> x40, local copies, waits for them, and re-layouts: 1.27 us -> 8.12 us
    pallas_call x9, Pallas kernels: 20.8 us -> 22.7 us  [run(): pl.pallas_call(body, out_shape=outs, grid=(1,), in_specs=[pl.BlockSpec(me...]
    all_to_all x2, starting transfers between devices: 16.9 us -> 15.6 us  [exchange(): lax.all_to_all(blocks, 'dp', 0, 0, axis_index_groups=groups, tiled=True)]
  transfers between devices with their start and end apart: 19 -> 19, of which waited for: 9 -> 7; matrix products, arithmetic and copies ran while one was open for 1% -> 2% of each run, Pallas kernels for 17% -> 17%
where the time goes in v6:
time: 133 us
  starting transfers between devices  54.6 us (41%)
  waiting for transfers between devices  41.1 us (31%)
  Pallas kernels  22.7 us (17%)
  local copies, waits for them, and re-layouts  9.02 us (7%)
  other arithmetic  4.25 us (3%)
    ppermute x17, waiting for transfers between devices, send(): return lax.ppermute(value, AXES, pairs)  40.3 us
    ppermute x17, starting transfers between devices, send(): return lax.ppermute(value, AXES, pairs)  39 us
    pallas_call x9, Pallas kernels, run(): pl.pallas_call(body, out_shape=outs, grid=(1,), in_specs=[pl.BlockSpec(me...  22.7 us
    all_to_all x2, starting transfers between devices, exchange(): lax.all_to_all(blocks, 'dp', 0, 0, axis_index_groups=groups, tiled=True)  15.6 us
    unnamed x40, local copies, waits for them, and re-layouts  8.12 us
  transfers between devices with their start and end apart: 19, of which 7 were waited for; matrix products, arithmetic and copies ran while one was open for 2% of the time, Pallas kernels for 17%

profile of v6, /device:TPU:4, one launch (start us, length us, event | category | flops | bytes accessed | tf_op | source)
XLA Modules:
  0.0 132.5 jit_solution(6925711811296663310)
XLA Ops:
  0.6 0.0 copy-start.4
  0.7 1.3 collective-permute-start.5
  1.9 5.3 %collective-permute-start.7 = (bf16[80,512]{1,0:T(8,128)(2,1)}, bf16[80,512]{1,0:T(8,128)(2,1)S(1)}, u32[]{:S(2)}, u32[]{:S(2)}) collective-permute-start(bf16[80,512]{1,0:T(8,128)(2,1)} %bitcast.9), channel_id=1, source_target_pairs={{0,0},{1,4},{2,64},{3,68},{4,192},{5,196},{6,128},{7,132},{8,8},{9... | collective-permute-start | bytes 245768 | tf_op jit(solution)/shard_map/ppermute | solution.py:54
  7.3 13.4 %collective-permute-done.7 = bf16[80,512]{1,0:T(8,128)(2,1)S(1)} collective-permute-done((bf16[80,512]{1,0:T(8,128)(2,1)}, bf16[80,512]{1,0:T(8,128)(2,1)S(1)}, u32[]{:S(2)}, u32[]{:S(2)}) %collective-permute-start.7) | collective-permute-done | bytes 81952 | tf_op jit(solution)/shard_map/ppermute | solution.py:54
  20.6 0.9 broadcast_in_dim.2
  21.5 8.5 %all-to-all-start = ((bf16[8,80,512]{2,1,0:T(8,128)(2,1)}), bf16[8,80,512]{2,1,0:T(8,128)(2,1)}, u32[]{:S(2)}, u32[]{:S(2)}) async-start(bf16[8,80,512]{2,1,0:T(8,128)(2,1)} %broadcast_in_dim.2), calls=%async_computation | async-start | bytes 1310720 | tf_op jit(solution)/shard_map/all_to_all | solution.py:58
  30.0 0.1 collective-permute-start.4
  30.2 0.0 collective-permute-done.5.o2
  30.2 0.4 collective-permute-start.6
  30.6 0.6 pad_add_fusion.place._
  31.2 3.1 %shard_map.101 = (bf16[256,512]{1,0:T(8,128)(2,1)}, f32[4,256,256]{2,1,0:T(8,128)}) custom-call(s32[11]{0:T(128)} %pad_add_fusion.place._, bf16[256,512]{1,0:T(8,128)(2,1)} %q_ref.3, bf16[256,128]{1,0:T(8,128)(2,1)} %k_ref.3, bf16[256,128]{1,0:T(8,128)(2,1)} %v_ref.3), custom_call_target="tpu_custom_call" | custom-call | flops 134217728 | bytes 2097152 | tf_op jit(solution)/shard_map/pallas_call | solution.py:72
  34.2 2.9 %collective-permute-start = (bf16[256,512]{1,0:T(8,128)(2,1)}, bf16[256,512]{1,0:T(8,128)(2,1)S(1)}, u32[]{:S(2)}, u32[]{:S(2)}) collective-permute-start(bf16[256,512]{1,0:T(8,128)(2,1)} %get-tuple-element.19), channel_id=1, source_target_pairs={{0,0},{1,4},{2,64},{3,68},{4,1},{5,5},{6,65},{7,69},{8,8},{9,12},{... | collective-permute-start | bytes 786440 | tf_op jit(solution)/shard_map/ppermute | solution.py:54
  37.1 10.2 %collective-permute-done.r0 = bf16[256,512]{1,0:T(8,128)(2,1)S(1)} collective-permute-done((bf16[256,512]{1,0:T(8,128)(2,1)}, bf16[256,512]{1,0:T(8,128)(2,1)S(1)}, u32[]{:S(2)}, u32[]{:S(2)}) %collective-permute-start) | collective-permute-done | bytes 262176 | tf_op jit(solution)/shard_map/ppermute | solution.py:54
  47.3 0.0 collective-permute-start.3
  47.3 0.0 collective-permute-start.2
  47.3 2.0 %collective-permute-start.1 = (bf16[256,512]{1,0:T(8,128)(2,1)S(1)}, bf16[256,512]{1,0:T(8,128)(2,1)S(1)}, u32[]{:S(2)}, u32[]{:S(2)}) collective-permute-start(bf16[256,512]{1,0:T(8,128)(2,1)S(1)} %collective-permute-done.r0), channel_id=1, source_target_pairs={{0,1},{1,2},{2,3},{3,0},{4,5},{5,6},{6,7},{7,4},{8,9},{9,10},{10,1... | collective-permute-start | bytes 786440 | tf_op jit(solution)/shard_map/ppermute | solution.py:54
  49.3 7.1 %collective-permute-done.3.r3 = bf16[256,512]{1,0:T(8,128)(2,1)S(1)} collective-permute-done((bf16[256,512]{1,0:T(8,128)(2,1)S(1)}, bf16[256,512]{1,0:T(8,128)(2,1)S(1)}, u32[]{:S(2)}, u32[]{:S(2)}) %collective-permute-start.3) | collective-permute-done | bytes 262176 | tf_op jit(solution)/shard_map/ppermute | solution.py:54
  56.5 0.0 all-to-all-done.w0
  56.5 2.5 %collective-permute-start.8 = (bf16[8,80,512]{2,1,0:T(8,128)(2,1)}, bf16[8,80,512]{2,1,0:T(8,128)(2,1)}, u32[]{:S(2)}, u32[]{:S(2)}) collective-permute-start(bf16[8,80,512]{2,1,0:T(8,128)(2,1)} %all-to-all-done.w0), channel_id=1, source_target_pairs={{0,192},{1,193},{2,194},{3,195},{4,196},{5,197},{6,198},{7,199},{8... | collective-permute-start | bytes 1966088 | tf_op jit(solution)/shard_map/ppermute | solution.py:54
  59.0 0.0 collective-permute-done.2.r2
  59.0 3.8 %collective-permute-done.1.r1 = bf16[256,512]{1,0:T(8,128)(2,1)S(1)} collective-permute-done((bf16[256,512]{1,0:T(8,128)(2,1)S(1)}, bf16[256,512]{1,0:T(8,128)(2,1)S(1)}, u32[]{:S(2)}, u32[]{:S(2)}) %collective-permute-start.1) | collective-permute-done | bytes 262176 | tf_op jit(solution)/shard_map/ppermute | solution.py:54
  62.8 0.0 collective-permute-done.4.o1
  62.8 0.0 collective-permute-done.6.o3
  62.8 0.6 copy-done.12
  63.4 4.2 %shard_map.108 = bf16[1280,512]{1,0:T(8,128)(2,1)} custom-call(s32[11]{0:T(128)S(1)} %copy-done.12, bf16[256,1280]{1,0:T(8,128)(2,1)S(1)} %copy-done.4, bf16[256,1280]{1,0:T(8,128)(2,1)} %collective-permute-done.4.o1, bf16[256,1280]{1,0:T(8,128)(2,1)} %collective-permute-done.5.o2, bf16[256,1280]{1,0:T(8,128)(2,1)} %collective-permute-done.6.o3, ...), custom_call_target="tpu_custom_call" | custom-call | flops 1342177280 | bytes 6291456 | tf_op jit(solution)/shard_map/pallas_call | solution.py:72
  67.6 0.0 copy-done.10
  67.6 7.1 %all-to-all-start.1 = ((bf16[8,160,512]{2,1,0:T(8,128)(2,1)}), bf16[8,160,512]{2,1,0:T(8,128)(2,1)}, u32[]{:S(2)}, u32[]{:S(2)}) async-start(bf16[8,160,512]{2,1,0:T(8,128)(2,1)} %bitcast.5), calls=%async_computation.1 | async-start | bytes 2621440 | tf_op jit(solution)/shard_map/all_to_all | solution.py:58
  74.7 0.0 collective-permute-done.8.w1
  74.7 5.0 %shard_map.102 = (bf16[256,512]{1,0:T(8,128)(2,1)}, bf16[256,512]{1,0:T(8,128)(2,1)}, bf16[256,512]{1,0:T(8,128)(2,1)}, bf16[256,512]{1,0:T(8,128)(2,1)}, bf16[1280,512]{1,0:T(8,128)(2,1)}) custom-call(s32[11]{0:T(128)} %pad_add_fusion.place._, bf16[256,1280]{1,0:T(8,128)(2,1)} %o0.3, bf16[256,1280]{1,0:T(8,128)(2,1)} %collective-permute-done.4.o1, ...), custom_call_target="tpu_custom_call" | custom-call | flops 1342177280 | bytes 6291456 | tf_op jit(solution)/shard_map/pallas_call | solution.py:72
  79.7 0.0 copy-done.13
  79.7 1.3 copy-done
  81.0 0.9 copy-done.6
  82.0 0.9 copy-done.8
  82.9 0.9 copy-done.11
  83.9 1.5 %shard_map.103 = (bf16[2,256,1280]{2,1,0:T(8,128)(2,1)S(1)}, bf16[2,256,512]{2,1,0:T(8,128)(2,1)S(1)}) custom-call(s32[11]{0:T(128)S(1)} %copy-done.13, bf16[256,512]{1,0:T(8,128)(2,1)S(1)} %collective-permute-done.r0, bf16[256,512]{1,0:T(8,128)(2,1)S(1)} %copy-done.11, bf16[256,512]{1,0:T(8,128)(2,1)S(1)} %copy-done.8, bf16[256,512]{1,0:T(8,128)(2,1)S(1)} %copy-done.6, ...), custom_call_target="tpu_custom_call" | custom-call | flops 671088640 | bytes 4194304 | tf_op jit(solution)/shard_map/pallas_call | solution.py:72
  85.4 0.1 collective-permute-start.9
  85.5 0.1 collective-permute-start.11
  85.6 2.6 %collective-permute-start.12 = (bf16[256,512]{1,0:T(8,128)(2,1)S(1)}, bf16[256,512]{1,0:T(8,128)(2,1)S(1)}, u32[]{:S(2)}, u32[]{:S(2)}) collective-permute-start(bf16[256,512]{1,0:T(8,128)(2,1)S(1)} %copy-done.18), channel_id=1, source_target_pairs={{0,2},{1,3},{2,0},{3,1},{4,6},{5,7},{6,4},{7,5},{8,10},{9,11},{10,... | collective-permute-start | bytes 786440 | tf_op jit(solution)/shard_map/ppermute | solution.py:54
  88.3 0.7 collective-permute-start.13
  88.9 0.0 collective-permute-done.9.pair
  88.9 1.9 %shard_map.105 = bf16[256,1280]{1,0:T(8,128)(2,1)} custom-call(s32[11]{0:T(128)S(1)} %copy-done.13, bf16[2,256,512]{2,1,0:T(8,128)(2,1)S(1)} %get-tuple-element.21.att, bf16[1280,512]{1,0:T(8,128)(2,1)S(1)} %copy-done, bf16[2,256,1280]{2,1,0:T(8,128)(2,1)S(1)} %collective-permute-done.9.pair), custom_call_target="tpu_custom_call" | custom-call | flops 335544320 | bytes 3145728 | tf_op jit(solution)/shard_map/pallas_call | solution.py:72
  90.9 0.0 copy-done.2
  90.9 5.0 %collective-permute-start.10 = (bf16[256,1280]{1,0:T(8,128)(2,1)}, bf16[256,1280]{1,0:T(8,128)(2,1)}, u32[]{:S(2)}, u32[]{:S(2)}) collective-permute-start(bf16[256,1280]{1,0:T(8,128)(2,1)} %shard_map.105), channel_id=1, source_target_pairs={{0,64},{1,65},{2,66},{3,67},{4,68},{5,69},{6,70},{7,71},{8,72},{9,... | collective-permute-start | bytes 1966088 | tf_op jit(solution)/shard_map/ppermute | solution.py:54
  95.9 5.2 %collective-permute-done.11.a1 = bf16[256,512]{1,0:T(8,128)(2,1)S(1)} collective-permute-done((bf16[256,512]{1,0:T(8,128)(2,1)S(1)}, bf16[256,512]{1,0:T(8,128)(2,1)S(1)}, u32[]{:S(2)}, u32[]{:S(2)}) %collective-permute-start.11) | collective-permute-done | bytes 262176 | tf_op jit(solution)/shard_map/ppermute | solution.py:54
  101.0 0.0 collective-permute-done.12.a2
  101.1 0.6 collective-permute-done.13.a3
  101.7 0.7 shard_map.106
  102.4 0.0 copy-start.14
  102.4 6.2 %collective-permute-start.14 = (bf16[256,512]{1,0:T(8,128)(2,1)S(1)}, bf16[256,512]{1,0:T(8,128)(2,1)S(1)}, u32[]{:S(2)}, u32[]{:S(2)}) collective-permute-start(bf16[256,512]{1,0:T(8,128)(2,1)S(1)} %shard_map.106), channel_id=1, source_target_pairs={{0,0},{1,4},{2,64},{3,68},{4,1},{5,5},{6,65},{7,69},{8,8},{9,12},{... | collective-permute-start | bytes 786440 | tf_op jit(solution)/shard_map/ppermute | solution.py:54
  108.6 0.7 all-to-all-done.1.blocks
  109.3 1.5 %shard_map.109 = (bf16[80,512]{1,0:T(8,128)(2,1)S(1)}, bf16[80,512]{1,0:T(8,128)(2,1)S(1)}) custom-call(s32[11]{0:T(128)S(1)} %copy-done.13, bf16[8,160,512]{2,1,0:T(8,128)(2,1)} %all-to-all-done.1.blocks), custom_call_target="tpu_custom_call" | custom-call | bytes 2097152 | tf_op jit(solution)/shard_map/pallas_call | solution.py:72
  110.8 1.9 %collective-permute-start.15 = (bf16[80,512]{1,0:T(8,128)(2,1)S(1)}, bf16[80,512]{1,0:T(8,128)(2,1)}, u32[]{:S(2)}, u32[]{:S(2)}) collective-permute-start(bf16[80,512]{1,0:T(8,128)(2,1)S(1)} %get-tuple-element.31), channel_id=1, source_target_pairs={{0,0},{1,64},{2,128},{3,192},{4,1},{5,65},{6,129},{7,193},{8,8},{9... | collective-permute-start | bytes 245768 | tf_op jit(solution)/shard_map/ppermute | solution.py:54
  112.8 7.8 %collective-permute-start.16 = (bf16[80,512]{1,0:T(8,128)(2,1)S(1)}, bf16[80,512]{1,0:T(8,128)(2,1)}, u32[]{:S(2)}, u32[]{:S(2)}) collective-permute-start(bf16[80,512]{1,0:T(8,128)(2,1)S(1)} %get-tuple-element.32), channel_id=1, source_target_pairs={{0,4},{1,68},{2,132},{3,196},{4,5},{5,69},{6,133},{7,197},{8,12},{... | collective-permute-start | bytes 245768 | tf_op jit(solution)/shard_map/ppermute | solution.py:54
  120.6 0.0 collective-permute-done.14.up_ref
  120.6 0.7 copy-done.15
  121.3 3.7 %shard_map.107 = (bf16[256,512]{1,0:T(8,128)(2,1)}, bf16[256,128]{1,0:T(8,128)(2,1)}, bf16[256,128]{1,0:T(8,128)(2,1)}) custom-call(s32[11]{0:T(128)} %pad_add_fusion.place._, bf16[256,512]{1,0:T(8,128)(2,1)} %copy-done.15, bf16[256,512]{1,0:T(8,128)(2,1)} %q_ref.3, bf16[256,128]{1,0:T(8,128)(2,1)} %k_ref.3, bf16[256,128]{1,0:T(8,128)(2,1)} %v_ref.3, ...), custom_call_target="tpu_custom_call" | custom-call | flops 335544320 | bytes 3145728 | tf_op jit(solution)/shard_map/pallas_call | solution.py:72
  125.1 1.3 copy-done.1
  126.4 1.3 copy-done.3
  127.7 1.1 shard_map.104
  128.8 0.0 collective-permute-done.15
  128.8 0.0 collective-permute-done.16
  128.8 1.6 %add_bitcast_fusion = f32[512,80]{0,1:T(8,128)} fusion(bf16[80,512]{1,0:T(8,128)(2,1)} %collective-permute-done.16, bf16[80,512]{1,0:T(8,128)(2,1)} %collective-permute-done.15), kind=kLoop, calls=%fused_computation.1 | loop fusion | flops 122880 | bytes 327680 | tf_op jit(solution)/shard_map/transpose | solution.py:261
  130.5 0.0 collective-permute-done.10
  130.5 2.1 %add_convert_fusion = bf16[256,1280]{1,0:T(8,128)(2,1)} fusion(bf16[256,1280]{1,0:T(8,128)(2,1)} %collective-permute-done.10, bf16[256,1280]{1,0:T(8,128)(2,1)S(1)} %shard_map.104), kind=kLoop, calls=%fused_computation | loop fusion | flops 1310720 | bytes 1966080 | tf_op jit(solution)/shard_map/convert_element_type | solution.py:244
  (27 shorter events, 0.0 us)
Async XLA Ops:
  0.6 29.4 %copy-start.4 = (bf16[256,1280]{1,0:T(8,128)(2,1)S(1)}, bf16[256,1280]{1,0:T(8,128)(2,1)}, u32[]{:S(2)}) copy-start(bf16[256,1280]{1,0:T(8,128)(2,1)} %o0.3) | copy-start | bytes 1966084
  0.6 30.0 %copy-start.16 = (s32[1,8]{1,0:T(1,128)S(1)}, s32[1,8]{1,0:T(1,128)}, u32[]{:S(2)}) copy-start(s32[1,8]{1,0:T(1,128)} %param.11) | copy-start | bytes 100
  0.7 29.5 %collective-permute-start.5 = (bf16[256,1280]{1,0:T(8,128)(2,1)}, bf16[256,1280]{1,0:T(8,128)(2,1)}, u32[]{:S(2)}, u32[]{:S(2)}) collective-permute-start(bf16[256,1280]{1,0:T(8,128)(2,1)} %o0.3), channel_id=1, source_target_pairs={{0,64},{1,65},{2,66},{3,67},{4,68},{5,69},{6,70},{7,71},{8,72},{9,... | collective-permute-start | bytes 1966088 | tf_op jit(solution)/shard_map/ppermute | solution.py:54
  1.9 18.7 %collective-permute-start.7 = (bf16[80,512]{1,0:T(8,128)(2,1)}, bf16[80,512]{1,0:T(8,128)(2,1)S(1)}, u32[]{:S(2)}, u32[]{:S(2)}) collective-permute-start(bf16[80,512]{1,0:T(8,128)(2,1)} %bitcast.9), channel_id=1, source_target_pairs={{0,0},{1,4},{2,64},{3,68},{4,192},{5,196},{6,128},{7,132},{8,8},{9... | collective-permute-start | bytes 245768 | tf_op jit(solution)/shard_map/ppermute | solution.py:54
  21.5 34.9 %all-to-all-start = ((bf16[8,80,512]{2,1,0:T(8,128)(2,1)}), bf16[8,80,512]{2,1,0:T(8,128)(2,1)}, u32[]{:S(2)}, u32[]{:S(2)}) async-start(bf16[8,80,512]{2,1,0:T(8,128)(2,1)} %broadcast_in_dim.2), calls=%async_computation | async-start | bytes 1310720 | tf_op jit(solution)/shard_map/all_to_all | solution.py:58
  30.0 32.8 %collective-permute-start.4 = (bf16[256,1280]{1,0:T(8,128)(2,1)S(1)}, bf16[256,1280]{1,0:T(8,128)(2,1)}, u32[]{:S(2)}, u32[]{:S(2)}) collective-permute-start(bf16[256,1280]{1,0:T(8,128)(2,1)S(1)} %copy-done.4), channel_id=1, source_target_pairs={{0,4},{1,5},{2,6},{3,7},{4,0},{5,1},{6,2},{7,3},{8,12},{9,13},{10,... | collective-permute-start | bytes 1966088 | tf_op jit(solution)/shard_map/ppermute | solution.py:54
  30.2 32.6 %collective-permute-start.6 = (bf16[256,1280]{1,0:T(8,128)(2,1)}, bf16[256,1280]{1,0:T(8,128)(2,1)}, u32[]{:S(2)}, u32[]{:S(2)}) collective-permute-start(bf16[256,1280]{1,0:T(8,128)(2,1)} %collective-permute-done.5.o2), channel_id=1, source_target_pairs={{0,4},{1,5},{2,6},{3,7},{4,0},{5,1},{6,2},{7,3},{8,12},{9,13},{10,... | collective-permute-start | bytes 1966088 | tf_op jit(solution)/shard_map/ppermute | solution.py:54
  34.2 13.1 %collective-permute-start = (bf16[256,512]{1,0:T(8,128)(2,1)}, bf16[256,512]{1,0:T(8,128)(2,1)S(1)}, u32[]{:S(2)}, u32[]{:S(2)}) collective-permute-start(bf16[256,512]{1,0:T(8,128)(2,1)} %get-tuple-element.19), channel_id=1, source_target_pairs={{0,0},{1,4},{2,64},{3,68},{4,1},{5,5},{6,65},{7,69},{8,8},{9,12},{... | collective-permute-start | bytes 786440 | tf_op jit(solution)/shard_map/ppermute | solution.py:54
  47.3 9.2 %collective-permute-start.3 = (bf16[256,512]{1,0:T(8,128)(2,1)S(1)}, bf16[256,512]{1,0:T(8,128)(2,1)S(1)}, u32[]{:S(2)}, u32[]{:S(2)}) collective-permute-start(bf16[256,512]{1,0:T(8,128)(2,1)S(1)} %collective-permute-done.r0), channel_id=1, source_target_pairs={{0,3},{1,0},{2,1},{3,2},{4,7},{5,4},{6,5},{7,6},{8,11},{9,8},{10,9... | collective-permute-start | bytes 786440 | tf_op jit(solution)/shard_map/ppermute | solution.py:54
  47.3 11.7 %collective-permute-start.2 = (bf16[256,512]{1,0:T(8,128)(2,1)S(1)}, bf16[256,512]{1,0:T(8,128)(2,1)S(1)}, u32[]{:S(2)}, u32[]{:S(2)}) collective-permute-start(bf16[256,512]{1,0:T(8,128)(2,1)S(1)} %collective-permute-done.r0), channel_id=1, source_target_pairs={{0,2},{1,3},{2,0},{3,1},{4,6},{5,7},{6,4},{7,5},{8,10},{9,11},{10,... | collective-permute-start | bytes 786440 | tf_op jit(solution)/shard_map/ppermute | solution.py:54
  47.3 15.5 %collective-permute-start.1 = (bf16[256,512]{1,0:T(8,128)(2,1)S(1)}, bf16[256,512]{1,0:T(8,128)(2,1)S(1)}, u32[]{:S(2)}, u32[]{:S(2)}) collective-permute-start(bf16[256,512]{1,0:T(8,128)(2,1)S(1)} %collective-permute-done.r0), channel_id=1, source_target_pairs={{0,1},{1,2},{2,3},{3,0},{4,5},{5,6},{6,7},{7,4},{8,9},{9,10},{10,1... | collective-permute-start | bytes 786440 | tf_op jit(solution)/shard_map/ppermute | solution.py:54
  56.5 11.1 %copy-start.5 = (bf16[256,512]{1,0:T(8,128)(2,1)}, bf16[256,512]{1,0:T(8,128)(2,1)S(1)}, u32[]{:S(2)}) copy-start(bf16[256,512]{1,0:T(8,128)(2,1)S(1)} %collective-permute-done.3.r3) | copy-start | bytes 786436
  56.5 18.2 %collective-permute-start.8 = (bf16[8,80,512]{2,1,0:T(8,128)(2,1)}, bf16[8,80,512]{2,1,0:T(8,128)(2,1)}, u32[]{:S(2)}, u32[]{:S(2)}) collective-permute-start(bf16[8,80,512]{2,1,0:T(8,128)(2,1)} %all-to-all-done.w0), channel_id=1, source_target_pairs={{0,192},{1,193},{2,194},{3,195},{4,196},{5,197},{6,198},{7,199},{8... | collective-permute-start | bytes 1966088 | tf_op jit(solution)/shard_map/ppermute | solution.py:54
  59.0 8.6 %copy-start.7 = (bf16[256,512]{1,0:T(8,128)(2,1)}, bf16[256,512]{1,0:T(8,128)(2,1)S(1)}, u32[]{:S(2)}) copy-start(bf16[256,512]{1,0:T(8,128)(2,1)S(1)} %collective-permute-done.2.r2) | copy-start | bytes 786436
  62.8 4.8 %copy-start.10 = (bf16[256,512]{1,0:T(8,128)(2,1)}, bf16[256,512]{1,0:T(8,128)(2,1)S(1)}, u32[]{:S(2)}) copy-start(bf16[256,512]{1,0:T(8,128)(2,1)S(1)} %collective-permute-done.1.r1) | copy-start | bytes 786436
  62.8 0.6 copy-start.12
  67.6 41.8 %all-to-all-start.1 = ((bf16[8,160,512]{2,1,0:T(8,128)(2,1)}), bf16[8,160,512]{2,1,0:T(8,128)(2,1)}, u32[]{:S(2)}, u32[]{:S(2)}) async-start(bf16[8,160,512]{2,1,0:T(8,128)(2,1)} %bitcast.5), calls=%async_computation.1 | async-start | bytes 2621440 | tf_op jit(solution)/shard_map/all_to_all | solution.py:58
  74.7 5.0 %copy-start.13 = (s32[11]{0:T(128)S(1)}, s32[11]{0:T(128)}, u32[]{:S(2)}) copy-start(s32[11]{0:T(128)} %pad_add_fusion.place._) | copy-start | bytes 136
  79.7 1.3 copy-start
  81.0 0.9 copy-start.6
  82.0 0.9 copy-start.8
  82.9 0.9 copy-start.11
  83.9 1.6 %copy-start.19 = (bf16[256,512]{1,0:T(8,128)(2,1)S(1)}, bf16[256,512]{1,0:T(8,128)(2,1)}, u32[]{:S(2)}) copy-start(bf16[256,512]{1,0:T(8,128)(2,1)} %get-tuple-element.24) | copy-start | bytes 786436
  83.9 1.7 %copy-start.18 = (bf16[256,512]{1,0:T(8,128)(2,1)S(1)}, bf16[256,512]{1,0:T(8,128)(2,1)}, u32[]{:S(2)}) copy-start(bf16[256,512]{1,0:T(8,128)(2,1)} %get-tuple-element.25) | copy-start | bytes 786436
  83.9 4.4 %copy-start.17 = (bf16[256,512]{1,0:T(8,128)(2,1)S(1)}, bf16[256,512]{1,0:T(8,128)(2,1)}, u32[]{:S(2)}) copy-start(bf16[256,512]{1,0:T(8,128)(2,1)} %get-tuple-element.26) | copy-start | bytes 786436
  85.4 3.5 %collective-permute-start.9 = (bf16[2,256,1280]{2,1,0:T(8,128)(2,1)S(1)}, bf16[2,256,1280]{2,1,0:T(8,128)(2,1)S(1)}, u32[]{:S(2)}, u32[]{:S(2)}) collective-permute-start(bf16[2,256,1280]{2,1,0:T(8,128)(2,1)S(1)} %get-tuple-element.22), channel_id=1, source_target_pairs={{0,4},{1,5},{2,6},{3,7},{4,0},{5,1},{6,2},{7,3},{8,12},{9,13},{10,... | collective-permute-start | bytes 3932168 | tf_op jit(solution)/shard_map/ppermute | solution.py:54
  85.5 15.5 %collective-permute-start.11 = (bf16[256,512]{1,0:T(8,128)(2,1)S(1)}, bf16[256,512]{1,0:T(8,128)(2,1)S(1)}, u32[]{:S(2)}, u32[]{:S(2)}) collective-permute-start(bf16[256,512]{1,0:T(8,128)(2,1)S(1)} %copy-done.19), channel_id=1, source_target_pairs={{0,1},{1,2},{2,3},{3,0},{4,5},{5,6},{6,7},{7,4},{8,9},{9,10},{10,1... | collective-permute-start | bytes 786440 | tf_op jit(solution)/shard_map/ppermute | solution.py:54
  85.6 15.4 %collective-permute-start.12 = (bf16[256,512]{1,0:T(8,128)(2,1)S(1)}, bf16[256,512]{1,0:T(8,128)(2,1)S(1)}, u32[]{:S(2)}, u32[]{:S(2)}) collective-permute-start(bf16[256,512]{1,0:T(8,128)(2,1)S(1)} %copy-done.18), channel_id=1, source_target_pairs={{0,2},{1,3},{2,0},{3,1},{4,6},{5,7},{6,4},{7,5},{8,10},{9,11},{10,... | collective-permute-start | bytes 786440 | tf_op jit(solution)/shard_map/ppermute | solution.py:54
  88.3 13.4 %collective-permute-start.13 = (bf16[256,512]{1,0:T(8,128)(2,1)S(1)}, bf16[256,512]{1,0:T(8,128)(2,1)S(1)}, u32[]{:S(2)}, u32[]{:S(2)}) collective-permute-start(bf16[256,512]{1,0:T(8,128)(2,1)S(1)} %copy-done.17), channel_id=1, source_target_pairs={{0,3},{1,0},{2,1},{3,2},{4,7},{5,4},{6,5},{7,6},{8,11},{9,8},{10,9... | collective-permute-start | bytes 786440 | tf_op jit(solution)/shard_map/ppermute | solution.py:54
  88.9 2.0 %copy-start.2 = (bf16[2,256,1280]{2,1,0:T(8,128)(2,1)}, bf16[2,256,1280]{2,1,0:T(8,128)(2,1)S(1)}, u32[]{:S(2)}) copy-start(bf16[2,256,1280]{2,1,0:T(8,128)(2,1)S(1)} %collective-permute-done.9.pair) | copy-start | bytes 3932164
  88.9 12.7 %copy-start.9 = (bf16[256,512]{1,0:T(8,128)(2,1)S(1)}, bf16[256,512]{1,0:T(8,128)(2,1)}, u32[]{:S(2)}) copy-start(bf16[256,512]{1,0:T(8,128)(2,1)} %get-tuple-element.23.a0) | copy-start | bytes 786436
  90.9 39.6 %collective-permute-start.10 = (bf16[256,1280]{1,0:T(8,128)(2,1)}, bf16[256,1280]{1,0:T(8,128)(2,1)}, u32[]{:S(2)}, u32[]{:S(2)}) collective-permute-start(bf16[256,1280]{1,0:T(8,128)(2,1)} %shard_map.105), channel_id=1, source_target_pairs={{0,64},{1,65},{2,66},{3,67},{4,68},{5,69},{6,70},{7,71},{8,72},{9,... | collective-permute-start | bytes 1966088 | tf_op jit(solution)/shard_map/ppermute | solution.py:54
  102.4 22.7 %copy-start.14 = (s32[11]{0:T(128)S(1)}, s32[11]{0:T(128)}, u32[]{:S(2)}) copy-start(s32[11]{0:T(128)} %pad_add_fusion.place._) | copy-start | bytes 136
  102.4 18.2 %collective-permute-start.14 = (bf16[256,512]{1,0:T(8,128)(2,1)S(1)}, bf16[256,512]{1,0:T(8,128)(2,1)S(1)}, u32[]{:S(2)}, u32[]{:S(2)}) collective-permute-start(bf16[256,512]{1,0:T(8,128)(2,1)S(1)} %shard_map.106), channel_id=1, source_target_pairs={{0,0},{1,4},{2,64},{3,68},{4,1},{5,5},{6,65},{7,69},{8,8},{9,12},{... | collective-permute-start | bytes 786440 | tf_op jit(solution)/shard_map/ppermute | solution.py:54
  110.8 18.0 %collective-permute-start.15 = (bf16[80,512]{1,0:T(8,128)(2,1)S(1)}, bf16[80,512]{1,0:T(8,128)(2,1)}, u32[]{:S(2)}, u32[]{:S(2)}) collective-permute-start(bf16[80,512]{1,0:T(8,128)(2,1)S(1)} %get-tuple-element.31), channel_id=1, source_target_pairs={{0,0},{1,64},{2,128},{3,192},{4,1},{5,65},{6,129},{7,193},{8,8},{9... | collective-permute-start | bytes 245768 | tf_op jit(solution)/shard_map/ppermute | solution.py:54
  112.8 16.1 %collective-permute-start.16 = (bf16[80,512]{1,0:T(8,128)(2,1)S(1)}, bf16[80,512]{1,0:T(8,128)(2,1)}, u32[]{:S(2)}, u32[]{:S(2)}) collective-permute-start(bf16[80,512]{1,0:T(8,128)(2,1)S(1)} %get-tuple-element.32), channel_id=1, source_target_pairs={{0,4},{1,68},{2,132},{3,196},{4,5},{5,69},{6,133},{7,197},{8,12},{... | collective-permute-start | bytes 245768 | tf_op jit(solution)/shard_map/ppermute | solution.py:54
  120.6 0.7 copy-start.15
  125.1 1.3 copy-start.1
  126.4 1.3 copy-start.3

commit v7 on v5

--- a/solution.py
+++ b/solution.py
@@ -67,18 +67,25 @@
     return pl.BlockSpec(dims, lambda i: (0,) * len(dims), pipeline_mode=pl.Buffered(1))
 
 
-def call(body, outs, scratch=(), flops=0, moved=0, limit=12):
-    def run(scalars, *operands):
+def place():
+    dp = lax.axis_index("dp")
+    x = dp // (NZ * NC)
+    return 2 * low_of(x) + dp % NC, lax.axis_index("mp"), x // 2
+
+
+def call(body, outs, scratch=(), flops=0, moved=0, limit=12, scalars=0):
+    def run(*operands):
         return pl.pallas_call(
             body,
             out_shape=outs,
             grid=(1,),
-            in_specs=[pl.BlockSpec(memory_space=pltpu.SMEM)] + [whole(a) for a in operands],
+            in_specs=[pl.BlockSpec(memory_space=pltpu.SMEM)] * scalars
+            + [whole(a) for a in operands[scalars:]],
             out_specs=jax.tree.map(whole, outs),
             scratch_shapes=list(scratch),
             compiler_params=pltpu.CompilerParams(vmem_limit_bytes=limit << 20),
             cost_estimate=pl.CostEstimate(flops=flops, bytes_accessed=moved, transcendentals=0),
-        )(scalars, *operands)
+        )(*operands)
 
     return run
 
@@ -110,13 +117,13 @@
         att_ref[:, at] = dot(prob.astype(BF), v_ref[...], ((1,), (0,))).astype(BF)
 
 
-def sum_four_body(_, a0, a1, a2, a3, out):
+def sum_four_body(a0, a1, a2, a3, out):
     out[...] = (
         (a0[...].astype(F32) + a1[...].astype(F32)) + (a2[...].astype(F32) + a3[...].astype(F32))
     ).astype(BF)
 
 
-def backward_body(_, up_ref, q_ref, k_ref, v_ref, prob_ref, own, across, dq_ref, dk_ref, dv_ref, out):
+def backward_body(up_ref, q_ref, k_ref, v_ref, prob_ref, own, across, dq_ref, dk_ref, dv_ref, out):
     out[...] = (own[...].astype(F32) + across[...].astype(F32)).astype(BF)
     key_sum = jnp.zeros((TOK, HEAD), F32)
     value_sum = jnp.zeros((TOK, HEAD), F32)
@@ -134,8 +141,8 @@
     dv_ref[...] = value_sum.astype(BF)
 
 
-def weight_grad_body(place, o0, o1, o2, o3, r0, r1, r2, r3, grad_ref, att):
-    g, y = place[0], place[1]
+def weight_grad_body(o0, o1, o2, o3, r0, r1, r2, r3, grad_ref, att):
+    g, y, _ = place()
     for k, ref in enumerate((r0, r1, r2, r3)):
         att[jnp.bitwise_xor((y + 4 - k) % 4, g)] = ref[...]
     for i in range(COLS // 256):
@@ -146,8 +153,8 @@
         grad_ref[at, :] = total.astype(BF)
 
 
-def layer_pair_body(place, r0, r1, r2, r3, wt, pair_ref, att_ref, att):
-    g, y = place[0], place[1]
+def layer_pair_body(r0, r1, r2, r3, wt, pair_ref, att_ref, att):
+    g, y, _ = place()
     for k, ref in enumerate((r0, r1, r2, r3)):
         att[jnp.bitwise_xor((y + 4 - k) % 4, g)] = ref[...]
     for i in range(2):
@@ -155,16 +162,16 @@
         att_ref[i] = att[2 * i]
 
 
-def layer_across_body(_, att, wt, pair, out):
+def layer_across_body(att, wt, pair, out):
     out[...] = (dot(att[1], wt[...], ((1,), (1,))) + pair[1].astype(F32)).astype(BF)
 
 
-def layer_own_body(_, att, wt, pair, out):
+def layer_own_body(att, wt, pair, out):
     out[...] = (dot(att[0], wt[...], ((1,), (1,))) + pair[0].astype(F32)).astype(BF)
 
 
-def attn_grad_body(place, o0, o1, o2, o3, w0, w1, g0, g1, g2, g3, wt_ref, og):
-    g, y, high = place[0], place[1], place[2]
+def attn_grad_body(o0, o1, o2, o3, w0, w1, g0, g1, g2, g3, wt_ref, og):
+    g, y, high = place()
     for k, ref in enumerate((w0, w1)):
         c = (high + k) % 2
         for z in range(NZ):
@@ -176,8 +183,8 @@
         ref[...] = dot(og[at], wt_ref[...], ((1,), (0,))).astype(BF)
 
 
-def sum_z_body(place, blocks, o0, o1):
-    high = place[2]
+def sum_z_body(blocks, o0, o1):
+    high = place()[2]
     for k, ref in enumerate((o0, o1)):
         at = pl.ds(pl.multiple_of((high + k) % 2 * SHARD, 16), SHARD)
         total = blocks[0, at, :].astype(F32)
@@ -187,9 +194,6 @@
 
 
 def per_device(query_rows, key_rows, value_matrix, out_weight, out_grad, doc_lengths):
-    dp, y = lax.axis_index("dp"), lax.axis_index("mp")
-    x = dp // (NZ * NC)
-    place = jnp.stack([2 * low_of(x) + dp % NC, y, x // 2]).astype(jnp.int32)
     across_grad = send(out_grad, ACROSS)
     cols = [out_grad, send(out_grad, SWAP), across_grad, send(across_grad, SWAP)]
 
@@ -203,6 +207,7 @@
         flops=4 * 4 * TOK * TOK * HEAD,
         moved=2 << 20,
         limit=63,
+        scalars=1,
     )(doc_lengths[0], query_rows, key_rows, value_matrix)
     heads = send(attended, TURN)
     heads = [heads] + [send(heads, pairs) for pairs in ALONG_Y]
@@ -214,8 +219,7 @@
         scratch=(pltpu.VMEM((4, TOK, GROUP), BF),),
         flops=big,
         moved=6 << 20,
-        limit=63,
-    )(place, *cols, *heads)
+    )(*cols, *heads)
     grad_rows = exchange(grad_part.reshape(NZ, 2 * SHARD, GROUP), Z_GROUPS)
 
     *partials, wt_all = call(
@@ -224,7 +228,7 @@
         scratch=(pltpu.VMEM((4, TOK, COLS), BF),),
         flops=big,
         moved=6 << 20,
-    )(place, *cols, *blocks)
+    )(*cols, *blocks)
 
     pair, attended_two = call(
         layer_pair_body,
@@ -232,18 +236,18 @@
         scratch=(pltpu.VMEM((4, TOK, GROUP), BF),),
         flops=big // 2,
         moved=4 << 20,
-    )(place, *heads, wt_all)
+    )(*heads, wt_all)
     pair = send(pair, SWAP)
     across = call(
         layer_across_body, shape(TOK, COLS), flops=big // 4, moved=3 << 20
-    )(place, attended_two, wt_all, pair)
+    )(attended_two, wt_all, pair)
     across = send(across, ACROSS)
     own = call(layer_own_body, shape(TOK, COLS), flops=big // 4, moved=4 << 20)(
-        place, attended_two, wt_all, pair
+        attended_two, wt_all, pair
     )
 
     partials = [partials[0]] + [send(p, pairs) for p, pairs in zip(partials[1:], ALONG_Y)]
-    upstream = call(sum_four_body, shape(TOK, GROUP), moved=1 << 20)(place, *partials)
+    upstream = call(sum_four_body, shape(TOK, GROUP), moved=1 << 20)(*partials)
     upstream = send(upstream, TURN)
 
     query_grad, key_grad, value_grad, layer_out = call(
@@ -252,9 +256,11 @@
         flops=5 * 4 * 2 * TOK * TOK * HEAD,
         moved=3 << 20,
         limit=63,
-    )(place, upstream, query_rows, key_rows, value_matrix, prob, own, across)
-
-    pieces = call(sum_z_body, (shape(SHARD, GROUP),) * 2, moved=2 << 20)(place, grad_rows)
+    )(upstream, query_rows, key_rows, value_matrix, prob, own, across)
+
+    pieces = call(sum_z_body, (shape(SHARD, GROUP),) * 2, moved=2 << 20)(
+        grad_rows
+    )
     pieces = [send(piece, pairs).astype(F32) for piece, pairs in zip(pieces, TO_OWNER)]
     weight_grad = pieces[0] + pieces[1]
     return (layer_out, query_grad, key_grad, value_grad, weight_grad.T)

time: 134 us -> 131 us (0.978)
  Pallas kernels: 23.9 us -> 20.3 us
    pallas_call x9, Pallas kernels: 23.9 us -> 20.3 us  [run(): pl.pallas_call(body, out_shape=outs, grid=(1,), in_specs=[pl.BlockSpec(me...]
    all_to_all x2, waiting for transfers between devices: 19.3 us -> 17.5 us  [exchange(): lax.all_to_all(blocks, 'dp', 0, 0, axis_index_groups=groups, tiled=True)]
    unnamed x26 -> x30, local copies, waits for them, and re-layouts: 2.3 us -> 3.53 us
  transfers between devices with their start and end apart: 19 -> 19, of which waited for: 9 -> 9; matrix products, arithmetic and copies ran while one was open for 2% -> 1% of each run, Pallas kernels for 14% -> 12%
where the time goes in v7:
time: 131 us
  waiting for transfers between devices  58.3 us (45%)
  starting transfers between devices  46.2 us (35%)
  Pallas kernels  20.3 us (15%)
  local copies, waits for them, and re-layouts  4.42 us (3%)
    ppermute x17, waiting for transfers between devices, send(): return lax.ppermute(value, AXES, pairs)  40.8 us
    ppermute x17, starting transfers between devices, send(): return lax.ppermute(value, AXES, pairs)  29.3 us
    pallas_call x9, Pallas kernels, run(): pl.pallas_call(body, out_shape=outs, grid=(1,), in_specs=[pl.BlockSpec(me...  20.3 us
    all_to_all x2, waiting for transfers between devices, exchange(): lax.all_to_all(blocks, 'dp', 0, 0, axis_index_groups=groups, tiled=True)  17.5 us
    all_to_all x2, starting transfers between devices, exchange(): lax.all_to_all(blocks, 'dp', 0, 0, axis_index_groups=groups, tiled=True)  17 us
    unnamed x30, local copies, waits for them, and re-layouts  3.53 us
  transfers between devices with their start and end apart: 19, of which 9 were waited for; matrix products, arithmetic and copies ran while one was open for 1% of the time, Pallas kernels for 12%

profile of v7, /device:TPU:4, one launch (start us, length us, event | category | flops | bytes accessed | tf_op | source)
XLA Modules:
  0.0 130.8 jit_solution(14560781199743610408)
XLA Ops:
  0.6 0.0 copy-start.3
  0.6 5.2 %collective-permute-start.3 = (bf16[80,512]{1,0:T(8,128)(2,1)}, bf16[80,512]{1,0:T(8,128)(2,1)S(1)}, u32[]{:S(2)}, u32[]{:S(2)}) collective-permute-start(bf16[80,512]{1,0:T(8,128)(2,1)} %bitcast.5), channel_id=1, source_target_pairs={{0,0},{1,4},{2,64},{3,68},{4,192},{5,196},{6,128},{7,132},{8,8},{9... | collective-permute-start | bytes 245768 | tf_op jit(solution)/shard_map/ppermute | solution.py:54
  5.8 1.1 collective-permute-start.1
  6.9 4.6 %collective-permute-done.3 = bf16[80,512]{1,0:T(8,128)(2,1)S(1)} collective-permute-done((bf16[80,512]{1,0:T(8,128)(2,1)}, bf16[80,512]{1,0:T(8,128)(2,1)S(1)}, u32[]{:S(2)}, u32[]{:S(2)}) %collective-permute-start.3) | collective-permute-done | bytes 81952 | tf_op jit(solution)/shard_map/ppermute | solution.py:54
  11.5 0.9 broadcast_in_dim.2
  12.4 8.5 %all-to-all-start = ((bf16[8,80,512]{2,1,0:T(8,128)(2,1)}), bf16[8,80,512]{2,1,0:T(8,128)(2,1)}, u32[]{:S(2)}, u32[]{:S(2)}) async-start(bf16[8,80,512]{2,1,0:T(8,128)(2,1)} %broadcast_in_dim.2), calls=%async_computation | async-start | bytes 1310720 | tf_op jit(solution)/shard_map/all_to_all | solution.py:58
  20.9 0.0 copy-done.3
  20.9 0.1 collective-permute-start
  21.0 2.7 %collective-permute-done.1.o2 = bf16[256,1280]{1,0:T(8,128)(2,1)} collective-permute-done((bf16[256,1280]{1,0:T(8,128)(2,1)}, bf16[256,1280]{1,0:T(8,128)(2,1)}, u32[]{:S(2)}, u32[]{:S(2)}) %collective-permute-start.1) | collective-permute-done | bytes 655392 | tf_op jit(solution)/shard_map/ppermute | solution.py:54
  23.7 0.0 collective-permute-start.2
  23.7 3.1 %shard_map.103 = (bf16[256,512]{1,0:T(8,128)(2,1)}, f32[4,256,256]{2,1,0:T(8,128)}) custom-call(s32[8]{0:T(128)} %bitcast.6, bf16[256,512]{1,0:T(8,128)(2,1)} %q_ref.3, bf16[256,128]{1,0:T(8,128)(2,1)} %k_ref.3, bf16[256,128]{1,0:T(8,128)(2,1)} %v_ref.3), custom_call_target="tpu_custom_call" | custom-call | flops 134217728 | bytes 2097152 | tf_op jit(solution)/shard_map/pallas_call | solution.py:78
  26.7 3.4 %collective-permute-start.9 = (bf16[256,512]{1,0:T(8,128)(2,1)}, bf16[256,512]{1,0:T(8,128)(2,1)S(1)}, u32[]{:S(2)}, u32[]{:S(2)}) collective-permute-start(bf16[256,512]{1,0:T(8,128)(2,1)} %get-tuple-element.25), channel_id=1, source_target_pairs={{0,0},{1,4},{2,64},{3,68},{4,1},{5,5},{6,65},{7,69},{8,8},{9,12},{... | collective-permute-start | bytes 786440 | tf_op jit(solution)/shard_map/ppermute | solution.py:54
  30.2 9.4 %collective-permute-done.9.r0 = bf16[256,512]{1,0:T(8,128)(2,1)S(1)} collective-permute-done((bf16[256,512]{1,0:T(8,128)(2,1)}, bf16[256,512]{1,0:T(8,128)(2,1)S(1)}, u32[]{:S(2)}, u32[]{:S(2)}) %collective-permute-start.9) | collective-permute-done | bytes 262176 | tf_op jit(solution)/shard_map/ppermute | solution.py:54
  39.6 0.0 collective-permute-start.12
  39.6 0.0 collective-permute-start.11
  39.6 2.0 %collective-permute-start.10 = (bf16[256,512]{1,0:T(8,128)(2,1)S(1)}, bf16[256,512]{1,0:T(8,128)(2,1)S(1)}, u32[]{:S(2)}, u32[]{:S(2)}) collective-permute-start(bf16[256,512]{1,0:T(8,128)(2,1)S(1)} %collective-permute-done.9.r0), channel_id=1, source_target_pairs={{0,1},{1,2},{2,3},{3,0},{4,5},{5,6},{6,7},{7,4},{8,9},{9,10},{10,1... | collective-permute-start | bytes 786440 | tf_op jit(solution)/shard_map/ppermute | solution.py:54
  41.6 7.1 %collective-permute-done.12.r3 = bf16[256,512]{1,0:T(8,128)(2,1)S(1)} collective-permute-done((bf16[256,512]{1,0:T(8,128)(2,1)S(1)}, bf16[256,512]{1,0:T(8,128)(2,1)S(1)}, u32[]{:S(2)}, u32[]{:S(2)}) %collective-permute-start.12) | collective-permute-done | bytes 262176 | tf_op jit(solution)/shard_map/ppermute | solution.py:54
  48.8 0.0 all-to-all-done.w0
  48.8 0.0 collective-permute-start.4
  48.8 1.5 %collective-permute-done.11.r2 = bf16[256,512]{1,0:T(8,128)(2,1)S(1)} collective-permute-done((bf16[256,512]{1,0:T(8,128)(2,1)S(1)}, bf16[256,512]{1,0:T(8,128)(2,1)S(1)}, u32[]{:S(2)}, u32[]{:S(2)}) %collective-permute-start.11) | collective-permute-done | bytes 262176 | tf_op jit(solution)/shard_map/ppermute | solution.py:54
  50.3 5.2 %collective-permute-done.10.r1 = bf16[256,512]{1,0:T(8,128)(2,1)S(1)} collective-permute-done((bf16[256,512]{1,0:T(8,128)(2,1)S(1)}, bf16[256,512]{1,0:T(8,128)(2,1)S(1)}, u32[]{:S(2)}, u32[]{:S(2)}) %collective-permute-start.10) | collective-permute-done | bytes 262176 | tf_op jit(solution)/shard_map/ppermute | solution.py:54
  55.5 0.0 collective-permute-done.o1
  55.5 0.0 collective-permute-done.2.o3
  55.5 4.3 %shard_map.108 = bf16[1280,512]{1,0:T(8,128)(2,1)} custom-call(bf16[256,1280]{1,0:T(8,128)(2,1)S(1)} %copy-done.3, bf16[256,1280]{1,0:T(8,128)(2,1)} %collective-permute-done.o1, bf16[256,1280]{1,0:T(8,128)(2,1)} %collective-permute-done.1.o2, bf16[256,1280]{1,0:T(8,128)(2,1)} %collective-permute-done.2.o3, bf16[256,512]{1,0:T(8,128)(2,1)S(1)} %collective-permute-done.9.r0, ...), custom_call_target="tpu_custom_call" | custom-call | flops 1342177280 | bytes 6291456 | tf_op jit(solution)/shard_map/pallas_call | solution.py:78
  59.8 0.0 copy-done.4
  59.8 0.0 copy-done.6
  59.8 0.0 copy-done.8
  59.8 0.0 copy-done.10
  59.8 8.5 %all-to-all-start.1 = ((bf16[8,160,512]{2,1,0:T(8,128)(2,1)}), bf16[8,160,512]{2,1,0:T(8,128)(2,1)S(1)}, u32[]{:S(2)}, u32[]{:S(2)}) async-start(bf16[8,160,512]{2,1,0:T(8,128)(2,1)} %bitcast.2), calls=%async_computation.1 | async-start | bytes 2621440 | tf_op jit(solution)/shard_map/all_to_all | solution.py:58
  68.3 0.0 copy-start.7
  68.3 0.0 copy-start.9
  68.3 0.0 copy-start.11
  68.3 0.0 collective-permute-done.4.w1
  68.3 0.0 copy-start.12
  68.4 0.8 copy-done.12
  69.2 1.1 copy-done.13
  70.3 4.1 %shard_map.101 = (bf16[256,512]{1,0:T(8,128)(2,1)S(1)}, bf16[256,512]{1,0:T(8,128)(2,1)}, bf16[256,512]{1,0:T(8,128)(2,1)}, bf16[256,512]{1,0:T(8,128)(2,1)}, bf16[1280,512]{1,0:T(8,128)(2,1)S(1)}) custom-call(bf16[256,1280]{1,0:T(8,128)(2,1)S(1)} %copy-done.3, bf16[256,1280]{1,0:T(8,128)(2,1)} %collective-permute-done.o1, ...), custom_call_target="tpu_custom_call" | custom-call | flops 1342177280 | bytes 6291456 | tf_op jit(solution)/shard_map/pallas_call | solution.py:78
  74.4 0.9 shard_map.104
  75.3 0.1 collective-permute-start.13
  75.4 3.0 %collective-permute-done.13.pair = bf16[2,256,1280]{2,1,0:T(8,128)(2,1)S(1)} collective-permute-done((bf16[2,256,1280]{2,1,0:T(8,128)(2,1)S(1)}, bf16[2,256,1280]{2,1,0:T(8,128)(2,1)S(1)}, u32[]{:S(2)}, u32[]{:S(2)}) %collective-permute-start.13) | collective-permute-done | bytes 1310752 | tf_op jit(solution)/shard_map/ppermute | solution.py:54
  78.4 1.4 %shard_map.106 = bf16[256,1280]{1,0:T(8,128)(2,1)} custom-call(bf16[2,256,512]{2,1,0:T(8,128)(2,1)S(1)} %get-tuple-element.27.att, bf16[1280,512]{1,0:T(8,128)(2,1)S(1)} %get-tuple-element.26.wt, bf16[2,256,1280]{2,1,0:T(8,128)(2,1)S(1)} %collective-permute-done.13.pair), custom_call_target="tpu_custom_call" | custom-call | flops 335544320 | bytes 3145728 | tf_op jit(solution)/shard_map/pallas_call | solution.py:78
  79.8 0.2 collective-permute-start.14
  80.1 0.0 collective-permute-start.5
  80.1 5.3 %collective-permute-start.6 = (bf16[256,512]{1,0:T(8,128)(2,1)}, bf16[256,512]{1,0:T(8,128)(2,1)}, u32[]{:S(2)}, u32[]{:S(2)}) collective-permute-start(bf16[256,512]{1,0:T(8,128)(2,1)} %get-tuple-element.22), channel_id=1, source_target_pairs={{0,2},{1,3},{2,0},{3,1},{4,6},{5,7},{6,4},{7,5},{8,10},{9,11},{10,... | collective-permute-start | bytes 786440 | tf_op jit(solution)/shard_map/ppermute | solution.py:54
  85.4 0.0 collective-permute-start.7
  85.4 17.5 %all-to-all-done.1.blocks = bf16[8,160,512]{2,1,0:T(8,128)(2,1)S(1)} async-done(((bf16[8,160,512]{2,1,0:T(8,128)(2,1)}), bf16[8,160,512]{2,1,0:T(8,128)(2,1)S(1)}, u32[]{:S(2)}, u32[]{:S(2)}) %all-to-all-start.1) | async-done | bytes 1310752 | tf_op jit(solution)/shard_map/all_to_all | solution.py:58
  102.9 0.2 shard_map.109
  103.0 2.1 %collective-permute-start.15 = (bf16[80,512]{1,0:T(8,128)(2,1)S(1)}, bf16[80,512]{1,0:T(8,128)(2,1)S(1)}, u32[]{:S(2)}, u32[]{:S(2)}) collective-permute-start(bf16[80,512]{1,0:T(8,128)(2,1)S(1)} %get-tuple-element.33), channel_id=1, source_target_pairs={{0,0},{1,64},{2,128},{3,192},{4,1},{5,65},{6,129},{7,193},{8,8},{9... | collective-permute-start | bytes 245768 | tf_op jit(solution)/shard_map/ppermute | solution.py:54
  105.1 0.0 collective-permute-done.5.a1
  105.1 7.8 %collective-permute-start.16 = (bf16[80,512]{1,0:T(8,128)(2,1)S(1)}, bf16[80,512]{1,0:T(8,128)(2,1)S(1)}, u32[]{:S(2)}, u32[]{:S(2)}) collective-permute-start(bf16[80,512]{1,0:T(8,128)(2,1)S(1)} %get-tuple-element.34), channel_id=1, source_target_pairs={{0,4},{1,68},{2,132},{3,196},{4,5},{5,69},{6,133},{7,197},{8,12},{... | collective-permute-start | bytes 245768 | tf_op jit(solution)/shard_map/ppermute | solution.py:54
  112.9 0.0 collective-permute-done.6.a2
  112.9 0.0 collective-permute-done.7.a3
  113.0 1.2 shard_map.102
  114.2 1.9 %collective-permute-start.8 = (bf16[256,512]{1,0:T(8,128)(2,1)S(1)}, bf16[256,512]{1,0:T(8,128)(2,1)S(1)}, u32[]{:S(2)}, u32[]{:S(2)}) collective-permute-start(bf16[256,512]{1,0:T(8,128)(2,1)S(1)} %shard_map.102), channel_id=1, source_target_pairs={{0,0},{1,4},{2,64},{3,68},{4,1},{5,5},{6,65},{7,69},{8,8},{9,12},{... | collective-permute-start | bytes 786440 | tf_op jit(solution)/shard_map/ppermute | solution.py:54
  116.1 0.0 copy-done.1
  116.1 0.5 shard_map.105.own
  116.7 0.8 copy-done.2
  117.5 0.0 collective-permute-done.15
  117.5 0.0 collective-permute-done.16
  117.6 0.7 add_bitcast_fusion
  118.2 7.2 %collective-permute-done.8.up_ref = bf16[256,512]{1,0:T(8,128)(2,1)S(1)} collective-permute-done((bf16[256,512]{1,0:T(8,128)(2,1)S(1)}, bf16[256,512]{1,0:T(8,128)(2,1)S(1)}, u32[]{:S(2)}, u32[]{:S(2)}) %collective-permute-start.8) | collective-permute-done | bytes 262176 | tf_op jit(solution)/shard_map/ppermute | solution.py:54
  125.4 0.0 collective-permute-done.14.across
  125.5 0.7 copy-done.14
  126.2 4.6 %shard_map.107 = (bf16[256,512]{1,0:T(8,128)(2,1)}, bf16[256,128]{1,0:T(8,128)(2,1)}, bf16[256,128]{1,0:T(8,128)(2,1)}, bf16[256,1280]{1,0:T(8,128)(2,1)}) custom-call(bf16[256,512]{1,0:T(8,128)(2,1)} %copy-done.14, bf16[256,512]{1,0:T(8,128)(2,1)} %q_ref.3, bf16[256,128]{1,0:T(8,128)(2,1)} %k_ref.3, bf16[256,128]{1,0:T(8,128)(2,1)} %v_ref.3, ...), custom_call_target="tpu_custom_call" | custom-call | flops 335544320 | bytes 3145728 | tf_op jit(solution)/shard_map/pallas_call | solution.py:78
  (15 shorter events, 0.0 us)
Async XLA Ops:
  0.6 20.3 %copy-start.3 = (bf16[256,1280]{1,0:T(8,128)(2,1)S(1)}, bf16[256,1280]{1,0:T(8,128)(2,1)}, u32[]{:S(2)}) copy-start(bf16[256,1280]{1,0:T(8,128)(2,1)} %o0.3) | copy-start | bytes 1966084
  0.6 10.9 %collective-permute-start.3 = (bf16[80,512]{1,0:T(8,128)(2,1)}, bf16[80,512]{1,0:T(8,128)(2,1)S(1)}, u32[]{:S(2)}, u32[]{:S(2)}) collective-permute-start(bf16[80,512]{1,0:T(8,128)(2,1)} %bitcast.5), channel_id=1, source_target_pairs={{0,0},{1,4},{2,64},{3,68},{4,192},{5,196},{6,128},{7,132},{8,8},{9... | collective-permute-start | bytes 245768 | tf_op jit(solution)/shard_map/ppermute | solution.py:54
  5.8 17.8 %collective-permute-start.1 = (bf16[256,1280]{1,0:T(8,128)(2,1)}, bf16[256,1280]{1,0:T(8,128)(2,1)}, u32[]{:S(2)}, u32[]{:S(2)}) collective-permute-start(bf16[256,1280]{1,0:T(8,128)(2,1)} %o0.3), channel_id=1, source_target_pairs={{0,64},{1,65},{2,66},{3,67},{4,68},{5,69},{6,70},{7,71},{8,72},{9,... | collective-permute-start | bytes 1966088 | tf_op jit(solution)/shard_map/ppermute | solution.py:54
  12.4 36.4 %all-to-all-start = ((bf16[8,80,512]{2,1,0:T(8,128)(2,1)}), bf16[8,80,512]{2,1,0:T(8,128)(2,1)}, u32[]{:S(2)}, u32[]{:S(2)}) async-start(bf16[8,80,512]{2,1,0:T(8,128)(2,1)} %broadcast_in_dim.2), calls=%async_computation | async-start | bytes 1310720 | tf_op jit(solution)/shard_map/all_to_all | solution.py:58
  20.9 34.6 %collective-permute-start = (bf16[256,1280]{1,0:T(8,128)(2,1)S(1)}, bf16[256,1280]{1,0:T(8,128)(2,1)}, u32[]{:S(2)}, u32[]{:S(2)}) collective-permute-start(bf16[256,1280]{1,0:T(8,128)(2,1)S(1)} %copy-done.3), channel_id=1, source_target_pairs={{0,4},{1,5},{2,6},{3,7},{4,0},{5,1},{6,2},{7,3},{8,12},{9,13},{10,... | collective-permute-start | bytes 1966088 | tf_op jit(solution)/shard_map/ppermute | solution.py:54
  23.7 31.8 %collective-permute-start.2 = (bf16[256,1280]{1,0:T(8,128)(2,1)}, bf16[256,1280]{1,0:T(8,128)(2,1)}, u32[]{:S(2)}, u32[]{:S(2)}) collective-permute-start(bf16[256,1280]{1,0:T(8,128)(2,1)} %collective-permute-done.1.o2), channel_id=1, source_target_pairs={{0,4},{1,5},{2,6},{3,7},{4,0},{5,1},{6,2},{7,3},{8,12},{9,13},{10,... | collective-permute-start | bytes 1966088 | tf_op jit(solution)/shard_map/ppermute | solution.py:54
  26.7 12.8 %collective-permute-start.9 = (bf16[256,512]{1,0:T(8,128)(2,1)}, bf16[256,512]{1,0:T(8,128)(2,1)S(1)}, u32[]{:S(2)}, u32[]{:S(2)}) collective-permute-start(bf16[256,512]{1,0:T(8,128)(2,1)} %get-tuple-element.25), channel_id=1, source_target_pairs={{0,0},{1,4},{2,64},{3,68},{4,1},{5,5},{6,65},{7,69},{8,8},{9,12},{... | collective-permute-start | bytes 786440 | tf_op jit(solution)/shard_map/ppermute | solution.py:54
  39.6 20.2 %copy-start.4 = (bf16[256,512]{1,0:T(8,128)(2,1)}, bf16[256,512]{1,0:T(8,128)(2,1)S(1)}, u32[]{:S(2)}) copy-start(bf16[256,512]{1,0:T(8,128)(2,1)S(1)} %collective-permute-done.9.r0) | copy-start | bytes 786436
  39.6 9.2 %collective-permute-start.12 = (bf16[256,512]{1,0:T(8,128)(2,1)S(1)}, bf16[256,512]{1,0:T(8,128)(2,1)S(1)}, u32[]{:S(2)}, u32[]{:S(2)}) collective-permute-start(bf16[256,512]{1,0:T(8,128)(2,1)S(1)} %collective-permute-done.9.r0), channel_id=1, source_target_pairs={{0,3},{1,0},{2,1},{3,2},{4,7},{5,4},{6,5},{7,6},{8,11},{9,8},{10,9... | collective-permute-start | bytes 786440 | tf_op jit(solution)/shard_map/ppermute | solution.py:54
  39.6 10.7 %collective-permute-start.11 = (bf16[256,512]{1,0:T(8,128)(2,1)S(1)}, bf16[256,512]{1,0:T(8,128)(2,1)S(1)}, u32[]{:S(2)}, u32[]{:S(2)}) collective-permute-start(bf16[256,512]{1,0:T(8,128)(2,1)S(1)} %collective-permute-done.9.r0), channel_id=1, source_target_pairs={{0,2},{1,3},{2,0},{3,1},{4,6},{5,7},{6,4},{7,5},{8,10},{9,11},{10,... | collective-permute-start | bytes 786440 | tf_op jit(solution)/shard_map/ppermute | solution.py:54
  39.6 15.9 %collective-permute-start.10 = (bf16[256,512]{1,0:T(8,128)(2,1)S(1)}, bf16[256,512]{1,0:T(8,128)(2,1)S(1)}, u32[]{:S(2)}, u32[]{:S(2)}) collective-permute-start(bf16[256,512]{1,0:T(8,128)(2,1)S(1)} %collective-permute-done.9.r0), channel_id=1, source_target_pairs={{0,1},{1,2},{2,3},{3,0},{4,5},{5,6},{6,7},{7,4},{8,9},{9,10},{10,1... | collective-permute-start | bytes 786440 | tf_op jit(solution)/shard_map/ppermute | solution.py:54
  48.8 11.0 %copy-start.6 = (bf16[256,512]{1,0:T(8,128)(2,1)}, bf16[256,512]{1,0:T(8,128)(2,1)S(1)}, u32[]{:S(2)}) copy-start(bf16[256,512]{1,0:T(8,128)(2,1)S(1)} %collective-permute-done.12.r3) | copy-start | bytes 786436
  48.8 19.6 %collective-permute-start.4 = (bf16[8,80,512]{2,1,0:T(8,128)(2,1)}, bf16[8,80,512]{2,1,0:T(8,128)(2,1)S(1)}, u32[]{:S(2)}, u32[]{:S(2)}) collective-permute-start(bf16[8,80,512]{2,1,0:T(8,128)(2,1)} %all-to-all-done.w0), channel_id=1, source_target_pairs={{0,192},{1,193},{2,194},{3,195},{4,196},{5,197},{6,198},{7,199},{8... | collective-permute-start | bytes 1966088 | tf_op jit(solution)/shard_map/ppermute | solution.py:54
  50.3 9.5 %copy-start.8 = (bf16[256,512]{1,0:T(8,128)(2,1)}, bf16[256,512]{1,0:T(8,128)(2,1)S(1)}, u32[]{:S(2)}) copy-start(bf16[256,512]{1,0:T(8,128)(2,1)S(1)} %collective-permute-done.11.r2) | copy-start | bytes 786436
  55.5 4.3 %copy-start.10 = (bf16[256,512]{1,0:T(8,128)(2,1)}, bf16[256,512]{1,0:T(8,128)(2,1)S(1)}, u32[]{:S(2)}) copy-start(bf16[256,512]{1,0:T(8,128)(2,1)S(1)} %collective-permute-done.10.r1) | copy-start | bytes 786436
  59.8 43.0 %all-to-all-start.1 = ((bf16[8,160,512]{2,1,0:T(8,128)(2,1)}), bf16[8,160,512]{2,1,0:T(8,128)(2,1)S(1)}, u32[]{:S(2)}, u32[]{:S(2)}) async-start(bf16[8,160,512]{2,1,0:T(8,128)(2,1)} %bitcast.2), calls=%async_computation.1 | async-start | bytes 2621440 | tf_op jit(solution)/shard_map/all_to_all | solution.py:58
  68.3 6.1 %copy-start.5 = (bf16[256,512]{1,0:T(8,128)(2,1)S(1)}, bf16[256,512]{1,0:T(8,128)(2,1)}, u32[]{:S(2)}) copy-start(bf16[256,512]{1,0:T(8,128)(2,1)} %copy-done.4) | copy-start | bytes 786436
  68.3 6.1 %copy-start.7 = (bf16[256,512]{1,0:T(8,128)(2,1)S(1)}, bf16[256,512]{1,0:T(8,128)(2,1)}, u32[]{:S(2)}) copy-start(bf16[256,512]{1,0:T(8,128)(2,1)} %copy-done.6) | copy-start | bytes 786436
  68.3 6.1 %copy-start.9 = (bf16[256,512]{1,0:T(8,128)(2,1)S(1)}, bf16[256,512]{1,0:T(8,128)(2,1)}, u32[]{:S(2)}) copy-start(bf16[256,512]{1,0:T(8,128)(2,1)} %copy-done.8) | copy-start | bytes 786436
  68.3 6.1 %copy-start.11 = (bf16[256,512]{1,0:T(8,128)(2,1)S(1)}, bf16[256,512]{1,0:T(8,128)(2,1)}, u32[]{:S(2)}) copy-start(bf16[256,512]{1,0:T(8,128)(2,1)} %copy-done.10) | copy-start | bytes 786436
  68.3 0.8 copy-start.12
  69.2 1.1 copy-start.13
  75.3 3.1 %collective-permute-start.13 = (bf16[2,256,1280]{2,1,0:T(8,128)(2,1)S(1)}, bf16[2,256,1280]{2,1,0:T(8,128)(2,1)S(1)}, u32[]{:S(2)}, u32[]{:S(2)}) collective-permute-start(bf16[2,256,1280]{2,1,0:T(8,128)(2,1)S(1)} %get-tuple-element.28), channel_id=1, source_target_pairs={{0,4},{1,5},{2,6},{3,7},{4,0},{5,1},{6,2},{7,3},{8,12},{9,13},{10,... | collective-permute-start | bytes 3932168 | tf_op jit(solution)/shard_map/ppermute | solution.py:54
  78.4 1.4 %copy-start = (bf16[2,256,1280]{2,1,0:T(8,128)(2,1)}, bf16[2,256,1280]{2,1,0:T(8,128)(2,1)S(1)}, u32[]{:S(2)}) copy-start(bf16[2,256,1280]{2,1,0:T(8,128)(2,1)S(1)} %collective-permute-done.13.pair) | copy-start | bytes 3932164
  79.8 45.6 %collective-permute-start.14 = (bf16[256,1280]{1,0:T(8,128)(2,1)}, bf16[256,1280]{1,0:T(8,128)(2,1)}, u32[]{:S(2)}, u32[]{:S(2)}) collective-permute-start(bf16[256,1280]{1,0:T(8,128)(2,1)} %shard_map.106), channel_id=1, source_target_pairs={{0,64},{1,65},{2,66},{3,67},{4,68},{5,69},{6,70},{7,71},{8,72},{9,... | collective-permute-start | bytes 1966088 | tf_op jit(solution)/shard_map/ppermute | solution.py:54
  80.1 25.0 %collective-permute-start.5 = (bf16[256,512]{1,0:T(8,128)(2,1)}, bf16[256,512]{1,0:T(8,128)(2,1)}, u32[]{:S(2)}, u32[]{:S(2)}) collective-permute-start(bf16[256,512]{1,0:T(8,128)(2,1)} %get-tuple-element.21), channel_id=1, source_target_pairs={{0,1},{1,2},{2,3},{3,0},{4,5},{5,6},{6,7},{7,4},{8,9},{9,10},{10,1... | collective-permute-start | bytes 786440 | tf_op jit(solution)/shard_map/ppermute | solution.py:54
  80.1 32.9 %collective-permute-start.6 = (bf16[256,512]{1,0:T(8,128)(2,1)}, bf16[256,512]{1,0:T(8,128)(2,1)}, u32[]{:S(2)}, u32[]{:S(2)}) collective-permute-start(bf16[256,512]{1,0:T(8,128)(2,1)} %get-tuple-element.22), channel_id=1, source_target_pairs={{0,2},{1,3},{2,0},{3,1},{4,6},{5,7},{6,4},{7,5},{8,10},{9,11},{10,... | collective-permute-start | bytes 786440 | tf_op jit(solution)/shard_map/ppermute | solution.py:54
  85.4 27.6 %collective-permute-start.7 = (bf16[256,512]{1,0:T(8,128)(2,1)}, bf16[256,512]{1,0:T(8,128)(2,1)}, u32[]{:S(2)}, u32[]{:S(2)}) collective-permute-start(bf16[256,512]{1,0:T(8,128)(2,1)} %get-tuple-element.23), channel_id=1, source_target_pairs={{0,3},{1,0},{2,1},{3,2},{4,7},{5,4},{6,5},{7,6},{8,11},{9,8},{10,9... | collective-permute-start | bytes 786440 | tf_op jit(solution)/shard_map/ppermute | solution.py:54
  102.9 13.3 %copy-start.1 = (bf16[2,256,1280]{2,1,0:T(8,128)(2,1)S(1)}, bf16[2,256,1280]{2,1,0:T(8,128)(2,1)}, u32[]{:S(2)}) copy-start(bf16[2,256,1280]{2,1,0:T(8,128)(2,1)} %copy-done) | copy-start | bytes 3932164
  103.0 14.5 %collective-permute-start.15 = (bf16[80,512]{1,0:T(8,128)(2,1)S(1)}, bf16[80,512]{1,0:T(8,128)(2,1)S(1)}, u32[]{:S(2)}, u32[]{:S(2)}) collective-permute-start(bf16[80,512]{1,0:T(8,128)(2,1)S(1)} %get-tuple-element.33), channel_id=1, source_target_pairs={{0,0},{1,64},{2,128},{3,192},{4,1},{5,65},{6,129},{7,193},{8,8},{9... | collective-permute-start | bytes 245768 | tf_op jit(solution)/shard_map/ppermute | solution.py:54
  105.1 12.5 %collective-permute-start.16 = (bf16[80,512]{1,0:T(8,128)(2,1)S(1)}, bf16[80,512]{1,0:T(8,128)(2,1)S(1)}, u32[]{:S(2)}, u32[]{:S(2)}) collective-permute-start(bf16[80,512]{1,0:T(8,128)(2,1)S(1)} %get-tuple-element.34), channel_id=1, source_target_pairs={{0,4},{1,68},{2,132},{3,196},{4,5},{5,69},{6,133},{7,197},{8,12},{... | collective-permute-start | bytes 245768 | tf_op jit(solution)/shard_map/ppermute | solution.py:54
  114.2 11.2 %collective-permute-start.8 = (bf16[256,512]{1,0:T(8,128)(2,1)S(1)}, bf16[256,512]{1,0:T(8,128)(2,1)S(1)}, u32[]{:S(2)}, u32[]{:S(2)}) collective-permute-start(bf16[256,512]{1,0:T(8,128)(2,1)S(1)} %shard_map.102), channel_id=1, source_target_pairs={{0,0},{1,4},{2,64},{3,68},{4,1},{5,5},{6,65},{7,69},{8,8},{9,12},{... | collective-permute-start | bytes 786440 | tf_op jit(solution)/shard_map/ppermute | solution.py:54
  116.7 0.9 copy-start.2
  125.4 0.7 copy-start.14

commit v8 on v7

--- a/solution.py
+++ b/solution.py
@@ -94,7 +94,10 @@
     return jax.ShapeDtypeStruct(dims, dtype)
 
 
-def forward_body(lengths, q_ref, k_ref, v_ref, att_ref, prob_ref):
+def forward_body(lengths, q_ref, k_ref, v_ref, att_ref, prob_ref, kept):
+    kept[:, :GROUP] = q_ref[...]
+    kept[:, GROUP : GROUP + HEAD] = k_ref[...]
+    kept[:, GROUP + HEAD :] = v_ref[...]
     rows = lax.broadcasted_iota(jnp.int32, (TOK, TOK), 0)
     cols = lax.broadcasted_iota(jnp.int32, (TOK, TOK), 1)
     row_at = lax.broadcasted_iota(jnp.int32, (TOK, 1), 0)
@@ -123,19 +126,20 @@
     ).astype(BF)
 
 
-def backward_body(up_ref, q_ref, k_ref, v_ref, prob_ref, own, across, dq_ref, dk_ref, dv_ref, out):
+def backward_body(up_ref, kept, prob_ref, own, across, dq_ref, dk_ref, dv_ref, out):
     out[...] = (own[...].astype(F32) + across[...].astype(F32)).astype(BF)
+    keys, values = kept[:, GROUP : GROUP + HEAD], kept[:, GROUP + HEAD :]
     key_sum = jnp.zeros((TOK, HEAD), F32)
     value_sum = jnp.zeros((TOK, HEAD), F32)
     for h in range(HEADS):
         at = slice(h * HEAD, (h + 1) * HEAD)
         up = up_ref[:, at]
         prob = prob_ref[h]
-        prob_grad = dot(up, v_ref[...], ((1,), (1,)))
+        prob_grad = dot(up, values, ((1,), (1,)))
         delta = jnp.sum(prob * prob_grad, axis=-1, keepdims=True)
         score = (prob * (prob_grad - delta) * SCALE).astype(BF)
-        dq_ref[:, at] = dot(score, k_ref[...], ((1,), (0,))).astype(BF)
-        key_sum = key_sum + dot(score, q_ref[:, at], ((0,), (0,)))
+        dq_ref[:, at] = dot(score, keys, ((1,), (0,))).astype(BF)
+        key_sum = key_sum + dot(score, kept[:, at], ((0,), (0,)))
         value_sum = value_sum + dot(prob.astype(BF), up, ((0,), (0,)))
     dk_ref[...] = key_sum.astype(BF)
     dv_ref[...] = value_sum.astype(BF)
@@ -153,34 +157,34 @@
         grad_ref[at, :] = total.astype(BF)
 
 
-def layer_pair_body(r0, r1, r2, r3, wt, pair_ref, att_ref, att):
-    g, y, _ = place()
+def layer_pair_body(r0, r1, r2, r3, w0, w1, pair_ref, att_ref, wt_ref, att):
+    g, y, high = place()
     for k, ref in enumerate((r0, r1, r2, r3)):
         att[jnp.bitwise_xor((y + 4 - k) % 4, g)] = ref[...]
-    for i in range(2):
-        pair_ref[i] = dot(att[2 * i + 1], wt[...], ((1,), (1,))).astype(BF)
-        att_ref[i] = att[2 * i]
-
-
-def layer_across_body(att, wt, pair, out):
-    out[...] = (dot(att[1], wt[...], ((1,), (1,))) + pair[1].astype(F32)).astype(BF)
-
-
-def layer_own_body(att, wt, pair, out):
-    out[...] = (dot(att[0], wt[...], ((1,), (1,))) + pair[0].astype(F32)).astype(BF)
-
-
-def attn_grad_body(o0, o1, o2, o3, w0, w1, g0, g1, g2, g3, wt_ref, og):
-    g, y, high = place()
     for k, ref in enumerate((w0, w1)):
         c = (high + k) % 2
         for z in range(NZ):
             wt_ref[pl.ds(pl.multiple_of(z * 160 + c * SHARD, 16), SHARD), :] = ref[z]
+    for i in range(2):
+        pair_ref[i] = dot(att[2 * i + 1], wt_ref[...], ((1,), (1,))).astype(BF)
+        att_ref[i] = att[2 * i]
+
+
+def layer_across_body(att, wt, pair, out):
+    out[...] = (dot(att[1], wt[...], ((1,), (1,))) + pair[1].astype(F32)).astype(BF)
+
+
+def layer_own_body(att, wt, pair, out):
+    out[...] = (dot(att[0], wt[...], ((1,), (1,))) + pair[0].astype(F32)).astype(BF)
+
+
+def attn_grad_body(o0, o1, o2, o3, wt, g0, g1, g2, g3, og):
+    g, y, _ = place()
     for r, ref in enumerate((o0, o1, o2, o3)):
         og[r] = ref[...]
     for k, ref in enumerate((g0, g1, g2, g3)):
         at = jnp.bitwise_xor((y + k) % 4, g)
-        ref[...] = dot(og[at], wt_ref[...], ((1,), (0,))).astype(BF)
+        ref[...] = dot(og[at], wt[...], ((1,), (0,))).astype(BF)
 
 
 def sum_z_body(blocks, o0, o1):
@@ -201,9 +205,9 @@
     wt = exchange(jnp.broadcast_to(wt[None], (NZ, SHARD, GROUP)), Z_GROUPS)
     blocks = [wt, send(wt, OTHER)]
 
-    attended, prob = call(
+    attended, prob, kept = call(
         forward_body,
-        (shape(TOK, GROUP), shape(HEADS, TOK, TOK, dtype=F32)),
+        (shape(TOK, GROUP), shape(HEADS, TOK, TOK, dtype=F32), shape(TOK, GROUP + 2 * HEAD)),
         flops=4 * 4 * TOK * TOK * HEAD,
         moved=2 << 20,
         limit=63,
@@ -222,21 +226,20 @@
     )(*cols, *heads)
     grad_rows = exchange(grad_part.reshape(NZ, 2 * SHARD, GROUP), Z_GROUPS)
 
-    *partials, wt_all = call(
+    pair, attended_two, wt_all = call(
+        layer_pair_body,
+        (shape(2, TOK, COLS), shape(2, TOK, GROUP), shape(COLS, GROUP)),
+        scratch=(pltpu.VMEM((4, TOK, GROUP), BF),),
+        flops=big // 2,
+        moved=6 << 20,
+    )(*heads, *blocks)
+    partials = call(
         attn_grad_body,
-        (shape(TOK, GROUP),) * 4 + (shape(COLS, GROUP),),
+        (shape(TOK, GROUP),) * 4,
         scratch=(pltpu.VMEM((4, TOK, COLS), BF),),
         flops=big,
         moved=6 << 20,
-    )(*cols, *blocks)
-
-    pair, attended_two = call(
-        layer_pair_body,
-        (shape(2, TOK, COLS), shape(2, TOK, GROUP)),
-        scratch=(pltpu.VMEM((4, TOK, GROUP), BF),),
-        flops=big // 2,
-        moved=4 << 20,
-    )(*heads, wt_all)
+    )(*cols, wt_all)
     pair = send(pair, SWAP)
     across = call(
         layer_across_body, shape(TOK, COLS), flops=big // 4, moved=3 << 20
@@ -255,8 +258,7 @@
         (shape(TOK, GROUP), shape(TOK, HEAD), shape(TOK, HEAD), shape(TOK, COLS)),
         flops=5 * 4 * 2 * TOK * TOK * HEAD,
         moved=3 << 20,
-        limit=63,
-    )(upstream, query_rows, key_rows, value_matrix, prob, own, across)
+    )(upstream, kept, prob, own, across)
 
     pieces = call(sum_z_body, (shape(SHARD, GROUP),) * 2, moved=2 << 20)(
         grad_rows

time: 131 us -> 135 us (1.031)
  the two profiles are of different devices: /device:TPU:4 before, /device:TPU:2 now
where the time goes in v8:
time: 135 us
  waiting for transfers between devices  63.7 us (47%)
  starting transfers between devices  42.9 us (32%)
  Pallas kernels  20.8 us (15%)
  local copies, waits for them, and re-layouts  5.85 us (4%)
    ppermute x17, waiting for transfers between devices, send(): return lax.ppermute(value, AXES, pairs)  50.6 us
    ppermute x17, starting transfers between devices, send(): return lax.ppermute(value, AXES, pairs)  27.3 us
    pallas_call x9, Pallas kernels, run(): pl.pallas_call(body, out_shape=outs, grid=(1,), in_specs=[pl.BlockSpec(me...  20.8 us
    all_to_all x2, starting transfers between devices, exchange(): lax.all_to_all(blocks, 'dp', 0, 0, axis_index_groups=groups, tiled=True)  15.6 us
    all_to_all x2, waiting for transfers between devices, exchange(): lax.all_to_all(blocks, 'dp', 0, 0, axis_index_groups=groups, tiled=True)  13.1 us
    unnamed x28, local copies, waits for them, and re-layouts  4.96 us
  transfers between devices with their start and end apart: 19, of which 7 were waited for; matrix products, arithmetic and copies ran while one was open for 1% of the time, Pallas kernels for 13%

profile of v8, /device:TPU:2, one launch (start us, length us, event | category | flops | bytes accessed | tf_op | source)
XLA Modules:
  0.0 134.7 jit_solution(12065994328425345338)
XLA Ops:
  0.6 0.0 copy-start.3
  0.6 2.3 %collective-permute-start.1 = (bf16[256,1280]{1,0:T(8,128)(2,1)}, bf16[256,1280]{1,0:T(8,128)(2,1)}, u32[]{:S(2)}, u32[]{:S(2)}) collective-permute-start(bf16[256,1280]{1,0:T(8,128)(2,1)} %o0.3), channel_id=1, source_target_pairs={{0,64},{1,65},{2,66},{3,67},{4,68},{5,69},{6,70},{7,71},{8,72},{9,... | collective-permute-start | bytes 1966088 | tf_op jit(solution)/shard_map/ppermute | solution.py:54
  3.0 2.7 %collective-permute-start.7 = (bf16[80,512]{1,0:T(8,128)(2,1)}, bf16[80,512]{1,0:T(8,128)(2,1)S(1)}, u32[]{:S(2)}, u32[]{:S(2)}) collective-permute-start(bf16[80,512]{1,0:T(8,128)(2,1)} %bitcast.5), channel_id=1, source_target_pairs={{0,0},{1,4},{2,64},{3,68},{4,192},{5,196},{6,128},{7,132},{8,8},{9... | collective-permute-start | bytes 245768 | tf_op jit(solution)/shard_map/ppermute | solution.py:54
  5.7 16.8 %collective-permute-done.7 = bf16[80,512]{1,0:T(8,128)(2,1)S(1)} collective-permute-done((bf16[80,512]{1,0:T(8,128)(2,1)}, bf16[80,512]{1,0:T(8,128)(2,1)S(1)}, u32[]{:S(2)}, u32[]{:S(2)}) %collective-permute-start.7) | collective-permute-done | bytes 81952 | tf_op jit(solution)/shard_map/ppermute | solution.py:54
  22.5 0.9 broadcast_in_dim.2
  23.4 8.5 %all-to-all-start = ((bf16[8,80,512]{2,1,0:T(8,128)(2,1)}), bf16[8,80,512]{2,1,0:T(8,128)(2,1)}, u32[]{:S(2)}, u32[]{:S(2)}) async-start(bf16[8,80,512]{2,1,0:T(8,128)(2,1)} %broadcast_in_dim.2), calls=%async_computation | async-start | bytes 1310720 | tf_op jit(solution)/shard_map/all_to_all | solution.py:58
  31.9 0.0 copy-done.3
  31.9 0.1 collective-permute-start
  32.0 0.0 collective-permute-done.1.o2
  32.0 0.5 collective-permute-start.2
  32.5 3.2 %shard_map.101 = (bf16[256,512]{1,0:T(8,128)(2,1)}, f32[4,256,256]{2,1,0:T(8,128)}, bf16[256,768]{1,0:T(8,128)(2,1)}) custom-call(s32[8]{0:T(128)} %bitcast.6, bf16[256,512]{1,0:T(8,128)(2,1)} %q_ref.1, bf16[256,128]{1,0:T(8,128)(2,1)} %k_ref.1, bf16[256,128]{1,0:T(8,128)(2,1)} %v_ref.1), custom_call_target="tpu_custom_call" | custom-call | flops 134217728 | bytes 2097152 | tf_op jit(solution)/shard_map/pallas_call | solution.py:78
  35.7 4.5 %collective-permute-start.3 = (bf16[256,512]{1,0:T(8,128)(2,1)}, bf16[256,512]{1,0:T(8,128)(2,1)S(1)}, u32[]{:S(2)}, u32[]{:S(2)}) collective-permute-start(bf16[256,512]{1,0:T(8,128)(2,1)} %get-tuple-element.21), channel_id=1, source_target_pairs={{0,0},{1,4},{2,64},{3,68},{4,1},{5,5},{6,65},{7,69},{8,8},{9,12},{... | collective-permute-start | bytes 786440 | tf_op jit(solution)/shard_map/ppermute | solution.py:54
  40.1 8.6 %collective-permute-done.3.r0 = bf16[256,512]{1,0:T(8,128)(2,1)S(1)} collective-permute-done((bf16[256,512]{1,0:T(8,128)(2,1)}, bf16[256,512]{1,0:T(8,128)(2,1)S(1)}, u32[]{:S(2)}, u32[]{:S(2)}) %collective-permute-start.3) | collective-permute-done | bytes 262176 | tf_op jit(solution)/shard_map/ppermute | solution.py:54
  48.7 0.0 collective-permute-start.4
  48.8 0.0 collective-permute-start.5
  48.8 3.2 %collective-permute-start.6 = (bf16[256,512]{1,0:T(8,128)(2,1)S(1)}, bf16[256,512]{1,0:T(8,128)(2,1)S(1)}, u32[]{:S(2)}, u32[]{:S(2)}) collective-permute-start(bf16[256,512]{1,0:T(8,128)(2,1)S(1)} %collective-permute-done.3.r0), channel_id=1, source_target_pairs={{0,3},{1,0},{2,1},{3,2},{4,7},{5,4},{6,5},{7,6},{8,11},{9,8},{10,9... | collective-permute-start | bytes 786440 | tf_op jit(solution)/shard_map/ppermute | solution.py:54
  52.0 10.5 %collective-permute-done.4.r1 = bf16[256,512]{1,0:T(8,128)(2,1)S(1)} collective-permute-done((bf16[256,512]{1,0:T(8,128)(2,1)S(1)}, bf16[256,512]{1,0:T(8,128)(2,1)S(1)}, u32[]{:S(2)}, u32[]{:S(2)}) %collective-permute-start.4) | collective-permute-done | bytes 262176 | tf_op jit(solution)/shard_map/ppermute | solution.py:54
  62.5 0.0 all-to-all-done.w0
  62.5 1.0 collective-permute-start.8
  63.5 0.0 collective-permute-done.5.r2
  63.5 0.0 collective-permute-done.6.r3
  63.5 0.0 copy-start.10
  63.6 0.0 collective-permute-done.o1
  63.6 0.0 collective-permute-done.2.o3
  63.6 4.4 %shard_map.108 = bf16[1280,512]{1,0:T(8,128)(2,1)} custom-call(bf16[256,1280]{1,0:T(8,128)(2,1)S(1)} %copy-done.3, bf16[256,1280]{1,0:T(8,128)(2,1)} %collective-permute-done.o1, bf16[256,1280]{1,0:T(8,128)(2,1)} %collective-permute-done.1.o2, bf16[256,1280]{1,0:T(8,128)(2,1)} %collective-permute-done.2.o3, bf16[256,512]{1,0:T(8,128)(2,1)S(1)} %collective-permute-done.3.r0, ...), custom_call_target="tpu_custom_call" | custom-call | flops 1342177280 | bytes 6291456 | tf_op jit(solution)/shard_map/pallas_call | solution.py:78
  67.9 0.0 copy-done.6
  67.9 0.0 copy-done.8
  67.9 0.0 copy-done.10
  67.9 7.1 %all-to-all-start.1 = ((bf16[8,160,512]{2,1,0:T(8,128)(2,1)}), bf16[8,160,512]{2,1,0:T(8,128)(2,1)S(1)}, u32[]{:S(2)}, u32[]{:S(2)}) async-start(bf16[8,160,512]{2,1,0:T(8,128)(2,1)} %bitcast.2), calls=%async_computation.1 | async-start | bytes 2621440 | tf_op jit(solution)/shard_map/all_to_all | solution.py:58
  75.1 3.1 %collective-permute-done.8.w1 = bf16[8,80,512]{2,1,0:T(8,128)(2,1)S(1)} collective-permute-done((bf16[8,80,512]{2,1,0:T(8,128)(2,1)}, bf16[8,80,512]{2,1,0:T(8,128)(2,1)S(1)}, u32[]{:S(2)}, u32[]{:S(2)}) %collective-permute-start.8) | collective-permute-done | bytes 655392 | tf_op jit(solution)/shard_map/ppermute | solution.py:54
  78.1 0.8 copy-done.12
  79.0 0.9 copy-done.7
  79.9 0.9 copy-done.9
  80.9 0.9 copy-done.11
  81.8 1.1 copy-done.13
  82.9 2.2 %shard_map.102 = (bf16[2,256,1280]{2,1,0:T(8,128)(2,1)S(1)}, bf16[2,256,512]{2,1,0:T(8,128)(2,1)S(1)}, bf16[1280,512]{1,0:T(8,128)(2,1)S(1)}) custom-call(bf16[256,512]{1,0:T(8,128)(2,1)S(1)} %collective-permute-done.3.r0, bf16[256,512]{1,0:T(8,128)(2,1)S(1)} %copy-done.7, bf16[256,512]{1,0:T(8,128)(2,1)S(1)} %copy-done.9, bf16[256,512]{1,0:T(8,128)(2,1)S(1)} %copy-done.11, ...), custom_call_target="tpu_custom_call" | custom-call | flops 671088640 | bytes 6291456 | tf_op jit(solution)/shard_map/pallas_call | solution.py:78
  85.1 0.1 collective-permute-start.13
  85.2 3.0 %collective-permute-done.13.pair = bf16[2,256,1280]{2,1,0:T(8,128)(2,1)S(1)} collective-permute-done((bf16[2,256,1280]{2,1,0:T(8,128)(2,1)S(1)}, bf16[2,256,1280]{2,1,0:T(8,128)(2,1)S(1)}, u32[]{:S(2)}, u32[]{:S(2)}) %collective-permute-start.13) | collective-permute-done | bytes 1310752 | tf_op jit(solution)/shard_map/ppermute | solution.py:54
  88.3 1.4 %shard_map.106 = bf16[256,1280]{1,0:T(8,128)(2,1)} custom-call(bf16[2,256,512]{2,1,0:T(8,128)(2,1)S(1)} %get-tuple-element.29.att, bf16[1280,512]{1,0:T(8,128)(2,1)S(1)} %get-tuple-element.22.wt, bf16[2,256,1280]{2,1,0:T(8,128)(2,1)S(1)} %collective-permute-done.13.pair), custom_call_target="tpu_custom_call" | custom-call | flops 335544320 | bytes 3145728 | tf_op jit(solution)/shard_map/pallas_call | solution.py:78
  89.6 0.0 copy-done
  89.7 0.0 collective-permute-start.14
  89.7 0.2 copy-done.4
  89.8 3.8 %shard_map.103 = (bf16[256,512]{1,0:T(8,128)(2,1)S(1)}, bf16[256,512]{1,0:T(8,128)(2,1)}, bf16[256,512]{1,0:T(8,128)(2,1)}, bf16[256,512]{1,0:T(8,128)(2,1)}) custom-call(bf16[256,1280]{1,0:T(8,128)(2,1)S(1)} %copy-done.4, bf16[256,1280]{1,0:T(8,128)(2,1)} %collective-permute-done.o1, bf16[256,1280]{1,0:T(8,128)(2,1)} %collective-permute-done.1.o2, ...), custom_call_target="tpu_custom_call" | custom-call | flops 1342177280 | bytes 6291456 | tf_op jit(solution)/shard_map/pallas_call | solution.py:78
  93.6 0.0 collective-permute-start.10
  93.6 0.0 collective-permute-start.11
  93.7 2.0 %collective-permute-start.9 = (bf16[256,512]{1,0:T(8,128)(2,1)}, bf16[256,512]{1,0:T(8,128)(2,1)}, u32[]{:S(2)}, u32[]{:S(2)}) collective-permute-start(bf16[256,512]{1,0:T(8,128)(2,1)} %get-tuple-element.24), channel_id=1, source_target_pairs={{0,1},{1,2},{2,3},{3,0},{4,5},{5,6},{6,7},{7,4},{8,9},{9,10},{10,1... | collective-permute-start | bytes 786440 | tf_op jit(solution)/shard_map/ppermute | solution.py:54
  95.7 13.1 %all-to-all-done.1.blocks = bf16[8,160,512]{2,1,0:T(8,128)(2,1)S(1)} async-done(((bf16[8,160,512]{2,1,0:T(8,128)(2,1)}), bf16[8,160,512]{2,1,0:T(8,128)(2,1)S(1)}, u32[]{:S(2)}, u32[]{:S(2)}) %all-to-all-start.1) | async-done | bytes 1310752 | tf_op jit(solution)/shard_map/all_to_all | solution.py:58
  108.8 0.2 shard_map.109
  109.0 2.1 %collective-permute-start.15 = (bf16[80,512]{1,0:T(8,128)(2,1)S(1)}, bf16[80,512]{1,0:T(8,128)(2,1)S(1)}, u32[]{:S(2)}, u32[]{:S(2)}) collective-permute-start(bf16[80,512]{1,0:T(8,128)(2,1)S(1)} %get-tuple-element.35), channel_id=1, source_target_pairs={{0,0},{1,64},{2,128},{3,192},{4,1},{5,65},{6,129},{7,193},{8,8},{9... | collective-permute-start | bytes 245768 | tf_op jit(solution)/shard_map/ppermute | solution.py:54
  111.0 0.0 collective-permute-done.10.a2
  111.0 6.2 %collective-permute-start.16 = (bf16[80,512]{1,0:T(8,128)(2,1)S(1)}, bf16[80,512]{1,0:T(8,128)(2,1)S(1)}, u32[]{:S(2)}, u32[]{:S(2)}) collective-permute-start(bf16[80,512]{1,0:T(8,128)(2,1)S(1)} %get-tuple-element.36), channel_id=1, source_target_pairs={{0,4},{1,68},{2,132},{3,196},{4,5},{5,69},{6,133},{7,197},{8,12},{... | collective-permute-start | bytes 245768 | tf_op jit(solution)/shard_map/ppermute | solution.py:54
  117.2 0.0 collective-permute-done.11.a3
  117.2 0.0 collective-permute-done.9.a1
  117.3 1.2 shard_map.104
  118.5 0.0 copy-start.2
  118.5 0.0 copy-start.5
  118.5 2.6 %collective-permute-start.12 = (bf16[256,512]{1,0:T(8,128)(2,1)S(1)}, bf16[256,512]{1,0:T(8,128)(2,1)S(1)}, u32[]{:S(2)}, u32[]{:S(2)}) collective-permute-start(bf16[256,512]{1,0:T(8,128)(2,1)S(1)} %shard_map.104), channel_id=1, source_target_pairs={{0,0},{1,4},{2,64},{3,68},{4,1},{5,5},{6,65},{7,69},{8,8},{9,12},{... | collective-permute-start | bytes 786440 | tf_op jit(solution)/shard_map/ppermute | solution.py:54
  121.1 0.5 shard_map.105.own
  121.7 0.0 collective-permute-done.15
  121.7 0.0 collective-permute-done.16
  121.7 0.7 add_bitcast_fusion
  122.4 8.5 %collective-permute-done.12.up_ref = bf16[256,512]{1,0:T(8,128)(2,1)S(1)} collective-permute-done((bf16[256,512]{1,0:T(8,128)(2,1)S(1)}, bf16[256,512]{1,0:T(8,128)(2,1)S(1)}, u32[]{:S(2)}, u32[]{:S(2)}) %collective-permute-start.12) | collective-permute-done | bytes 262176 | tf_op jit(solution)/shard_map/ppermute | solution.py:54
  130.9 0.0 collective-permute-done.14.across
  130.9 3.9 %shard_map.107 = (bf16[256,512]{1,0:T(8,128)(2,1)}, bf16[256,128]{1,0:T(8,128)(2,1)}, bf16[256,128]{1,0:T(8,128)(2,1)}, bf16[256,1280]{1,0:T(8,128)(2,1)}) custom-call(bf16[256,512]{1,0:T(8,128)(2,1)S(1)} %collective-permute-done.12.up_ref, bf16[256,768]{1,0:T(8,128)(2,1)S(1)} %copy-done.5, f32[4,256,256]{2,1,0:T(8,128)S(1)} %copy-done.2, ...), custom_call_target="tpu_custom_call" | custom-call | flops 335544320 | bytes 3145728 | tf_op jit(solution)/shard_map/pallas_call | solution.py:78
  (13 shorter events, 0.0 us)
Async XLA Ops:
  0.6 31.2 %copy-start.3 = (bf16[256,1280]{1,0:T(8,128)(2,1)S(1)}, bf16[256,1280]{1,0:T(8,128)(2,1)}, u32[]{:S(2)}) copy-start(bf16[256,1280]{1,0:T(8,128)(2,1)} %o0.3) | copy-start | bytes 1966084
  0.6 31.3 %collective-permute-start.1 = (bf16[256,1280]{1,0:T(8,128)(2,1)}, bf16[256,1280]{1,0:T(8,128)(2,1)}, u32[]{:S(2)}, u32[]{:S(2)}) collective-permute-start(bf16[256,1280]{1,0:T(8,128)(2,1)} %o0.3), channel_id=1, source_target_pairs={{0,64},{1,65},{2,66},{3,67},{4,68},{5,69},{6,70},{7,71},{8,72},{9,... | collective-permute-start | bytes 1966088 | tf_op jit(solution)/shard_map/ppermute | solution.py:54
  3.0 19.5 %collective-permute-start.7 = (bf16[80,512]{1,0:T(8,128)(2,1)}, bf16[80,512]{1,0:T(8,128)(2,1)S(1)}, u32[]{:S(2)}, u32[]{:S(2)}) collective-permute-start(bf16[80,512]{1,0:T(8,128)(2,1)} %bitcast.5), channel_id=1, source_target_pairs={{0,0},{1,4},{2,64},{3,68},{4,192},{5,196},{6,128},{7,132},{8,8},{9... | collective-permute-start | bytes 245768 | tf_op jit(solution)/shard_map/ppermute | solution.py:54
  23.4 39.1 %all-to-all-start = ((bf16[8,80,512]{2,1,0:T(8,128)(2,1)}), bf16[8,80,512]{2,1,0:T(8,128)(2,1)}, u32[]{:S(2)}, u32[]{:S(2)}) async-start(bf16[8,80,512]{2,1,0:T(8,128)(2,1)} %broadcast_in_dim.2), calls=%async_computation | async-start | bytes 1310720 | tf_op jit(solution)/shard_map/all_to_all | solution.py:58
  31.9 31.7 %collective-permute-start = (bf16[256,1280]{1,0:T(8,128)(2,1)S(1)}, bf16[256,1280]{1,0:T(8,128)(2,1)}, u32[]{:S(2)}, u32[]{:S(2)}) collective-permute-start(bf16[256,1280]{1,0:T(8,128)(2,1)S(1)} %copy-done.3), channel_id=1, source_target_pairs={{0,4},{1,5},{2,6},{3,7},{4,0},{5,1},{6,2},{7,3},{8,12},{9,13},{10,... | collective-permute-start | bytes 1966088 | tf_op jit(solution)/shard_map/ppermute | solution.py:54
  32.0 31.6 %collective-permute-start.2 = (bf16[256,1280]{1,0:T(8,128)(2,1)}, bf16[256,1280]{1,0:T(8,128)(2,1)}, u32[]{:S(2)}, u32[]{:S(2)}) collective-permute-start(bf16[256,1280]{1,0:T(8,128)(2,1)} %collective-permute-done.1.o2), channel_id=1, source_target_pairs={{0,4},{1,5},{2,6},{3,7},{4,0},{5,1},{6,2},{7,3},{8,12},{9,13},{10,... | collective-permute-start | bytes 1966088 | tf_op jit(solution)/shard_map/ppermute | solution.py:54
  35.7 13.1 %collective-permute-start.3 = (bf16[256,512]{1,0:T(8,128)(2,1)}, bf16[256,512]{1,0:T(8,128)(2,1)S(1)}, u32[]{:S(2)}, u32[]{:S(2)}) collective-permute-start(bf16[256,512]{1,0:T(8,128)(2,1)} %get-tuple-element.21), channel_id=1, source_target_pairs={{0,0},{1,4},{2,64},{3,68},{4,1},{5,5},{6,65},{7,69},{8,8},{9,12},{... | collective-permute-start | bytes 786440 | tf_op jit(solution)/shard_map/ppermute | solution.py:54
  48.7 13.7 %collective-permute-start.4 = (bf16[256,512]{1,0:T(8,128)(2,1)S(1)}, bf16[256,512]{1,0:T(8,128)(2,1)S(1)}, u32[]{:S(2)}, u32[]{:S(2)}) collective-permute-start(bf16[256,512]{1,0:T(8,128)(2,1)S(1)} %collective-permute-done.3.r0), channel_id=1, source_target_pairs={{0,1},{1,2},{2,3},{3,0},{4,5},{5,6},{6,7},{7,4},{8,9},{9,10},{10,1... | collective-permute-start | bytes 786440 | tf_op jit(solution)/shard_map/ppermute | solution.py:54
  48.8 14.8 %collective-permute-start.5 = (bf16[256,512]{1,0:T(8,128)(2,1)S(1)}, bf16[256,512]{1,0:T(8,128)(2,1)S(1)}, u32[]{:S(2)}, u32[]{:S(2)}) collective-permute-start(bf16[256,512]{1,0:T(8,128)(2,1)S(1)} %collective-permute-done.3.r0), channel_id=1, source_target_pairs={{0,2},{1,3},{2,0},{3,1},{4,6},{5,7},{6,4},{7,5},{8,10},{9,11},{10,... | collective-permute-start | bytes 786440 | tf_op jit(solution)/shard_map/ppermute | solution.py:54
  48.8 14.8 %collective-permute-start.6 = (bf16[256,512]{1,0:T(8,128)(2,1)S(1)}, bf16[256,512]{1,0:T(8,128)(2,1)S(1)}, u32[]{:S(2)}, u32[]{:S(2)}) collective-permute-start(bf16[256,512]{1,0:T(8,128)(2,1)S(1)} %collective-permute-done.3.r0), channel_id=1, source_target_pairs={{0,3},{1,0},{2,1},{3,2},{4,7},{5,4},{6,5},{7,6},{8,11},{9,8},{10,9... | collective-permute-start | bytes 786440 | tf_op jit(solution)/shard_map/ppermute | solution.py:54
  62.5 5.5 %copy-start.6 = (bf16[256,512]{1,0:T(8,128)(2,1)}, bf16[256,512]{1,0:T(8,128)(2,1)S(1)}, u32[]{:S(2)}) copy-start(bf16[256,512]{1,0:T(8,128)(2,1)S(1)} %collective-permute-done.4.r1) | copy-start | bytes 786436
  62.5 15.6 %collective-permute-start.8 = (bf16[8,80,512]{2,1,0:T(8,128)(2,1)}, bf16[8,80,512]{2,1,0:T(8,128)(2,1)S(1)}, u32[]{:S(2)}, u32[]{:S(2)}) collective-permute-start(bf16[8,80,512]{2,1,0:T(8,128)(2,1)} %all-to-all-done.w0), channel_id=1, source_target_pairs={{0,192},{1,193},{2,194},{3,195},{4,196},{5,197},{6,198},{7,199},{8... | collective-permute-start | bytes 1966088 | tf_op jit(solution)/shard_map/ppermute | solution.py:54
  63.5 4.4 %copy-start.8 = (bf16[256,512]{1,0:T(8,128)(2,1)}, bf16[256,512]{1,0:T(8,128)(2,1)S(1)}, u32[]{:S(2)}) copy-start(bf16[256,512]{1,0:T(8,128)(2,1)S(1)} %collective-permute-done.5.r2) | copy-start | bytes 786436
  63.5 4.4 %copy-start.10 = (bf16[256,512]{1,0:T(8,128)(2,1)}, bf16[256,512]{1,0:T(8,128)(2,1)S(1)}, u32[]{:S(2)}) copy-start(bf16[256,512]{1,0:T(8,128)(2,1)S(1)} %collective-permute-done.6.r3) | copy-start | bytes 786436
  67.9 40.8 %all-to-all-start.1 = ((bf16[8,160,512]{2,1,0:T(8,128)(2,1)}), bf16[8,160,512]{2,1,0:T(8,128)(2,1)S(1)}, u32[]{:S(2)}, u32[]{:S(2)}) async-start(bf16[8,160,512]{2,1,0:T(8,128)(2,1)} %bitcast.2), calls=%async_computation.1 | async-start | bytes 2621440 | tf_op jit(solution)/shard_map/all_to_all | solution.py:58
  78.1 0.8 copy-start.12
  79.0 0.9 copy-start.7
  79.9 0.9 copy-start.9
  80.9 0.9 copy-start.11
  81.8 1.1 copy-start.13
  85.1 3.1 %collective-permute-start.13 = (bf16[2,256,1280]{2,1,0:T(8,128)(2,1)S(1)}, bf16[2,256,1280]{2,1,0:T(8,128)(2,1)S(1)}, u32[]{:S(2)}, u32[]{:S(2)}) collective-permute-start(bf16[2,256,1280]{2,1,0:T(8,128)(2,1)S(1)} %get-tuple-element.30), channel_id=1, source_target_pairs={{0,4},{1,5},{2,6},{3,7},{4,0},{5,1},{6,2},{7,3},{8,12},{9,13},{10,... | collective-permute-start | bytes 3932168 | tf_op jit(solution)/shard_map/ppermute | solution.py:54
  88.3 1.4 %copy-start = (bf16[2,256,1280]{2,1,0:T(8,128)(2,1)}, bf16[2,256,1280]{2,1,0:T(8,128)(2,1)S(1)}, u32[]{:S(2)}) copy-start(bf16[2,256,1280]{2,1,0:T(8,128)(2,1)S(1)} %collective-permute-done.13.pair) | copy-start | bytes 3932164
  88.3 1.5 %copy-start.4 = (bf16[256,1280]{1,0:T(8,128)(2,1)S(1)}, bf16[256,1280]{1,0:T(8,128)(2,1)}, u32[]{:S(2)}) copy-start(bf16[256,1280]{1,0:T(8,128)(2,1)} %o0.3) | copy-start | bytes 1966084
  89.7 41.2 %collective-permute-start.14 = (bf16[256,1280]{1,0:T(8,128)(2,1)}, bf16[256,1280]{1,0:T(8,128)(2,1)}, u32[]{:S(2)}, u32[]{:S(2)}) collective-permute-start(bf16[256,1280]{1,0:T(8,128)(2,1)} %shard_map.106), channel_id=1, source_target_pairs={{0,64},{1,65},{2,66},{3,67},{4,68},{5,69},{6,70},{7,71},{8,72},{9,... | collective-permute-start | bytes 1966088 | tf_op jit(solution)/shard_map/ppermute | solution.py:54
  93.6 17.4 %collective-permute-start.10 = (bf16[256,512]{1,0:T(8,128)(2,1)}, bf16[256,512]{1,0:T(8,128)(2,1)}, u32[]{:S(2)}, u32[]{:S(2)}) collective-permute-start(bf16[256,512]{1,0:T(8,128)(2,1)} %get-tuple-element.25), channel_id=1, source_target_pairs={{0,2},{1,3},{2,0},{3,1},{4,6},{5,7},{6,4},{7,5},{8,10},{9,11},{10,... | collective-permute-start | bytes 786440 | tf_op jit(solution)/shard_map/ppermute | solution.py:54
  93.6 23.6 %collective-permute-start.11 = (bf16[256,512]{1,0:T(8,128)(2,1)}, bf16[256,512]{1,0:T(8,128)(2,1)}, u32[]{:S(2)}, u32[]{:S(2)}) collective-permute-start(bf16[256,512]{1,0:T(8,128)(2,1)} %get-tuple-element.26), channel_id=1, source_target_pairs={{0,3},{1,0},{2,1},{3,2},{4,7},{5,4},{6,5},{7,6},{8,11},{9,8},{10,9... | collective-permute-start | bytes 786440 | tf_op jit(solution)/shard_map/ppermute | solution.py:54
  93.7 23.6 %collective-permute-start.9 = (bf16[256,512]{1,0:T(8,128)(2,1)}, bf16[256,512]{1,0:T(8,128)(2,1)}, u32[]{:S(2)}, u32[]{:S(2)}) collective-permute-start(bf16[256,512]{1,0:T(8,128)(2,1)} %get-tuple-element.24), channel_id=1, source_target_pairs={{0,1},{1,2},{2,3},{3,0},{4,5},{5,6},{6,7},{7,4},{8,9},{9,10},{10,1... | collective-permute-start | bytes 786440 | tf_op jit(solution)/shard_map/ppermute | solution.py:54
  108.8 12.3 %copy-start.1 = (bf16[2,256,1280]{2,1,0:T(8,128)(2,1)S(1)}, bf16[2,256,1280]{2,1,0:T(8,128)(2,1)}, u32[]{:S(2)}) copy-start(bf16[2,256,1280]{2,1,0:T(8,128)(2,1)} %copy-done) | copy-start | bytes 3932164
  109.0 12.7 %collective-permute-start.15 = (bf16[80,512]{1,0:T(8,128)(2,1)S(1)}, bf16[80,512]{1,0:T(8,128)(2,1)S(1)}, u32[]{:S(2)}, u32[]{:S(2)}) collective-permute-start(bf16[80,512]{1,0:T(8,128)(2,1)S(1)} %get-tuple-element.35), channel_id=1, source_target_pairs={{0,0},{1,64},{2,128},{3,192},{4,1},{5,65},{6,129},{7,193},{8,8},{9... | collective-permute-start | bytes 245768 | tf_op jit(solution)/shard_map/ppermute | solution.py:54
  111.0 10.6 %collective-permute-start.16 = (bf16[80,512]{1,0:T(8,128)(2,1)S(1)}, bf16[80,512]{1,0:T(8,128)(2,1)S(1)}, u32[]{:S(2)}, u32[]{:S(2)}) collective-permute-start(bf16[80,512]{1,0:T(8,128)(2,1)S(1)} %get-tuple-element.36), channel_id=1, source_target_pairs={{0,4},{1,68},{2,132},{3,196},{4,5},{5,69},{6,133},{7,197},{8,12},{... | collective-permute-start | bytes 245768 | tf_op jit(solution)/shard_map/ppermute | solution.py:54
  118.5 12.4 %copy-start.2 = (f32[4,256,256]{2,1,0:T(8,128)S(1)}, f32[4,256,256]{2,1,0:T(8,128)}, u32[]{:S(2)}) copy-start(f32[4,256,256]{2,1,0:T(8,128)} %get-tuple-element.28.prob_ref) | copy-start | bytes 3145732
  118.5 12.4 %copy-start.5 = (bf16[256,768]{1,0:T(8,128)(2,1)S(1)}, bf16[256,768]{1,0:T(8,128)(2,1)}, u32[]{:S(2)}) copy-start(bf16[256,768]{1,0:T(8,128)(2,1)} %get-tuple-element.27.kept) | copy-start | bytes 1179652
  118.5 12.4 %collective-permute-start.12 = (bf16[256,512]{1,0:T(8,128)(2,1)S(1)}, bf16[256,512]{1,0:T(8,128)(2,1)S(1)}, u32[]{:S(2)}, u32[]{:S(2)}) collective-permute-start(bf16[256,512]{1,0:T(8,128)(2,1)S(1)} %shard_map.104), channel_id=1, source_target_pairs={{0,0},{1,4},{2,64},{3,68},{4,1},{5,5},{6,65},{7,69},{8,8},{9,12},{... | collective-permute-start | bytes 786440 | tf_op jit(solution)/shard_map/ppermute | solution.py:54
